TPU v7x, 32 devices: a whole 2x2x4 slice. The times are simulated.
32 devices in a mesh: pipe: 4 (over y, x), dp: 8 (over z, core).
Axes of the slice: x: 2, y: 2, z: 4, core: 2. Of those that a mesh axis runs over, the one named last changes fastest.
Arguments:
- inputs: bfloat16 [8, 4, 32, 8192], P('dp'), may hold values from -48 to 48
- segments: int32 [8, 4, 32], P('dp'), may hold values from 0 to 3, never falling along the last dimension, each value on 1 to 16 neighbouring positions
- cotangent: bfloat16 [8, 4, 32, 8192], P('dp'), may hold values from -6 to 6
- w_query: bfloat16 [4, 8192, 128], P('pipe', 'dp'), may hold values from -3 to 3
- w_key: bfloat16 [4, 8192, 128], P('pipe', 'dp'), may hold values from -3 to 3
- w_value: bfloat16 [4, 8192, 128], P('pipe', 'dp'), may hold values from -0.0625 to 0.0625
- w_out: bfloat16 [4, 8192, 128], P('pipe', 'dp'), may hold values from -0.5 to 0.5
Outputs:
- input_grads: bfloat16 [4, 8, 4, 32, 8192], P('pipe', 'dp')
- grad_query: float32 [4, 8192, 128], P('pipe', 'dp')
- grad_key: float32 [4, 8192, 128], P('pipe', 'dp')
- grad_value: float32 [4, 8192, 128], P('pipe', 'dp')
- grad_out: float32 [4, 8192, 128], P('pipe', 'dp')
Inputs may be any that keep to these rules, and one draw needn't show every extreme that they name: `segments`: along each micro-batch the numbers never fall; a document has 1 to 16 tokens, and one has exactly 16.
All inputs are finite; a program needn't handle non-finite values.
Results may differ from a plain program's by a relative error of at most 0.025.
Values may be sent and summed in bfloat16 or wider, within the bound.
No kernel may reach another device: no remote copies, remote signals or barrier semaphores. Data moves between devices by JAX's collectives and lax.ppermute only.
A program may use at most 192 MiB of HBM per device.

v0:
```python
import jax
import jax.numpy as jnp
from jax import lax
from jax.sharding import PartitionSpec as P


def shifted(block, axis, distance):
    devices = range(lax.axis_size(axis))
    route = [(i - distance, i) for i in devices if i - distance in devices]
    return lax.ppermute(block, axis, route)


def section(hidden, doc_ids, w_query, w_key, w_value, w_out):
    widen = hidden.astype(jnp.float32)
    normed = (widen * lax.rsqrt(jnp.mean(widen * widen, axis=-1, keepdims=True) + 1e-05)).astype(
        jnp.bfloat16
    )
    query = jnp.dot(normed, w_query, preferred_element_type=jnp.float32).astype(jnp.bfloat16)
    keys = jnp.dot(normed, w_key, preferred_element_type=jnp.float32).astype(jnp.bfloat16)
    values = jnp.dot(normed, w_value, preferred_element_type=jnp.float32).astype(jnp.bfloat16)
    scores = jnp.dot(query, keys.T, preferred_element_type=jnp.float32) * w_query.shape[1] ** (-0.5)
    places = jnp.arange(hidden.shape[0])
    allowed = (places[:, None] >= places[None, :]) & (doc_ids[:, None] == doc_ids[None, :])
    scores = jnp.where(allowed, scores, -1e30)
    highest = jnp.max(scores, axis=-1, keepdims=True)
    exponent = jnp.where(allowed, jnp.exp(scores - highest), 0.0)
    attend = (exponent / jnp.sum(exponent, axis=-1, keepdims=True)).astype(jnp.bfloat16)
    mixed = jnp.dot(attend, values, preferred_element_type=jnp.float32).astype(jnp.bfloat16)
    update = jnp.dot(mixed, w_out.T, preferred_element_type=jnp.float32)
    return (widen + update).astype(jnp.bfloat16)


def shards(inputs, segments, cotangent, w_query, w_key, w_value, w_out):
    sections = lax.axis_size("pipe")
    section_id = lax.axis_index("pipe")
    full_query, full_key, full_value, full_out = (
        lax.all_gather(w_query, "dp", axis=1, tiled=True),
        lax.all_gather(w_key, "dp", axis=1, tiled=True),
        lax.all_gather(w_value, "dp", axis=1, tiled=True),
        lax.all_gather(w_out, "dp", axis=1, tiled=True),
    )
    layer = (full_query[0], full_key[0], full_value[0], full_out[0])
    features = inputs[0]
    doc_table = segments[0]
    final_cots = cotangent[0]
    batches = features.shape[0]
    ticks = sections + batches - 1

    def forward_tick(tick, carry):
        incoming, stash = carry
        offset = tick - section_id
        active = (offset >= 0) & (offset < batches)
        batch_slot = jnp.clip(offset, 0, batches - 1)
        first = lax.dynamic_index_in_dim(features, batch_slot, 0, keepdims=False)
        section_input = jnp.where(section_id == 0, first, incoming)
        doc_ids = lax.dynamic_index_in_dim(doc_table, batch_slot, 0, keepdims=False)
        result = lax.cond(
            active,
            lambda: section(section_input, doc_ids, *layer),
            lambda: jnp.zeros_like(section_input),
        )
        previous = lax.dynamic_index_in_dim(stash, batch_slot, 0, keepdims=False)
        stash = lax.dynamic_update_index_in_dim(
            stash, jnp.where(active, section_input, previous), batch_slot, 0
        )
        incoming = shifted(result, "pipe", 1)
        return (incoming, stash)

    start_buffer = jnp.zeros(features.shape[1:], jnp.bfloat16)
    _, stash = lax.fori_loop(0, ticks, forward_tick, (start_buffer, jnp.zeros_like(features)))

    def backward_tick(tick, carry):
        incoming, totals, stored = carry
        offset = tick - (sections - 1 - section_id)
        active = (offset >= 0) & (offset < batches)
        batch_slot = jnp.clip(offset, 0, batches - 1)
        last_cot = lax.dynamic_index_in_dim(final_cots, batch_slot, 0, keepdims=False)
        grad_input = jnp.where(section_id == sections - 1, last_cot, incoming)
        saved_h = lax.dynamic_index_in_dim(stash, batch_slot, 0, keepdims=False)
        doc_ids = lax.dynamic_index_in_dim(doc_table, batch_slot, 0, keepdims=False)

        def run_back():
            _, pull = jax.vjp(
                lambda hid, wa, wb, wc, wd: section(hid, doc_ids, wa, wb, wc, wd), saved_h, *layer
            )
            outs = pull(grad_input)
            return (outs[0], tuple((grad.astype(jnp.float32) for grad in outs[1:])))

        def skip_back():
            return (
                jnp.zeros_like(saved_h),
                tuple((jnp.zeros(part.shape, jnp.float32) for part in layer)),
            )

        cot_input, parts = lax.cond(active, run_back, skip_back)
        totals = tuple((total + part for total, part in zip(totals, parts)))
        previous = lax.dynamic_index_in_dim(stored, batch_slot, 0, keepdims=False)
        stored = lax.dynamic_update_index_in_dim(
            stored, jnp.where(active, cot_input, previous), batch_slot, 0
        )
        incoming = shifted(cot_input, "pipe", -1)
        return (incoming, totals, stored)

    zero_totals = tuple((jnp.zeros(part.shape, jnp.float32) for part in layer))
    _, totals, stored = lax.fori_loop(
        0, ticks, backward_tick, (start_buffer, zero_totals, jnp.zeros_like(features))
    )
    owned_grads = (
        lax.psum_scatter(
            totals[0].astype(jnp.bfloat16)[None], "dp", scatter_dimension=1, tiled=True
        ).astype(jnp.float32),
        lax.psum_scatter(
            totals[1].astype(jnp.bfloat16)[None], "dp", scatter_dimension=1, tiled=True
        ).astype(jnp.float32),
        lax.psum_scatter(
            totals[2].astype(jnp.bfloat16)[None], "dp", scatter_dimension=1, tiled=True
        ).astype(jnp.float32),
        lax.psum_scatter(
            totals[3].astype(jnp.bfloat16)[None], "dp", scatter_dimension=1, tiled=True
        ).astype(jnp.float32),
    )
    return (stored[None, None], owned_grads[0], owned_grads[1], owned_grads[2], owned_grads[3])


def solution(mesh):
    placed = (
        P("dp", None, None, None),
        P("dp", None, None),
        P("dp", None, None, None),
        P("pipe", "dp", None),
        P("pipe", "dp", None),
        P("pipe", "dp", None),
        P("pipe", "dp", None),
    )
    return jax.shard_map(
        shards,
        mesh=mesh,
        in_specs=placed,
        out_specs=(
            P("pipe", "dp", None, None, None),
            P("pipe", "dp", None),
            P("pipe", "dp", None),
            P("pipe", "dp", None),
            P("pipe", "dp", None),
        ),
        check_vma=False,
    )
```

profile of v0, /device:TPU:0, one launch (start us, length us, event | category | flops | bytes accessed | tf_op | source)
XLA Modules:
  0.0 771.5 jit_solution(6863091489487590063)
XLA Ops:
  10.1 31.4 %all-gather.5.cloned.1.call-done = bf16[1,8192,128]{2,1,0:T(8,128)(2,1)} async-done(((bf16[1,1024,128]{2,1,0:T(8,128)(2,1)}), bf16[1,8192,128]{2,1,0:T(8,128)(2,1)}) %all-gather.5.cloned.1.call-update) | async-done | bytes 2097168 | tf_op jit(solution)/shard_map/all_gather | solution.py:37
  41.4 30.2 %all-gather.7.cloned.1.call-done = bf16[1,8192,128]{2,1,0:T(8,128)(2,1)} async-done(((bf16[1,1024,128]{2,1,0:T(8,128)(2,1)}), bf16[1,8192,128]{2,1,0:T(8,128)(2,1)}) %all-gather.7.cloned.1.call-update) | async-done | bytes 2097168 | tf_op jit(solution)/shard_map/all_gather | solution.py:38
  71.7 30.2 %all-gather.9.cloned.1.call-done = bf16[1,8192,128]{2,1,0:T(8,128)(2,1)} async-done(((bf16[1,1024,128]{2,1,0:T(8,128)(2,1)}), bf16[1,8192,128]{2,1,0:T(8,128)(2,1)}) %all-gather.9.cloned.1.call-update) | async-done | bytes 2097168 | tf_op jit(solution)/shard_map/all_gather | solution.py:39
  101.9 30.1 %all-gather.11.cloned.1.call-done = bf16[1,8192,128]{2,1,0:T(8,128)(2,1)} async-done(((bf16[1,1024,128]{2,1,0:T(8,128)(2,1)}), bf16[1,8192,128]{2,1,0:T(8,128)(2,1)}) %all-gather.11.cloned.1.call-update) | async-done | bytes 2097168 | tf_op jit(solution)/shard_map/all_gather | solution.py:40
  133.6 171.1 %while.42 = (s32[]{:T(128)}, bf16[32,8192]{1,0:T(8,128)(2,1)S(1)}, bf16[4,32,8192]{2,1,0:T(8,128)(2,1)}, s32[]{:T(128)}, pred[]{:T(512)}, /*index=5*/bf16[4,32,8...) while((s32[]{:T(128)}, bf16[32,8192]{1,0:T(8,128)(2,1)S(1)}, ...), condition=%wide.region_6.7_spmd, body=%wide.region_0.6_spmd.sunk | while | flops 273452000 | bytes 19447128 | solution.py:70
  136.8 7.7 %conditional.5 = (bf16[32,8192]{1,0:T(8,128)(2,1)S(1)}) conditional(s32[]{:T(128)} %convert_element_type.325, () %tuple.110, (bf16[32,8192]{1,0:T(8,128)(2,1)S(1)}, s32[4,32]{1,0:T(4,128)S(1)}, s32[]{:T(128)}, bf16[8192,128]{1,0:T(8,128)(2,1)S(1)}, bf16[8192,128]{1,0:T(8,128)(2,1)}, /*index=5*/bf16[8192,128]{1,0:T(8,128)(2,1)}, ...), branch_computations={%region_1.1_spmd, %region_2.5_spmd} | conditional | flops 272927712 | bytes 11581452 | solution.py:57
  146.7 12.1 %collective-permute-done = bf16[32,8192]{1,0:T(8,128)(2,1)S(1)} collective-permute-done((bf16[32,8192]{1,0:T(8,128)(2,1)}, bf16[32,8192]{1,0:T(8,128)(2,1)S(1)}, u32[]{:S(2)}, u32[]{:S(2)}) %collective-permute-start) | collective-permute-done | bytes 524320 | tf_op jit(solution)/shard_map/while/body/eval_jaxpr/ppermute | solution.py:10
  161.9 7.7 %conditional.5 = (bf16[32,8192]{1,0:T(8,128)(2,1)S(1)}) conditional(s32[]{:T(128)} %convert_element_type.325, () %tuple.110, (bf16[32,8192]{1,0:T(8,128)(2,1)S(1)}, s32[4,32]{1,0:T(4,128)S(1)}, s32[]{:T(128)}, bf16[8192,128]{1,0:T(8,128)(2,1)S(1)}, bf16[8192,128]{1,0:T(8,128)(2,1)}, /*index=5*/bf16[8192,128]{1,0:T(8,128)(2,1)}, ...), branch_computations={%region_1.1_spmd, %region_2.5_spmd} | conditional | flops 272927712 | bytes 11581452 | solution.py:57
  170.4 4.4 collective-permute-start
  174.8 11.3 %collective-permute-done = bf16[32,8192]{1,0:T(8,128)(2,1)S(1)} collective-permute-done((bf16[32,8192]{1,0:T(8,128)(2,1)}, bf16[32,8192]{1,0:T(8,128)(2,1)S(1)}, u32[]{:S(2)}, u32[]{:S(2)}) %collective-permute-start) | collective-permute-done | bytes 524320 | tf_op jit(solution)/shard_map/while/body/eval_jaxpr/ppermute | solution.py:10
  189.3 7.7 %conditional.5 = (bf16[32,8192]{1,0:T(8,128)(2,1)S(1)}) conditional(s32[]{:T(128)} %convert_element_type.325, () %tuple.110, (bf16[32,8192]{1,0:T(8,128)(2,1)S(1)}, s32[4,32]{1,0:T(4,128)S(1)}, s32[]{:T(128)}, bf16[8192,128]{1,0:T(8,128)(2,1)S(1)}, bf16[8192,128]{1,0:T(8,128)(2,1)}, /*index=5*/bf16[8192,128]{1,0:T(8,128)(2,1)}, ...), branch_computations={%region_1.1_spmd, %region_2.5_spmd} | conditional | flops 272927712 | bytes 11581452 | solution.py:57
  202.1 10.5 %collective-permute-done = bf16[32,8192]{1,0:T(8,128)(2,1)S(1)} collective-permute-done((bf16[32,8192]{1,0:T(8,128)(2,1)}, bf16[32,8192]{1,0:T(8,128)(2,1)S(1)}, u32[]{:S(2)}, u32[]{:S(2)}) %collective-permute-start) | collective-permute-done | bytes 524320 | tf_op jit(solution)/shard_map/while/body/eval_jaxpr/ppermute | solution.py:10
  215.7 7.7 %conditional.5 = (bf16[32,8192]{1,0:T(8,128)(2,1)S(1)}) conditional(s32[]{:T(128)} %convert_element_type.325, () %tuple.110, (bf16[32,8192]{1,0:T(8,128)(2,1)S(1)}, s32[4,32]{1,0:T(4,128)S(1)}, s32[]{:T(128)}, bf16[8192,128]{1,0:T(8,128)(2,1)S(1)}, bf16[8192,128]{1,0:T(8,128)(2,1)}, /*index=5*/bf16[8192,128]{1,0:T(8,128)(2,1)}, ...), branch_computations={%region_1.1_spmd, %region_2.5_spmd} | conditional | flops 272927712 | bytes 11581452 | solution.py:57
  224.3 4.3 collective-permute-start
  228.6 9.5 %collective-permute-done = bf16[32,8192]{1,0:T(8,128)(2,1)S(1)} collective-permute-done((bf16[32,8192]{1,0:T(8,128)(2,1)}, bf16[32,8192]{1,0:T(8,128)(2,1)S(1)}, u32[]{:S(2)}, u32[]{:S(2)}) %collective-permute-start) | collective-permute-done | bytes 524320 | tf_op jit(solution)/shard_map/while/body/eval_jaxpr/ppermute | solution.py:10
  242.1 12.4 %collective-permute-start = (bf16[32,8192]{1,0:T(8,128)(2,1)}, bf16[32,8192]{1,0:T(8,128)(2,1)S(1)}, u32[]{:S(2)}, u32[]{:S(2)}) collective-permute-start(bf16[32,8192]{1,0:T(8,128)(2,1)} %copy-done.9), channel_id=1, source_target_pairs={{0,8},{8,16},{16,24},{1,9},{9,17},{17,25},{2,10},{10,18},{18,26},{... | collective-permute-start | bytes 1572872 | tf_op jit(solution)/shard_map/while/body/eval_jaxpr/ppermute | solution.py:10
  254.5 8.9 %collective-permute-done = bf16[32,8192]{1,0:T(8,128)(2,1)S(1)} collective-permute-done((bf16[32,8192]{1,0:T(8,128)(2,1)}, bf16[32,8192]{1,0:T(8,128)(2,1)S(1)}, u32[]{:S(2)}, u32[]{:S(2)}) %collective-permute-start) | collective-permute-done | bytes 524320 | tf_op jit(solution)/shard_map/while/body/eval_jaxpr/ppermute | solution.py:10
  267.5 5.2 collective-permute-start
  272.6 8.0 %collective-permute-done = bf16[32,8192]{1,0:T(8,128)(2,1)S(1)} collective-permute-done((bf16[32,8192]{1,0:T(8,128)(2,1)}, bf16[32,8192]{1,0:T(8,128)(2,1)S(1)}, u32[]{:S(2)}, u32[]{:S(2)}) %collective-permute-start) | collective-permute-done | bytes 524320 | tf_op jit(solution)/shard_map/while/body/eval_jaxpr/ppermute | solution.py:10
  284.7 12.9 %collective-permute-start = (bf16[32,8192]{1,0:T(8,128)(2,1)}, bf16[32,8192]{1,0:T(8,128)(2,1)S(1)}, u32[]{:S(2)}, u32[]{:S(2)}) collective-permute-start(bf16[32,8192]{1,0:T(8,128)(2,1)} %copy-done.9), channel_id=1, source_target_pairs={{0,8},{8,16},{16,24},{1,9},{9,17},{17,25},{2,10},{10,18},{18,26},{... | collective-permute-start | bytes 1572872 | tf_op jit(solution)/shard_map/while/body/eval_jaxpr/ppermute | solution.py:10
  297.6 7.1 collective-permute-done
  307.0 305.3 %while.43 = (s32[]{:T(128)}, bf16[32,8192]{1,0:T(8,128)(2,1)}, f32[8192,128]{1,0:T(8,128)}, f32[8192,128]{1,0:T(8,128)}, f32[8192,128]{1,0:T(8,128)}, /*index=5*...) while((s32[]{:T(128)}, bf16[32,8192]{1,0:T(8,128)(2,1)}, ...), condition=%wide.region_17.18_spmd.clone, body=%wide.region_7.17_spmd.clone.sunk | while | flops 767129792 | bytes 153846560 | solution.py:105
  307.0 8.9 %conditional.6 = (bf16[32,8192]{1,0:T(8,128)(2,1)S(1)}, f32[8192,128]{1,0:T(8,128)}, f32[8192,128]{1,0:T(8,128)}, f32[8192,128]{1,0:T(8,128)}, f32[8192,128]{1,0:T(8,128)}) conditional(s32[]{:T(128)} %convert_element_type.326, () %tuple.115, (pred[]{:T(512)}, bf16[4,32,8192]{2,1,0:T(8,128)(2,1)}, s32[]{:T(128)}, bf16[32,8192]{1,0:T(8,128)(2,1)}, ...), branch_computations={%region_8.8_spmd, %region_9.16_spmd} | conditional | flops 758479040 | bytes 96698248 | solution.py:95
  318.3 7.5 select_add_fusion.7
  325.9 7.5 select_add_fusion.6
  335.1 8.9 %conditional.6 = (bf16[32,8192]{1,0:T(8,128)(2,1)S(1)}, f32[8192,128]{1,0:T(8,128)}, f32[8192,128]{1,0:T(8,128)}, f32[8192,128]{1,0:T(8,128)}, f32[8192,128]{1,0:T(8,128)}) conditional(s32[]{:T(128)} %convert_element_type.326, () %tuple.115, (pred[]{:T(512)}, bf16[4,32,8192]{2,1,0:T(8,128)(2,1)}, s32[]{:T(128)}, bf16[32,8192]{1,0:T(8,128)(2,1)}, ...), branch_computations={%region_8.8_spmd, %region_9.16_spmd} | conditional | flops 758479040 | bytes 96698248 | solution.py:95
  346.4 9.9 %select_add_fusion.7 = (f32[8192,128]{1,0:T(8,128)}, f32[8192,128]{1,0:T(8,128)}) fusion(f32[8192,128]{1,0:T(8,128)} %get-tuple-element.1022, f32[8192,128]{1,0:T(8,128)} %get-tuple-element.1106, pred[]{:T(512)S(6)} %compare.3, f32[8192,128]{1,0:T(8,128)} %get-tuple-element.1023, f32[8192,128]{1,0:T(8,128)} %get-tuple-element.1105), kind=kLoop, calls=%fused_computation.93.clone.1 | loop fusion | flops 4194304 | bytes 25165824 | tf_op jit(solution)/shard_map/while/body/eval_jaxpr/add | solution.py:96
  356.3 9.9 %select_add_fusion.6 = (f32[8192,128]{1,0:T(8,128)}, f32[8192,128]{1,0:T(8,128)}) fusion(f32[8192,128]{1,0:T(8,128)} %get-tuple-element.1018, f32[8192,128]{1,0:T(8,128)} %get-tuple-element.1104, pred[]{:T(512)S(6)} %compare.3, f32[8192,128]{1,0:T(8,128)} %get-tuple-element.1019, f32[8192,128]{1,0:T(8,128)} %get-tuple-element.1103), kind=kLoop, calls=%fused_computation.95.clone.1 | loop fusion | flops 4194304 | bytes 25165824 | tf_op jit(solution)/shard_map/while/body/eval_jaxpr/add | solution.py:96
  367.9 8.9 %conditional.6 = (bf16[32,8192]{1,0:T(8,128)(2,1)S(1)}, f32[8192,128]{1,0:T(8,128)}, f32[8192,128]{1,0:T(8,128)}, f32[8192,128]{1,0:T(8,128)}, f32[8192,128]{1,0:T(8,128)}) conditional(s32[]{:T(128)} %convert_element_type.326, () %tuple.115, (pred[]{:T(512)}, bf16[4,32,8192]{2,1,0:T(8,128)(2,1)}, s32[]{:T(128)}, bf16[32,8192]{1,0:T(8,128)(2,1)}, ...), branch_computations={%region_8.8_spmd, %region_9.16_spmd} | conditional | flops 758479040 | bytes 96698248 | solution.py:95
  379.3 9.9 %select_add_fusion.7 = (f32[8192,128]{1,0:T(8,128)}, f32[8192,128]{1,0:T(8,128)}) fusion(f32[8192,128]{1,0:T(8,128)} %get-tuple-element.1022, f32[8192,128]{1,0:T(8,128)} %get-tuple-element.1106, pred[]{:T(512)S(6)} %compare.3, f32[8192,128]{1,0:T(8,128)} %get-tuple-element.1023, f32[8192,128]{1,0:T(8,128)} %get-tuple-element.1105), kind=kLoop, calls=%fused_computation.93.clone.1 | loop fusion | flops 4194304 | bytes 25165824 | tf_op jit(solution)/shard_map/while/body/eval_jaxpr/add | solution.py:96
  389.2 9.9 %select_add_fusion.6 = (f32[8192,128]{1,0:T(8,128)}, f32[8192,128]{1,0:T(8,128)}) fusion(f32[8192,128]{1,0:T(8,128)} %get-tuple-element.1018, f32[8192,128]{1,0:T(8,128)} %get-tuple-element.1104, pred[]{:T(512)S(6)} %compare.3, f32[8192,128]{1,0:T(8,128)} %get-tuple-element.1019, f32[8192,128]{1,0:T(8,128)} %get-tuple-element.1103), kind=kLoop, calls=%fused_computation.95.clone.1 | loop fusion | flops 4194304 | bytes 25165824 | tf_op jit(solution)/shard_map/while/body/eval_jaxpr/add | solution.py:96
  400.0 19.2 %collective-permute-done.1 = bf16[32,8192]{1,0:T(8,128)(2,1)S(1)} collective-permute-done((bf16[32,8192]{1,0:T(8,128)(2,1)S(1)}, bf16[32,8192]{1,0:T(8,128)(2,1)S(1)}, u32[]{:S(2)}, u32[]{:S(2)}) %collective-permute-start.1) | collective-permute-done | bytes 524320 | tf_op jit(solution)/shard_map/while/body/eval_jaxpr/ppermute | solution.py:10
  420.0 23.7 %conditional.6 = (bf16[32,8192]{1,0:T(8,128)(2,1)S(1)}, f32[8192,128]{1,0:T(8,128)}, f32[8192,128]{1,0:T(8,128)}, f32[8192,128]{1,0:T(8,128)}, f32[8192,128]{1,0:T(8,128)}) conditional(s32[]{:T(128)} %convert_element_type.326, () %tuple.115, (pred[]{:T(512)}, bf16[4,32,8192]{2,1,0:T(8,128)(2,1)}, s32[]{:T(128)}, bf16[32,8192]{1,0:T(8,128)(2,1)}, ...), branch_computations={%region_8.8_spmd, %region_9.16_spmd} | conditional | flops 758479040 | bytes 96698248 | solution.py:95
  446.1 9.9 %select_add_fusion.7 = (f32[8192,128]{1,0:T(8,128)}, f32[8192,128]{1,0:T(8,128)}) fusion(f32[8192,128]{1,0:T(8,128)} %get-tuple-element.1022, f32[8192,128]{1,0:T(8,128)} %get-tuple-element.1106, pred[]{:T(512)S(6)} %compare.3, f32[8192,128]{1,0:T(8,128)} %get-tuple-element.1023, f32[8192,128]{1,0:T(8,128)} %get-tuple-element.1105), kind=kLoop, calls=%fused_computation.93.clone.1 | loop fusion | flops 4194304 | bytes 25165824 | tf_op jit(solution)/shard_map/while/body/eval_jaxpr/add | solution.py:96
  456.0 9.9 %select_add_fusion.6 = (f32[8192,128]{1,0:T(8,128)}, f32[8192,128]{1,0:T(8,128)}) fusion(f32[8192,128]{1,0:T(8,128)} %get-tuple-element.1018, f32[8192,128]{1,0:T(8,128)} %get-tuple-element.1104, pred[]{:T(512)S(6)} %compare.3, f32[8192,128]{1,0:T(8,128)} %get-tuple-element.1019, f32[8192,128]{1,0:T(8,128)} %get-tuple-element.1103), kind=kLoop, calls=%fused_computation.95.clone.1 | loop fusion | flops 4194304 | bytes 25165824 | tf_op jit(solution)/shard_map/while/body/eval_jaxpr/add | solution.py:96
  468.2 23.7 %conditional.6 = (bf16[32,8192]{1,0:T(8,128)(2,1)S(1)}, f32[8192,128]{1,0:T(8,128)}, f32[8192,128]{1,0:T(8,128)}, f32[8192,128]{1,0:T(8,128)}, f32[8192,128]{1,0:T(8,128)}) conditional(s32[]{:T(128)} %convert_element_type.326, () %tuple.115, (pred[]{:T(512)}, bf16[4,32,8192]{2,1,0:T(8,128)(2,1)}, s32[]{:T(128)}, bf16[32,8192]{1,0:T(8,128)(2,1)}, ...), branch_computations={%region_8.8_spmd, %region_9.16_spmd} | conditional | flops 758479040 | bytes 96698248 | solution.py:95
  494.3 9.9 %select_add_fusion.7 = (f32[8192,128]{1,0:T(8,128)}, f32[8192,128]{1,0:T(8,128)}) fusion(f32[8192,128]{1,0:T(8,128)} %get-tuple-element.1022, f32[8192,128]{1,0:T(8,128)} %get-tuple-element.1106, pred[]{:T(512)S(6)} %compare.3, f32[8192,128]{1,0:T(8,128)} %get-tuple-element.1023, f32[8192,128]{1,0:T(8,128)} %get-tuple-element.1105), kind=kLoop, calls=%fused_computation.93.clone.1 | loop fusion | flops 4194304 | bytes 25165824 | tf_op jit(solution)/shard_map/while/body/eval_jaxpr/add | solution.py:96
  504.2 9.9 %select_add_fusion.6 = (f32[8192,128]{1,0:T(8,128)}, f32[8192,128]{1,0:T(8,128)}) fusion(f32[8192,128]{1,0:T(8,128)} %get-tuple-element.1018, f32[8192,128]{1,0:T(8,128)} %get-tuple-element.1104, pred[]{:T(512)S(6)} %compare.3, f32[8192,128]{1,0:T(8,128)} %get-tuple-element.1019, f32[8192,128]{1,0:T(8,128)} %get-tuple-element.1103), kind=kLoop, calls=%fused_computation.95.clone.1 | loop fusion | flops 4194304 | bytes 25165824 | tf_op jit(solution)/shard_map/while/body/eval_jaxpr/add | solution.py:96
  516.5 23.7 %conditional.6 = (bf16[32,8192]{1,0:T(8,128)(2,1)S(1)}, f32[8192,128]{1,0:T(8,128)}, f32[8192,128]{1,0:T(8,128)}, f32[8192,128]{1,0:T(8,128)}, f32[8192,128]{1,0:T(8,128)}) conditional(s32[]{:T(128)} %convert_element_type.326, () %tuple.115, (pred[]{:T(512)}, bf16[4,32,8192]{2,1,0:T(8,128)(2,1)}, s32[]{:T(128)}, bf16[32,8192]{1,0:T(8,128)(2,1)}, ...), branch_computations={%region_8.8_spmd, %region_9.16_spmd} | conditional | flops 758479040 | bytes 96698248 | solution.py:95
  542.5 9.9 %select_add_fusion.7 = (f32[8192,128]{1,0:T(8,128)}, f32[8192,128]{1,0:T(8,128)}) fusion(f32[8192,128]{1,0:T(8,128)} %get-tuple-element.1022, f32[8192,128]{1,0:T(8,128)} %get-tuple-element.1106, pred[]{:T(512)S(6)} %compare.3, f32[8192,128]{1,0:T(8,128)} %get-tuple-element.1023, f32[8192,128]{1,0:T(8,128)} %get-tuple-element.1105), kind=kLoop, calls=%fused_computation.93.clone.1 | loop fusion | flops 4194304 | bytes 25165824 | tf_op jit(solution)/shard_map/while/body/eval_jaxpr/add | solution.py:96
  552.4 9.9 %select_add_fusion.6 = (f32[8192,128]{1,0:T(8,128)}, f32[8192,128]{1,0:T(8,128)}) fusion(f32[8192,128]{1,0:T(8,128)} %get-tuple-element.1018, f32[8192,128]{1,0:T(8,128)} %get-tuple-element.1104, pred[]{:T(512)S(6)} %compare.3, f32[8192,128]{1,0:T(8,128)} %get-tuple-element.1019, f32[8192,128]{1,0:T(8,128)} %get-tuple-element.1103), kind=kLoop, calls=%fused_computation.95.clone.1 | loop fusion | flops 4194304 | bytes 25165824 | tf_op jit(solution)/shard_map/while/body/eval_jaxpr/add | solution.py:96
  564.7 23.7 %conditional.6 = (bf16[32,8192]{1,0:T(8,128)(2,1)S(1)}, f32[8192,128]{1,0:T(8,128)}, f32[8192,128]{1,0:T(8,128)}, f32[8192,128]{1,0:T(8,128)}, f32[8192,128]{1,0:T(8,128)}) conditional(s32[]{:T(128)} %convert_element_type.326, () %tuple.115, (pred[]{:T(512)}, bf16[4,32,8192]{2,1,0:T(8,128)(2,1)}, s32[]{:T(128)}, bf16[32,8192]{1,0:T(8,128)(2,1)}, ...), branch_computations={%region_8.8_spmd, %region_9.16_spmd} | conditional | flops 758479040 | bytes 96698248 | solution.py:95
  590.7 9.9 %select_add_fusion.7 = (f32[8192,128]{1,0:T(8,128)}, f32[8192,128]{1,0:T(8,128)}) fusion(f32[8192,128]{1,0:T(8,128)} %get-tuple-element.1022, f32[8192,128]{1,0:T(8,128)} %get-tuple-element.1106, pred[]{:T(512)S(6)} %compare.3, f32[8192,128]{1,0:T(8,128)} %get-tuple-element.1023, f32[8192,128]{1,0:T(8,128)} %get-tuple-element.1105), kind=kLoop, calls=%fused_computation.93.clone.1 | loop fusion | flops 4194304 | bytes 25165824 | tf_op jit(solution)/shard_map/while/body/eval_jaxpr/add | solution.py:96
  600.7 9.9 %select_add_fusion.6 = (f32[8192,128]{1,0:T(8,128)}, f32[8192,128]{1,0:T(8,128)}) fusion(f32[8192,128]{1,0:T(8,128)} %get-tuple-element.1018, f32[8192,128]{1,0:T(8,128)} %get-tuple-element.1104, pred[]{:T(512)S(6)} %compare.3, f32[8192,128]{1,0:T(8,128)} %get-tuple-element.1019, f32[8192,128]{1,0:T(8,128)} %get-tuple-element.1103), kind=kLoop, calls=%fused_computation.95.clone.1 | loop fusion | flops 4194304 | bytes 25165824 | tf_op jit(solution)/shard_map/while/body/eval_jaxpr/add | solution.py:96
  627.4 25.3 %reduce-scatter.5.cloned.1.call-done = bf16[1,1024,128]{2,1,0:T(8,128)(2,1)} async-done(((bf16[1,8192,128]{2,1,0:T(8,128)(2,1)}), bf16[1,1024,128]{2,1,0:T(8,128)(2,1)}) %reduce-scatter.5.cloned.1.call-update) | async-done | bytes 262160 | tf_op jit(solution)/shard_map/reduce_scatter | solution.py:109
  654.5 34.9 %reduce-scatter.7.cloned.1.call-done = bf16[1,1024,128]{2,1,0:T(8,128)(2,1)} async-done(((bf16[1,8192,128]{2,1,0:T(8,128)(2,1)}), bf16[1,1024,128]{2,1,0:T(8,128)(2,1)}) %reduce-scatter.7.cloned.1.call-update) | async-done | bytes 262160 | tf_op jit(solution)/shard_map/reduce_scatter | solution.py:112
  691.2 35.0 %reduce-scatter.9.cloned.1.call-done = bf16[1,1024,128]{2,1,0:T(8,128)(2,1)} async-done(((bf16[1,8192,128]{2,1,0:T(8,128)(2,1)}), bf16[1,1024,128]{2,1,0:T(8,128)(2,1)}) %reduce-scatter.9.cloned.1.call-update) | async-done | bytes 262160 | tf_op jit(solution)/shard_map/reduce_scatter | solution.py:115
  727.9 35.0 %reduce-scatter.11.cloned.1.call-done = bf16[1,1024,128]{2,1,0:T(8,128)(2,1)} async-done(((bf16[1,8192,128]{2,1,0:T(8,128)(2,1)}), bf16[1,1024,128]{2,1,0:T(8,128)(2,1)}) %reduce-scatter.11.cloned.1.call-update) | async-done | bytes 262160 | tf_op jit(solution)/shard_map/reduce_scatter | solution.py:118
  (324 shorter events, 244.6 us)
Async XLA Ops:
  7.2 126.4 %copy-start.10 = (s32[1,4,32]{2,1,0:T(4,128)S(1)}, s32[1,4,32]{2,1,0:T(4,128)}, u32[]{:S(2)}) copy-start(s32[1,4,32]{2,1,0:T(4,128)} %param.16) | copy-start | bytes 1540
  7.2 34.3 %all-gather.5.cloned.1.call-start = ((), (), s32[]{:S(2)}) async-start(), calls=%async_computation.4 | async-start | bytes 2359296 | tf_op jit(solution)/shard_map/all_gather | solution.py:37
  7.9 63.8 %all-gather.7.cloned.1.call-start = ((), (), s32[]{:S(2)}) async-start(), calls=%async_computation.5 | async-start | bytes 2359296 | tf_op jit(solution)/shard_map/all_gather | solution.py:38
  8.7 93.2 %all-gather.9.cloned.1.call-start = ((), (), s32[]{:S(2)}) async-start(), calls=%async_computation.6 | async-start | bytes 2359296 | tf_op jit(solution)/shard_map/all_gather | solution.py:39
  9.4 122.6 %all-gather.11.cloned.1.call-start = ((), (), s32[]{:S(2)}) async-start(), calls=%async_computation.7 | async-start | bytes 2359296 | tf_op jit(solution)/shard_map/all_gather | solution.py:40
  10.0 642.8 %reduce-scatter.5.cloned.1.call-start = ((), (), s32[]{:S(2)}) async-start(), calls=%async_computation.8 | async-start | bytes 2359296 | tf_op jit(solution)/shard_map/reduce_scatter | solution.py:109
  41.4 92.1 %copy-start = (bf16[1,8192,128]{2,1,0:T(8,128)(2,1)S(1)}, bf16[1,8192,128]{2,1,0:T(8,128)(2,1)}, u32[]{:S(2)}) copy-start(bf16[1,8192,128]{2,1,0:T(8,128)(2,1)} %all-gather.5.cloned.1.call-done) | copy-start | bytes 6291460
  145.3 13.4 %collective-permute-start = (bf16[32,8192]{1,0:T(8,128)(2,1)}, bf16[32,8192]{1,0:T(8,128)(2,1)S(1)}, u32[]{:S(2)}, u32[]{:S(2)}) collective-permute-start(bf16[32,8192]{1,0:T(8,128)(2,1)} %copy-done.9), channel_id=1, source_target_pairs={{0,8},{8,16},{16,24},{1,9},{9,17},{17,25},{2,10},{10,18},{18,26},{... | collective-permute-start | bytes 1572872 | tf_op jit(solution)/shard_map/while/body/eval_jaxpr/ppermute | solution.py:10
  170.4 15.7 %collective-permute-start = (bf16[32,8192]{1,0:T(8,128)(2,1)}, bf16[32,8192]{1,0:T(8,128)(2,1)S(1)}, u32[]{:S(2)}, u32[]{:S(2)}) collective-permute-start(bf16[32,8192]{1,0:T(8,128)(2,1)} %copy-done.9), channel_id=1, source_target_pairs={{0,8},{8,16},{16,24},{1,9},{9,17},{17,25},{2,10},{10,18},{18,26},{... | collective-permute-start | bytes 1572872 | tf_op jit(solution)/shard_map/while/body/eval_jaxpr/ppermute | solution.py:10
  197.8 14.7 %collective-permute-start = (bf16[32,8192]{1,0:T(8,128)(2,1)}, bf16[32,8192]{1,0:T(8,128)(2,1)S(1)}, u32[]{:S(2)}, u32[]{:S(2)}) collective-permute-start(bf16[32,8192]{1,0:T(8,128)(2,1)} %copy-done.9), channel_id=1, source_target_pairs={{0,8},{8,16},{16,24},{1,9},{9,17},{17,25},{2,10},{10,18},{18,26},{... | collective-permute-start | bytes 1572872 | tf_op jit(solution)/shard_map/while/body/eval_jaxpr/ppermute | solution.py:10
  224.3 13.8 %collective-permute-start = (bf16[32,8192]{1,0:T(8,128)(2,1)}, bf16[32,8192]{1,0:T(8,128)(2,1)S(1)}, u32[]{:S(2)}, u32[]{:S(2)}) collective-permute-start(bf16[32,8192]{1,0:T(8,128)(2,1)} %copy-done.9), channel_id=1, source_target_pairs={{0,8},{8,16},{16,24},{1,9},{9,17},{17,25},{2,10},{10,18},{18,26},{... | collective-permute-start | bytes 1572872 | tf_op jit(solution)/shard_map/while/body/eval_jaxpr/ppermute | solution.py:10
  242.1 21.3 %collective-permute-start = (bf16[32,8192]{1,0:T(8,128)(2,1)}, bf16[32,8192]{1,0:T(8,128)(2,1)S(1)}, u32[]{:S(2)}, u32[]{:S(2)}) collective-permute-start(bf16[32,8192]{1,0:T(8,128)(2,1)} %copy-done.9), channel_id=1, source_target_pairs={{0,8},{8,16},{16,24},{1,9},{9,17},{17,25},{2,10},{10,18},{18,26},{... | collective-permute-start | bytes 1572872 | tf_op jit(solution)/shard_map/while/body/eval_jaxpr/ppermute | solution.py:10
  267.5 13.2 %collective-permute-start = (bf16[32,8192]{1,0:T(8,128)(2,1)}, bf16[32,8192]{1,0:T(8,128)(2,1)S(1)}, u32[]{:S(2)}, u32[]{:S(2)}) collective-permute-start(bf16[32,8192]{1,0:T(8,128)(2,1)} %copy-done.9), channel_id=1, source_target_pairs={{0,8},{8,16},{16,24},{1,9},{9,17},{17,25},{2,10},{10,18},{18,26},{... | collective-permute-start | bytes 1572872 | tf_op jit(solution)/shard_map/while/body/eval_jaxpr/ppermute | solution.py:10
  284.7 20.0 %collective-permute-start = (bf16[32,8192]{1,0:T(8,128)(2,1)}, bf16[32,8192]{1,0:T(8,128)(2,1)S(1)}, u32[]{:S(2)}, u32[]{:S(2)}) collective-permute-start(bf16[32,8192]{1,0:T(8,128)(2,1)} %copy-done.9), channel_id=1, source_target_pairs={{0,8},{8,16},{16,24},{1,9},{9,17},{17,25},{2,10},{10,18},{18,26},{... | collective-permute-start | bytes 1572872 | tf_op jit(solution)/shard_map/while/body/eval_jaxpr/ppermute | solution.py:10
  315.9 18.3 %collective-permute-start.1 = (bf16[32,8192]{1,0:T(8,128)(2,1)S(1)}, bf16[32,8192]{1,0:T(8,128)(2,1)S(1)}, u32[]{:S(2)}, u32[]{:S(2)}) collective-permute-start(bf16[32,8192]{1,0:T(8,128)(2,1)S(1)} %get-tuple-element.1017), channel_id=1, source_target_pairs={{8,0},{16,8},{24,16},{9,1},{17,9},{25,17},{10,2},{18,10},{26,18},{... | collective-permute-start | bytes 1572872 | tf_op jit(solution)/shard_map/while/body/eval_jaxpr/ppermute | solution.py:10
  344.0 23.1 %collective-permute-start.1 = (bf16[32,8192]{1,0:T(8,128)(2,1)S(1)}, bf16[32,8192]{1,0:T(8,128)(2,1)S(1)}, u32[]{:S(2)}, u32[]{:S(2)}) collective-permute-start(bf16[32,8192]{1,0:T(8,128)(2,1)S(1)} %get-tuple-element.1017), channel_id=1, source_target_pairs={{8,0},{16,8},{24,16},{9,1},{17,9},{25,17},{10,2},{18,10},{26,18},{... | collective-permute-start | bytes 1572872 | tf_op jit(solution)/shard_map/while/body/eval_jaxpr/ppermute | solution.py:10
  376.9 42.3 %collective-permute-start.1 = (bf16[32,8192]{1,0:T(8,128)(2,1)S(1)}, bf16[32,8192]{1,0:T(8,128)(2,1)S(1)}, u32[]{:S(2)}, u32[]{:S(2)}) collective-permute-start(bf16[32,8192]{1,0:T(8,128)(2,1)S(1)} %get-tuple-element.1017), channel_id=1, source_target_pairs={{8,0},{16,8},{24,16},{9,1},{17,9},{25,17},{10,2},{18,10},{26,18},{... | collective-permute-start | bytes 1572872 | tf_op jit(solution)/shard_map/while/body/eval_jaxpr/ppermute | solution.py:10
  420.0 3.8 copy-start.4
  421.4 3.2 copy-start.2
  424.6 1.7 copy-start.6
  436.2 4.0 copy-start.1
  440.2 1.6 copy-start.3
  440.2 2.2 copy-start.5
  443.7 23.7 %collective-permute-start.1 = (bf16[32,8192]{1,0:T(8,128)(2,1)S(1)}, bf16[32,8192]{1,0:T(8,128)(2,1)S(1)}, u32[]{:S(2)}, u32[]{:S(2)}) collective-permute-start(bf16[32,8192]{1,0:T(8,128)(2,1)S(1)} %get-tuple-element.1017), channel_id=1, source_target_pairs={{8,0},{16,8},{24,16},{9,1},{17,9},{25,17},{10,2},{18,10},{26,18},{... | collective-permute-start | bytes 1572872 | tf_op jit(solution)/shard_map/while/body/eval_jaxpr/ppermute | solution.py:10
  468.2 3.8 copy-start.4
  469.6 3.2 copy-start.2
  472.8 1.7 copy-start.6
  484.4 4.0 copy-start.1
  488.4 1.6 copy-start.3
  488.4 2.2 copy-start.5
  491.9 23.7 %collective-permute-start.1 = (bf16[32,8192]{1,0:T(8,128)(2,1)S(1)}, bf16[32,8192]{1,0:T(8,128)(2,1)S(1)}, u32[]{:S(2)}, u32[]{:S(2)}) collective-permute-start(bf16[32,8192]{1,0:T(8,128)(2,1)S(1)} %get-tuple-element.1017), channel_id=1, source_target_pairs={{8,0},{16,8},{24,16},{9,1},{17,9},{25,17},{10,2},{18,10},{26,18},{... | collective-permute-start | bytes 1572872 | tf_op jit(solution)/shard_map/while/body/eval_jaxpr/ppermute | solution.py:10
  516.5 3.8 copy-start.4
  517.9 3.2 copy-start.2
  521.0 1.7 copy-start.6
  532.6 4.0 copy-start.1
  536.6 1.6 copy-start.3
  536.6 2.2 copy-start.5
  540.1 23.7 %collective-permute-start.1 = (bf16[32,8192]{1,0:T(8,128)(2,1)S(1)}, bf16[32,8192]{1,0:T(8,128)(2,1)S(1)}, u32[]{:S(2)}, u32[]{:S(2)}) collective-permute-start(bf16[32,8192]{1,0:T(8,128)(2,1)S(1)} %get-tuple-element.1017), channel_id=1, source_target_pairs={{8,0},{16,8},{24,16},{9,1},{17,9},{25,17},{10,2},{18,10},{26,18},{... | collective-permute-start | bytes 1572872 | tf_op jit(solution)/shard_map/while/body/eval_jaxpr/ppermute | solution.py:10
  564.7 3.8 copy-start.4
  566.1 3.2 copy-start.2
  569.2 1.7 copy-start.6
  580.8 4.0 copy-start.1
  584.8 1.6 copy-start.3
  584.8 2.2 copy-start.5
  588.4 23.1 %collective-permute-start.1 = (bf16[32,8192]{1,0:T(8,128)(2,1)S(1)}, bf16[32,8192]{1,0:T(8,128)(2,1)S(1)}, u32[]{:S(2)}, u32[]{:S(2)}) collective-permute-start(bf16[32,8192]{1,0:T(8,128)(2,1)S(1)} %get-tuple-element.1017), channel_id=1, source_target_pairs={{8,0},{16,8},{24,16},{9,1},{17,9},{25,17},{10,2},{18,10},{26,18},{... | collective-permute-start | bytes 1572872 | tf_op jit(solution)/shard_map/while/body/eval_jaxpr/ppermute | solution.py:10
  616.0 73.4 %reduce-scatter.7.cloned.1.call-start = ((), (), s32[]{:S(2)}) async-start(), calls=%async_computation.9 | async-start | bytes 2359296 | tf_op jit(solution)/shard_map/reduce_scatter | solution.py:112
  619.8 106.3 %reduce-scatter.9.cloned.1.call-start = ((), (), s32[]{:S(2)}) async-start(), calls=%async_computation.10 | async-start | bytes 2359296 | tf_op jit(solution)/shard_map/reduce_scatter | solution.py:115
  623.6 139.3 %reduce-scatter.11.cloned.1.call-start = ((), (), s32[]{:S(2)}) async-start(), calls=%async_computation.11 | async-start | bytes 2359296 | tf_op jit(solution)/shard_map/reduce_scatter | solution.py:118
  (18 other events, 16.2 us)
Sparse Core Ops, SparseCore 0:
  9.6 31.7 all-gather.4
  43.0 28.5 all-gather.6
  73.3 28.5 all-gather.8
  103.4 28.5 all-gather.10
  616.1 36.5 reduce-scatter.4
  654.9 34.4 reduce-scatter.6
  691.7 34.4 reduce-scatter.8
  728.4 34.4 reduce-scatter.10
where the time goes:
time: 774 us; the launch traced here: 772 us
  waiting for transfers between devices  343 us (44%)
  other arithmetic  191 us (25%)
  matrix products  108 us (14%)
  local copies, waits for them, and re-layouts  59.5 us (8%)
  starting transfers between devices  54.1 us (7%)
  between operations  14.2 us (2%)
    add x14, other arithmetic, backward_tick(): totals = tuple((total + part for total, part in zip(totals, parts)))  134 us
    ppermute x14, waiting for transfers between devices, shifted(): return lax.ppermute(block, axis, route)  88.6 us
    ppermute x14, starting transfers between devices, shifted(): return lax.ppermute(block, axis, route)  53.8 us
    reduce_scatter x1, waiting for transfers between devices, shards(): lax.psum_scatter(totals[3].astype(jnp.bfloat16)[None], 'dp', scatter_dime...  35 us
    reduce_scatter x1, waiting for transfers between devices, shards(): lax.psum_scatter(totals[2].astype(jnp.bfloat16)[None], 'dp', scatter_dime...  35 us
    reduce_scatter x1, waiting for transfers between devices, shards(): lax.psum_scatter(totals[1].astype(jnp.bfloat16)[None], 'dp', scatter_dime...  34.9 us
    dot_general x16, matrix products, section(): jnp.dot(normed, w_key, preferred_element_type=jnp.float32)  32.3 us
    all_gather x1, waiting for transfers between devices, shards(): lax.all_gather(w_query, 'dp', axis=1, tiled=True)  31.4 us
  transfers between devices with their start and end apart: 22, of which 19 were waited for; matrix products, arithmetic and copies ran while one was open for 21% of the time, Pallas kernels for 0%

commit v1 on v0

v1 whole, which is shorter than its diff:
```python
import functools

import jax
import jax.numpy as jnp
from jax import lax
from jax.experimental import pallas as pl
from jax.experimental.pallas import tpu as pltpu
from jax.sharding import PartitionSpec as P

BF = jnp.bfloat16
F32 = jnp.float32
NN = (((1,), (0,)), ((), ()))
NT = (((1,), (1,)), ((), ()))
TN = (((0,), (0,)), ((), ()))
VMEM_BYTES = 56 * 2**20
CORES = 2


def dot(a, b, dims=NN):
    return lax.dot_general(a, b, dims, preferred_element_type=F32)


def hop(block, axis, step):
    return lax.ppermute(block, axis, [(i, i ^ step) for i in range(lax.axis_size(axis))])


def place():
    b = lax.axis_index("dp")
    return lax.axis_index("pipe"), b // CORES, b % CORES


def vmem(count):
    return [pl.BlockSpec(memory_space=pltpu.VMEM)] * count


def anywhere(count):
    return [pl.BlockSpec(memory_space=pl.ANY)] * count


def pack(features, cots, chips):
    _, total, seq, width = features.shape
    group = total // lax.axis_size("pipe")
    eighth = width // (chips * CORES)

    def kernel(x_ref, g_ref, *rest):
        outs, sems = rest[:chips], rest[chips]
        p, z, c = place()
        copies = []
        for k in range(chips):
            for h in range(CORES):
                start = pl.multiple_of(((z ^ k) * CORES + (c ^ h)) * eighth, eighth)
                for a, ref in enumerate((x_ref, g_ref)):
                    copies.append(
                        pltpu.make_async_copy(
                            ref.at[0, pl.ds(p * group, group), :, pl.ds(start, eighth)],
                            outs[k].at[a, :, :, pl.ds(h * eighth, eighth)],
                            sems.at[len(copies)],
                        )
                    )
        for copy in copies:
            copy.start()
        for copy in copies:
            copy.wait()

    piece = jax.ShapeDtypeStruct((2, group, seq, CORES * eighth), BF)
    outs = pl.pallas_call(
        kernel,
        name="pack",
        out_shape=[piece] * chips,
        in_specs=anywhere(2),
        out_specs=vmem(chips),
        scratch_shapes=[pltpu.SemaphoreType.DMA((chips * CORES * 2,))],
    )(features, cots)
    return [out.reshape(2, group * seq, CORES * eighth) for out in outs]


def unpack(pieces, chips, width):
    rows, eighth = pieces[0].shape

    def kernel(*refs):
        ins, out, sems = refs[:-2], refs[-2], refs[-1]
        _, z, c = place()
        copies = []
        for k in range(chips):
            for h in range(CORES):
                start = pl.multiple_of(((z ^ k) * CORES + (c ^ h)) * eighth, eighth)
                copies.append(
                    pltpu.make_async_copy(
                        ins[k * CORES + h], out.at[:, pl.ds(start, eighth)], sems.at[len(copies)]
                    )
                )
        for copy in copies:
            copy.start()
        for copy in copies:
            copy.wait()

    return pl.pallas_call(
        kernel,
        name="unpack",
        out_shape=jax.ShapeDtypeStruct((rows, width), BF),
        in_specs=vmem(len(pieces)),
        out_specs=pl.BlockSpec(memory_space=pl.ANY),
        scratch_shapes=[pltpu.SemaphoreType.DMA((len(pieces),))],
    )(*pieces)


def project(tokens, own, other, head):
    chips, sections = len(tokens), len(own)
    rows = tokens[0].shape[1]
    half = own[0].shape[0]

    def kernel(*refs):
        tok = refs[:chips]
        ws = refs[chips : chips + sections]
        vs = refs[chips + sections : chips + 2 * sections]
        outs = refs[chips + 2 * sections : 2 * chips + 2 * sections]
        gram = refs[-1]
        p, _, c = place()
        h = jnp.concatenate([t[0] for t in tok], axis=0)
        g = jnp.concatenate([t[1] for t in tok], axis=0)
        for j in range(sections):
            a = dot(h[:, :half], ws[j][...]) + dot(h[:, half:], vs[j][...])
            b = dot(g[:, :half], ws[j][:, 3 * head :]) + dot(g[:, half:], vs[j][:, 3 * head :])
            for k in range(chips):
                outs[k][j, :, : 4 * head] = a[k * rows : (k + 1) * rows]
                outs[k][j, :, 4 * head :] = b[k * rows : (k + 1) * rows]

        def put(j, low, high, block):
            cols = slice(block * head, (block + 1) * head)
            gram[j] = sum(
                dot(w[low][:, 3 * head :], w[high][:, cols], TN) for w in (ws, vs)
            )

        put(0, 0, 0, 3)
        for j in range(1, sections):
            below = p < (p ^ j)
            for core in range(CORES):
                pl.when(below & (c == core))(functools.partial(put, j, 0, j, core))
                pl.when(jnp.logical_not(below) & (c == core))(
                    functools.partial(put, j, j, 0, CORES + core)
                )

    outs = pl.pallas_call(
        kernel,
        name="project",
        out_shape=[jax.ShapeDtypeStruct((sections, rows, 5 * head), F32)] * chips
        + [jax.ShapeDtypeStruct((sections, head, head), F32)],
        in_specs=vmem(chips + 2 * sections),
        out_specs=vmem(chips + 1),
        compiler_params=pltpu.CompilerParams(vmem_limit_bytes=VMEM_BYTES),
    )(*tokens, *own, *other)
    return outs[:chips], outs[chips]


def chain(partials, squares, docs, grams, head, width, seq):
    sections = len(grams)
    parts = len(partials)
    rows = squares.shape[0]
    lanes = sections * 4 * head

    def kernel(*refs):
        a_refs = refs[:parts]
        sq_ref, dr_ref, dc_ref = refs[parts : parts + 3]
        g_refs = refs[parts + 3 : parts + 3 + sections * CORES]
        out, a_all, hi, lo = refs[parts + 3 + sections * CORES :]
        p, _, c = place()
        for j in range(sections):
            total = a_refs[0][j]
            for ref in a_refs[1:]:
                total = total + ref[j]
            a_all[p ^ j] = total
        for i in range(sections):
            for h in range(CORES):
                for j in range(sections):
                    if j == 0 and h > 0:
                        continue
                    block = g_refs[i * CORES + h][j]
                    coarse = block.astype(BF)
                    fine = (block - coarse.astype(F32)).astype(BF)
                    one, two = p ^ i, p ^ i ^ j
                    low, high = jnp.minimum(one, two), jnp.maximum(one, two)
                    if j == 0:
                        kind = 3
                    else:
                        kind = jnp.where(one < two, 0, CORES) + (c ^ h)
                    hi[low, high, kind] = coarse
                    lo[low, high, kind] = fine

        def times(m, low, high, kind, dims=NN):
            return dot(m, hi[low, high, kind], dims) + dot(m, lo[low, high, kind], dims)

        places_r = lax.broadcasted_iota(jnp.int32, (rows, rows), 0)
        places_c = lax.broadcasted_iota(jnp.int32, (rows, rows), 1)
        allowed = (places_r >= places_c) & (dr_ref[...] == dc_ref[...])
        if rows > seq:
            allowed = allowed & (places_r // seq == places_c // seq)
        scale = head ** (-0.5)

        x = [[a_all[s, :, i * head : (i + 1) * head] for i in range(3)] for s in range(sections)]
        ho = [a_all[s, :, 3 * head : 4 * head] for s in range(sections)]
        bo = [a_all[s, :, 4 * head :] for s in range(sections)]
        norm = sq_ref[...]
        saved = []
        for s in range(sections):
            inv = lax.rsqrt(jnp.maximum(norm, 0.0) / width + 1e-05)
            q, k, v = ((part * inv).astype(BF) for part in x[s])
            scores = jnp.where(allowed, dot(q, k, NT) * scale, -1e30)
            highest = jnp.max(scores, axis=-1, keepdims=True)
            exponent = jnp.where(allowed, jnp.exp(scores - highest), 0.0)
            soft = exponent / jnp.sum(exponent, axis=-1, keepdims=True)
            attend = soft.astype(BF)
            mixed = dot(attend, v).astype(BF)
            saved.append((inv, q, k, v, soft, attend, mixed, list(ho)))
            if s < sections - 1:
                before = ho[s]
                for t in range(s + 1, sections):
                    x[t] = [x[t][i] + times(mixed, s, t, i) for i in range(3)]
                for t in range(sections - 1):
                    if t >= s:
                        ho[t] = ho[t] + times(mixed, s, t, 3)
                    else:
                        ho[t] = ho[t] + times(mixed, t, s, 3, NT)
                wide = mixed.astype(F32)
                norm = norm + jnp.sum(wide * (before + ho[s]), axis=-1, keepdims=True)

        lane = lax.broadcasted_iota(jnp.int32, (rows, head), 1)
        scalars = jnp.zeros((rows, head), F32)
        for s in reversed(range(sections)):
            inv, q, k, v, soft, attend, mixed, along = saved[s]
            d_mixed = bo[s].astype(BF)
            d_attend = dot(d_mixed, v, NT).astype(BF).astype(F32)
            d_values = dot(attend, d_mixed, TN)
            inner = jnp.sum(soft * d_attend, axis=-1, keepdims=True)
            d_scores = (soft * (d_attend - inner) * scale).astype(BF)
            d_query = dot(d_scores, k)
            d_keys = dot(d_scores, q, TN)
            y = [(part * inv).astype(BF) for part in (d_query, d_keys, d_values)]
            inner = sum(y[i].astype(F32) * x[s][i] for i in range(3))
            coef = inv * inv * jnp.sum(inner, axis=-1, keepdims=True) / width
            for t in range(s):
                add = sum(times(y[i], t, s, i, NT) for i in range(3))
                bo[t] = bo[t] + add - coef * along[t]
            at = s * 4 * head
            for i in range(3):
                out[:, at + i * head : at + (i + 1) * head] = y[i]
            out[:, at + 3 * head : at + 4 * head] = mixed
            coarse = coef.astype(BF).astype(F32)
            scalars = jnp.where(lane == 2 * s, coarse, scalars)
            scalars = jnp.where(lane == 2 * s + 1, coef - coarse, scalars)
        out[:, lanes:] = scalars.astype(BF)

    return pl.pallas_call(
        kernel,
        name="chain",
        out_shape=jax.ShapeDtypeStruct((rows, lanes + head), BF),
        in_specs=vmem(parts + 3 + sections * CORES),
        out_specs=pl.BlockSpec(memory_space=pltpu.VMEM),
        scratch_shapes=[
            pltpu.VMEM((sections, rows, 5 * head), F32),
            pltpu.VMEM((sections, sections, 4, head, head), BF),
            pltpu.VMEM((sections, sections, 4, head, head), BF),
        ],
        compiler_params=pltpu.CompilerParams(vmem_limit_bytes=VMEM_BYTES),
    )(*partials, squares, docs[:, None], docs[None, :], *[g for pair in grams for g in pair])


def factors(p, j, sections, head, section_of, scalars):
    s = p ^ j
    both = section_of(s)
    side = lax.broadcasted_iota(jnp.int32, scalars.shape, 1) // 2
    after = jnp.where((side > jnp.maximum(p, s)) & (side < sections), scalars, 0.0)
    share = jnp.where(s >= p, jnp.sum(after, axis=-1, keepdims=True), 0.0)
    y = both[:, : 3 * head]
    m = both[:, 3 * head :]
    into_g = (
        jnp.where(s > p, y, jnp.zeros_like(y)),
        (-share * m.astype(F32)).astype(BF),
    )
    into_h = jnp.where(s < p, m, jnp.zeros_like(m))
    return into_g, into_h, share


def rebuild(tokens, coefs, weights, column, columns, head):
    sections, chips = len(weights), len(tokens[0])
    rows, lanes = coefs[0][0].shape
    half = weights[0].shape[0]
    groups = len(tokens)
    count = groups * chips * rows
    block = min(256, half)
    steps = half // block
    flat_t = [t for line in tokens for t in line]
    flat_c = [t for line in coefs for t in line]

    def kernel(*refs):
        n = groups * chips
        t_refs, c_refs = refs[:n], refs[n : 2 * n]
        w_refs = refs[2 * n : 2 * n + sections]
        outs = refs[2 * n + sections : 2 * n + sections + chips]
        grads, left_g, left_h, own, edge = refs[2 * n + sections + chips :]
        p, _, _ = place()

        @pl.when(pl.program_id(0) == 0)
        def _():
            for i in range(n):
                at = pl.ds(i * rows, rows)
                scalars = c_refs[i][:, lanes - head :].astype(F32)
                ref = c_refs[i]

                def section_of(s, ref=ref):
                    return ref[:, pl.ds(pl.multiple_of(s * 4 * head, 4 * head), 4 * head)]

                for j in range(sections):
                    (g_y, g_m), into_h, share = factors(p, j, sections, head, section_of, scalars)
                    left_g[j, at, : 3 * head] = g_y
                    left_g[j, at, 3 * head :] = g_m
                    if j > 0:
                        left_h[j - 1, at, :] = into_h
                    else:
                        own[at, :] = section_of(p)
                        side = lax.broadcasted_iota(jnp.int32, scalars.shape, 1) // 2
                        here = jnp.where(side == p, scalars, 0.0)
                        here = jnp.sum(here, axis=-1, keepdims=True)
                        edge[0, at, :] = jnp.broadcast_to(share, (rows, head))
                        edge[1, at, :] = jnp.broadcast_to(here, (rows, head))

        h = jnp.concatenate([t[0] for t in t_refs], axis=0).astype(F32)
        g = jnp.concatenate([t[1] for t in t_refs], axis=0).astype(F32)
        for j in range(1, sections):
            h = h + dot(left_h[j - 1], w_refs[j][:, 3 * head :], NT)
        for j in range(sections):
            g = g + dot(left_g[j], w_refs[j][...], NT)
        g = g - edge[0][:, :1] * h
        y, m = own[:, : 3 * head], own[:, 3 * head :]
        grads[:, : 3 * head] = dot(h.astype(BF), y, TN)
        grads[:, 3 * head :] = dot(g.astype(BF), m, TN)
        result = (g + dot(y, w_refs[0][:, : 3 * head], NT) - edge[1][:, :1] * h).astype(BF)
        for j in range(groups):
            for k in range(chips):
                at = (j * chips + k) * rows
                outs[k][p ^ j] = result[at : at + rows]

    held = columns // block
    outs = pl.pallas_call(
        kernel,
        name="rebuild",
        grid=(steps,),
        out_shape=[jax.ShapeDtypeStruct((groups, rows, half), BF)] * chips
        + [jax.ShapeDtypeStruct((half, 4 * head), F32)],
        in_specs=[pl.BlockSpec((2, rows, block), lambda i: (0, 0, i + column // block))]
        * len(flat_t)
        + vmem(len(flat_c))
        + [pl.BlockSpec((block, 4 * head), lambda i: (i, 0))] * sections,
        out_specs=[pl.BlockSpec((groups, rows, block), lambda i: (0, 0, i))] * chips
        + [pl.BlockSpec((block, 4 * head), lambda i: (i, 0))],
        scratch_shapes=[
            pltpu.VMEM((sections, count, 4 * head), BF),
            pltpu.VMEM((sections - 1, count, head), BF),
            pltpu.VMEM((count, 4 * head), BF),
            pltpu.VMEM((2, count, head), F32),
        ],
        compiler_params=pltpu.CompilerParams(vmem_limit_bytes=VMEM_BYTES),
    )(*flat_t, *flat_c, *weights)
    return outs[:chips], outs[chips]


def rebuild_wide(tokens, coefs, weights, column, columns, head):
    sections, chips = len(weights), len(tokens[0])
    rows, lanes = coefs[0][0].shape
    half = weights[0].shape[0]
    p, _, _ = place()
    grads = jnp.zeros((half, 4 * head), F32)
    results = []
    for group, line in zip(tokens, coefs):
        both = jnp.concatenate([t[:, :, column : column + half] for t in group], axis=1)
        both, coef, grads = lax.optimization_barrier((both, jnp.concatenate(line, axis=0), grads))
        scalars = coef[:, lanes - head :].astype(F32)

        def section_of(s, coef=coef):
            return lax.dynamic_slice_in_dim(coef, s * 4 * head, 4 * head, axis=1)

        h, g = both[0].astype(F32), both[1].astype(F32)
        for j in range(sections):
            (g_y, g_m), into_h, share = factors(p, j, sections, head, section_of, scalars)
            h = h + dot(into_h, weights[j][:, 3 * head :], NT)
            g = g + dot(g_y, weights[j][:, : 3 * head], NT)
            g = g + dot(g_m, weights[j][:, 3 * head :], NT)
            if j == 0:
                ahead = share
        g = g - ahead * h
        own = section_of(p)
        y, m = own[:, : 3 * head], own[:, 3 * head :]
        side = lax.broadcasted_iota(jnp.int32, scalars.shape, 1) // 2
        here = jnp.sum(jnp.where(side == p, scalars, 0.0), axis=-1, keepdims=True)
        grads = grads + jnp.concatenate(
            [dot(h.astype(BF), y, TN), dot(g.astype(BF), m, TN)], axis=1
        )
        result = (g + dot(y, weights[0][:, : 3 * head], NT) - here * h).astype(BF)
        results.append(result.reshape(chips, rows, half))
    result = jnp.take(jnp.stack(results), jnp.arange(len(tokens)) ^ p, axis=0)
    return [result[:, k] for k in range(chips)], grads


def shards(inputs, segments, cotangent, w_query, w_key, w_value, w_out):
    sections = lax.axis_size("pipe")
    chips = lax.axis_size("dp") // CORES
    head = w_query.shape[2]
    _, batches, seq, width = inputs.shape
    section_id, _, _ = place()
    short = -batches % sections
    if short:
        fill = ((0, 0), (0, short), (0, 0), (0, 0))
        inputs, cotangent = jnp.pad(inputs, fill), jnp.pad(cotangent, fill)
        segments = jnp.pad(segments, fill[:3])
    group = inputs.shape[1] // sections
    rows = group * seq

    pieces = pack(inputs, cotangent, chips)
    mine = jnp.concatenate([w_query[0], w_key[0], w_value[0], w_out[0]], axis=1)
    pieces, mine = lax.optimization_barrier((pieces, mine))
    tokens = [pieces[0]] + [hop(pieces[k], "dp", k * CORES) for k in range(1, chips)]
    own = [mine] + [hop(mine, "pipe", j) for j in range(1, sections)]
    other = [hop(w, "dp", 1) for w in own]
    start = lax.dynamic_slice_in_dim(inputs[0], section_id * group, group, 0)
    start = start.reshape(rows, width).astype(F32)
    squares = jnp.sum(start * start, axis=-1, keepdims=True)
    docs = lax.dynamic_slice_in_dim(segments[0], section_id * group, group, 0).reshape(rows)

    partials, gram = project(tokens, own, other, head)
    partials = [partials[0]] + [hop(partials[k], "dp", k * CORES) for k in range(1, chips)]
    gram = sum([hop(gram, "dp", k * CORES) for k in range(1, chips)], gram)
    near = [gram] + [hop(gram, "pipe", j) for j in range(1, sections)]
    grams = [(g, hop(g, "dp", 1)) for g in near]

    coef = chain(partials, squares, docs, grams, head, width, seq)
    line = [coef] + [hop(coef, "dp", k * CORES) for k in range(1, chips)]
    coefs = [line] + [[hop(t, "pipe", j) for t in line] for j in range(1, sections)]
    spread = [tokens] + [[hop(t, "pipe", j) for t in tokens] for j in range(1, sections)]

    half = own[0].shape[0]
    form = rebuild if sections * chips * rows <= 1024 else rebuild_wide
    far, far_grads = form(spread, coefs, other, half, CORES * half, head)
    close, grads = form(spread, coefs, own, 0, CORES * half, head)
    grads = grads + hop(far_grads, "dp", 1)
    out = []
    for k in range(chips):
        for part in (close[k], far[k]):
            part = part.reshape(sections * rows, half)
            out.append(hop(part, "dp", k * CORES) if k else part)
    stored = unpack(out, chips, width)[: batches * seq]
    stored = stored.reshape(1, 1, batches, seq, width)
    return (stored,) + tuple(grads[None, :, i * head : (i + 1) * head] for i in range(4))


def solution(mesh):
    wide = P("dp", None, None, None)
    weight = P("pipe", "dp", None)
    return jax.shard_map(
        shards,
        mesh=mesh,
        in_specs=(wide, P("dp", None, None), wide, weight, weight, weight, weight),
        out_specs=(P("pipe", "dp", None, None, None), weight, weight, weight, weight),
        check_vma=False,
    )
```

time: 774 us -> 269 us (0.35)
  waiting for transfers between devices: 343 us -> 133 us
  other arithmetic: 191 us -> 4.44 us
  matrix products: 108 us -> 0 us
  local copies, waits for them, and re-layouts: 59.5 us -> 5.63 us
  Pallas kernels: 0 us -> 43.5 us
  starting transfers between devices: 54.1 us -> 79.1 us
  between operations: 14.2 us -> 1.18 us
    add x14 -> x2, other arithmetic: 134 us -> 3.07 us  [the longest x1 2.07 us: shards(): grads = grads + hop(far_grads, 'dp', 1)]
    reduce_scatter x4 -> x0, waiting for transfers between devices: 130 us -> none  [the longest x1 35 us: shards(): lax.psum_scatter(totals[3].astype(jnp.bfloat16)[None], 'dp', scatter_dime...]
    all_gather x4 -> x0, waiting for transfers between devices: 122 us -> none  [the longest x1 31.4 us: shards(): lax.all_gather(w_query, 'dp', axis=1, tiled=True)]
    dot_general x80 -> x0, matrix products: 108 us -> none  [the longest x16 32.3 us: section(): jnp.dot(normed, w_key, preferred_element_type=jnp.float32)]
    ppermute x14 -> x57, waiting for transfers between devices: 88.6 us -> 133 us  [hop(): lax.ppermute(block, axis, [(i, i ^ step) for i in range(lax.axis_size(axi...]
    pallas_call x0 -> x6, Pallas kernels: none -> 43.5 us  [the longest x2 22 us: rebuild(): pl.pallas_call(kernel, name='rebuild', grid=(steps,), out_shape=[jax.Shap...]
    another operation x22 -> x1, local copies, waits for them, and re-layouts: 30.8 us -> 0.69 us  [chain(): docs[:, None]]
    ppermute x14 -> x57, starting transfers between devices: 53.8 us -> 79.1 us  [hop(): lax.ppermute(block, axis, [(i, i ^ step) for i in range(lax.axis_size(axi...]
  transfers between devices with their start and end apart: 22 -> 57, of which waited for: 19 -> 21; matrix products, arithmetic and copies ran while one was open for 21% -> 2% of each run, Pallas kernels for 0% -> 11%
where the time goes in v1:
time: 269 us; the launch traced here: 267 us
  waiting for transfers between devices  133 us (49%)
  starting transfers between devices  79.1 us (29%)
  Pallas kernels  43.5 us (16%)
  local copies, waits for them, and re-layouts  5.63 us (2%)
  other arithmetic  4.44 us (2%)
    ppermute x57, waiting for transfers between devices, hop(): lax.ppermute(block, axis, [(i, i ^ step) for i in range(lax.axis_size(axi...  133 us
    ppermute x57, starting transfers between devices, hop(): lax.ppermute(block, axis, [(i, i ^ step) for i in range(lax.axis_size(axi...  79.1 us
    pallas_call x2, Pallas kernels, rebuild(): pl.pallas_call(kernel, name='rebuild', grid=(steps,), out_shape=[jax.Shap...  22 us
    pallas_call x1, Pallas kernels, chain(): pl.pallas_call(kernel, name='chain', out_shape=jax.ShapeDtypeStruct((rows...  8.06 us
    pallas_call x1, Pallas kernels, project(): pl.pallas_call(kernel, name='project', out_shape=[jax.ShapeDtypeStruct((s...  8.04 us
  transfers between devices with their start and end apart: 57, of which 21 were waited for; matrix products, arithmetic and copies ran while one was open for 2% of the time, Pallas kernels for 11%

profile of v1, /device:TPU:0, one launch (start us, length us, event | category | flops | bytes accessed | tf_op | source)
XLA Modules:
  0.0 267.3 jit_solution(16846873754102808212)
XLA Ops:
  0.7 2.4 pack.1
  3.3 4.0 %collective-permute-start.17 = (bf16[1024,512]{1,0:T(8,128)(2,1)S(1)}, bf16[1024,512]{1,0:T(8,128)(2,1)S(1)}, u32[]{:S(2)}, u32[]{:S(2)}) collective-permute-start(bf16[1024,512]{1,0:T(8,128)(2,1)S(1)} %pad_maximum_fusion.refs_4_.refs_32_), channel_id=1, source_target_pairs={{0,24},{8,16},{16,8},{24,0},{1,25},{9,17},{17,9},{25,1},{2,26},{10... | collective-permute-start | bytes 3145736 | tf_op jit(solution)/shard_map/ppermute | solution.py:24
  7.9 23.4 %collective-permute-done.17.refs_7_.refs_35_ = bf16[1024,512]{1,0:T(8,128)(2,1)S(1)} collective-permute-done((bf16[1024,512]{1,0:T(8,128)(2,1)S(1)}, bf16[1024,512]{1,0:T(8,128)(2,1)S(1)}, u32[]{:S(2)}, u32[]{:S(2)}) %collective-permute-start.17) | collective-permute-done | bytes 1048608 | tf_op jit(solution)/shard_map/ppermute | solution.py:24
  31.3 21.6 %collective-permute-done.16.refs_6_.refs_34_ = bf16[1024,512]{1,0:T(8,128)(2,1)S(1)} collective-permute-done((bf16[1024,512]{1,0:T(8,128)(2,1)S(1)}, bf16[1024,512]{1,0:T(8,128)(2,1)S(1)}, u32[]{:S(2)}, u32[]{:S(2)}) %collective-permute-start.16) | collective-permute-done | bytes 1048608 | tf_op jit(solution)/shard_map/ppermute | solution.py:24
  53.4 1.8 collective-permute-start
  55.2 6.7 %collective-permute-done.refs_1_ = bf16[2,32,2048]{2,1,0:T(8,128)(2,1)S(1)} collective-permute-done((bf16[2,32,2048]{2,1,0:T(8,128)(2,1)S(1)}, bf16[2,32,2048]{2,1,0:T(8,128)(2,1)S(1)}, u32[]{:S(2)}, u32[]{:S(2)}) %collective-permute-start) | collective-permute-done | bytes 262176 | tf_op jit(solution)/shard_map/ppermute | solution.py:24
  62.0 2.6 collective-permute-start.1
  64.5 11.6 %collective-permute-done.1.refs_2_ = bf16[2,32,2048]{2,1,0:T(8,128)(2,1)S(1)} collective-permute-done((bf16[2,32,2048]{2,1,0:T(8,128)(2,1)S(1)}, bf16[2,32,2048]{2,1,0:T(8,128)(2,1)S(1)}, u32[]{:S(2)}, u32[]{:S(2)}) %collective-permute-start.1) | collective-permute-done | bytes 262176 | tf_op jit(solution)/shard_map/ppermute | solution.py:24
  76.2 3.3 %collective-permute-start.2 = (bf16[2,32,2048]{2,1,0:T(8,128)(2,1)S(1)}, bf16[2,32,2048]{2,1,0:T(8,128)(2,1)S(1)}, u32[]{:S(2)}, u32[]{:S(2)}) collective-permute-start(bf16[2,32,2048]{2,1,0:T(8,128)(2,1)S(1)} %bitcast.50), channel_id=1, source_target_pairs={{0,6},{1,7},{2,4},{3,5},{4,2},{5,3},{6,0},{7,1},{8,14},{9,15},{10,... | collective-permute-start | bytes 786440 | tf_op jit(solution)/shard_map/ppermute | solution.py:24
  79.4 6.6 %collective-permute-done.2.refs_3_ = bf16[2,32,2048]{2,1,0:T(8,128)(2,1)S(1)} collective-permute-done((bf16[2,32,2048]{2,1,0:T(8,128)(2,1)S(1)}, bf16[2,32,2048]{2,1,0:T(8,128)(2,1)S(1)}, u32[]{:S(2)}, u32[]{:S(2)}) %collective-permute-start.2) | collective-permute-done | bytes 262176 | tf_op jit(solution)/shard_map/ppermute | solution.py:24
  86.0 1.7 collective-permute-start.11
  89.5 1.8 collective-permute-start.12
  91.4 8.0 %project.1 = (f32[4,32,640]{2,1,0:T(8,128)}, f32[4,32,640]{2,1,0:T(8,128)}, f32[4,32,640]{2,1,0:T(8,128)}, f32[4,32,640]{2,1,0:T(8,128)}, f32[4,128,128]{2,1,0:T(8,128)}) custom-call(bf16[2,32,2048]{2,1,0:T(8,128)(2,1)} %bitcast.30, bf16[2,32,2048]{2,1,0:T(8,128)(2,1)} %copy-done.8, bf16[2,32,2048]{2,1,0:T(8,128)(2,1)} %copy-done.9, ...), custom_call_target="tpu_custom_call" | custom-call | tf_op jit(solution)/shard_map/project/pallas_call | solution.py:143
  99.4 3.5 %collective-permute-start.27 = (f32[4,128,128]{2,1,0:T(8,128)}, f32[4,128,128]{2,1,0:T(8,128)S(1)}, u32[]{:S(2)}, u32[]{:S(2)}) collective-permute-start(f32[4,128,128]{2,1,0:T(8,128)} %get-tuple-element.42), channel_id=1, source_target_pairs={{0,6},{1,7},{2,4},{3,5},{4,2},{5,3},{6,0},{7,1},{8,14},{9,15},{10,... | collective-permute-start | bytes 786440 | tf_op jit(solution)/shard_map/ppermute | solution.py:24
  103.0 2.4 collective-permute-start.26
  106.3 1.5 collective-permute-start.8
  108.5 1.8 collective-permute-done.27
  111.6 12.9 %collective-permute-done.26 = f32[4,128,128]{2,1,0:T(8,128)S(1)} collective-permute-done((f32[4,128,128]{2,1,0:T(8,128)}, f32[4,128,128]{2,1,0:T(8,128)S(1)}, u32[]{:S(2)}, u32[]{:S(2)}) %collective-permute-start.26) | collective-permute-done | bytes 262176 | tf_op jit(solution)/shard_map/ppermute | solution.py:24
  125.3 3.3 %collective-permute-start.23 = (f32[4,32,640]{2,1,0:T(8,128)}, f32[4,32,640]{2,1,0:T(8,128)S(1)}, u32[]{:S(2)}, u32[]{:S(2)}) collective-permute-start(f32[4,32,640]{2,1,0:T(8,128)} %get-tuple-element.40), channel_id=1, source_target_pairs={{0,4},{1,5},{2,6},{3,7},{4,0},{5,1},{6,2},{7,3},{8,12},{9,13},{10,... | collective-permute-start | bytes 983048 | tf_op jit(solution)/shard_map/ppermute | solution.py:24
  130.9 1.5 collective-permute-start.31
  133.2 7.8 %collective-permute-done.22.refs_1_ = f32[4,32,640]{2,1,0:T(8,128)S(1)} collective-permute-done((f32[4,32,640]{2,1,0:T(8,128)}, f32[4,32,640]{2,1,0:T(8,128)S(1)}, u32[]{:S(2)}, u32[]{:S(2)}) %collective-permute-start.22) | collective-permute-done | bytes 327712 | tf_op jit(solution)/shard_map/ppermute | solution.py:24
  141.0 2.1 collective-permute-start.24
  144.7 7.1 %collective-permute-done.24.refs_3_ = f32[4,32,640]{2,1,0:T(8,128)S(1)} collective-permute-done((f32[4,32,640]{2,1,0:T(8,128)}, f32[4,32,640]{2,1,0:T(8,128)S(1)}, u32[]{:S(2)}, u32[]{:S(2)}) %collective-permute-start.24) | collective-permute-done | bytes 327712 | tf_op jit(solution)/shard_map/ppermute | solution.py:24
  153.5 1.8 collective-permute-start.14
  161.2 8.1 %chain.1.refs_16_ = bf16[32,2176]{1,0:T(8,128)(2,1)} custom-call(f32[4,32,640]{2,1,0:T(8,128)} %get-tuple-element.38.refs_0_, f32[4,32,640]{2,1,0:T(8,128)} %copy-done.35, f32[4,32,640]{2,1,0:T(8,128)} %copy-done.36, f32[4,32,640]{2,1,0:T(8,128)} %copy-done.37, f32[32,1]{1,0:T(8,128)} %copy.12.refs_4_, s32[32,1]{1,0:T(8,128)} %copy.13.refs_5_, ...), custom_call_target="tpu_custom_call" | custom-call | tf_op jit(solution)/shard_map/chain/pallas_call | solution.py:252
  169.3 1.7 collective-permute-start.46
  171.0 2.3 collective-permute-start.37
  175.2 5.5 %collective-permute-start.36 = (bf16[32,2176]{1,0:T(8,128)(2,1)}, bf16[32,2176]{1,0:T(8,128)(2,1)S(1)}, u32[]{:S(2)}, u32[]{:S(2)}) collective-permute-start(bf16[32,2176]{1,0:T(8,128)(2,1)} %chain.1.refs_16_), channel_id=1, source_target_pairs={{0,4},{1,5},{2,6},{3,7},{4,0},{5,1},{6,2},{7,3},{8,12},{9,13},{10,... | collective-permute-start | bytes 417800 | tf_op jit(solution)/shard_map/ppermute | solution.py:24
  180.7 2.5 collective-permute-start.35
  183.2 1.4 collective-permute-start.49
  190.5 1.5 collective-permute-start.40
  192.0 1.6 collective-permute-done.45.refs_27_
  193.6 1.4 collective-permute-start.47
  195.0 1.9 collective-permute-start.43
  198.2 1.6 collective-permute-done.47.refs_29_
  199.9 1.4 collective-permute-done.43.refs_25_
  202.8 11.0 %rebuild.3 = (bf16[4,32,1024]{2,1,0:T(8,128)(2,1)}, bf16[4,32,1024]{2,1,0:T(8,128)(2,1)}, bf16[4,32,1024]{2,1,0:T(8,128)(2,1)}, bf16[4,32,1024]{2,1,0:T(8,128)(2,1)}, f32[1024,512]{1,0:T(8,128)}) custom-call(bf16[2,32,2048]{2,1,0:T(8,128)(2,1)} %bitcast.31, bf16[2,32,2048]{2,1,0:T(8,128)(2,1)} %copy-done.8, bf16[2,32,2048]{2,1,0:T(8,128)(2,1)} %copy-done.9, ...), custom_call_target="tpu_custom_call" | custom-call | tf_op jit(solution)/shard_map/rebuild/pallas_call | solution.py:343
  213.9 2.2 collective-permute-start.51
  216.6 2.0 collective-permute-start.55
  218.6 11.0 %rebuild.2 = (bf16[4,32,1024]{2,1,0:T(8,128)(2,1)}, bf16[4,32,1024]{2,1,0:T(8,128)(2,1)}, bf16[4,32,1024]{2,1,0:T(8,128)(2,1)}, bf16[4,32,1024]{2,1,0:T(8,128)(2,1)}, f32[1024,512]{1,0:T(8,128)}) custom-call(bf16[2,32,2048]{2,1,0:T(8,128)(2,1)} %bitcast.32, bf16[2,32,2048]{2,1,0:T(8,128)(2,1)} %copy-done.8, bf16[2,32,2048]{2,1,0:T(8,128)(2,1)} %copy-done.9, ...), custom_call_target="tpu_custom_call" | custom-call | tf_op jit(solution)/shard_map/rebuild/pallas_call | solution.py:343
  230.7 1.4 collective-permute-start.52
  232.1 5.6 %collective-permute-done.53.refs_5_ = bf16[128,1024]{1,0:T(8,128)(2,1)S(1)} collective-permute-done((bf16[128,1024]{1,0:T(8,128)(2,1)}, bf16[128,1024]{1,0:T(8,128)(2,1)S(1)}, u32[]{:S(2)}, u32[]{:S(2)}) %collective-permute-start.53) | collective-permute-done | bytes 262176 | tf_op jit(solution)/shard_map/ppermute | solution.py:24
  237.7 1.8 collective-permute-start.54
  239.5 3.0 %collective-permute-done.50.refs_2_ = bf16[128,1024]{1,0:T(8,128)(2,1)S(1)} collective-permute-done((bf16[128,1024]{1,0:T(8,128)(2,1)}, bf16[128,1024]{1,0:T(8,128)(2,1)S(1)}, u32[]{:S(2)}, u32[]{:S(2)}) %collective-permute-start.50) | collective-permute-done | bytes 262176 | tf_op jit(solution)/shard_map/ppermute | solution.py:24
  242.6 17.7 %collective-permute-done.52.refs_4_ = bf16[128,1024]{1,0:T(8,128)(2,1)S(1)} collective-permute-done((bf16[128,1024]{1,0:T(8,128)(2,1)}, bf16[128,1024]{1,0:T(8,128)(2,1)S(1)}, u32[]{:S(2)}, u32[]{:S(2)}) %collective-permute-start.52) | collective-permute-done | bytes 262176 | tf_op jit(solution)/shard_map/ppermute | solution.py:24
  260.9 2.9 %unpack.1 = bf16[128,8192]{1,0:T(8,128)(2,1)} custom-call(bf16[128,1024]{1,0:T(8,128)(2,1)} %bitcast.38, bf16[128,1024]{1,0:T(8,128)(2,1)} %bitcast.37, bf16[128,1024]{1,0:T(8,128)(2,1)} %copy-done.41, bf16[128,1024]{1,0:T(8,128)(2,1)} %copy-done.38, bf16[128,1024]{1,0:T(8,128)(2,1)} %copy-done.42, bf16[128,1024]{1,0:T(8,128)(2,1)} %copy-done.39, ...), custom_call_target="tpu_custom_call" | custom-call | tf_op jit(solution)/shard_map/unpack/pallas_call | solution.py:97
  263.8 2.1 add.20
  265.9 1.4 slice_bitcast_fusion
  (194 shorter events, 32.1 us)
Async XLA Ops:
  3.3 28.0 %collective-permute-start.17 = (bf16[1024,512]{1,0:T(8,128)(2,1)S(1)}, bf16[1024,512]{1,0:T(8,128)(2,1)S(1)}, u32[]{:S(2)}, u32[]{:S(2)}) collective-permute-start(bf16[1024,512]{1,0:T(8,128)(2,1)S(1)} %pad_maximum_fusion.refs_4_.refs_32_), channel_id=1, source_target_pairs={{0,24},{8,16},{16,8},{24,0},{1,25},{9,17},{17,9},{25,1},{2,26},{10... | collective-permute-start | bytes 3145736 | tf_op jit(solution)/shard_map/ppermute | solution.py:24
  7.3 45.6 %collective-permute-start.16 = (bf16[1024,512]{1,0:T(8,128)(2,1)S(1)}, bf16[1024,512]{1,0:T(8,128)(2,1)S(1)}, u32[]{:S(2)}, u32[]{:S(2)}) collective-permute-start(bf16[1024,512]{1,0:T(8,128)(2,1)S(1)} %pad_maximum_fusion.refs_4_.refs_32_), channel_id=1, source_target_pairs={{0,16},{8,24},{16,0},{24,8},{1,17},{9,25},{17,1},{25,9},{2,18},{10... | collective-permute-start | bytes 3145736 | tf_op jit(solution)/shard_map/ppermute | solution.py:24
  7.8 45.4 %collective-permute-start.15 = (bf16[1024,512]{1,0:T(8,128)(2,1)S(1)}, bf16[1024,512]{1,0:T(8,128)(2,1)S(1)}, u32[]{:S(2)}, u32[]{:S(2)}) collective-permute-start(bf16[1024,512]{1,0:T(8,128)(2,1)S(1)} %pad_maximum_fusion.refs_4_.refs_32_), channel_id=1, source_target_pairs={{0,8},{8,0},{16,24},{24,16},{1,9},{9,1},{17,25},{25,17},{2,10},{10... | collective-permute-start | bytes 3145736 | tf_op jit(solution)/shard_map/ppermute | solution.py:24
  7.9 79.8 %collective-permute-start.18 = (bf16[1024,512]{1,0:T(8,128)(2,1)S(1)}, bf16[1024,512]{1,0:T(8,128)(2,1)S(1)}, u32[]{:S(2)}, u32[]{:S(2)}) collective-permute-start(bf16[1024,512]{1,0:T(8,128)(2,1)S(1)} %pad_maximum_fusion.refs_4_.refs_32_), channel_id=1, source_target_pairs={{0,1},{1,0},{2,3},{3,2},{4,5},{5,4},{6,7},{7,6},{8,9},{9,8},{10,11... | collective-permute-start | bytes 3145736 | tf_op jit(solution)/shard_map/ppermute | solution.py:24
  31.3 57.7 %collective-permute-start.21 = (bf16[1024,512]{1,0:T(8,128)(2,1)S(1)}, bf16[1024,512]{1,0:T(8,128)(2,1)S(1)}, u32[]{:S(2)}, u32[]{:S(2)}) collective-permute-start(bf16[1024,512]{1,0:T(8,128)(2,1)S(1)} %collective-permute-done.17.refs_7_.refs_35_), channel_id=1, source_target_pairs={{0,1},{1,0},{2,3},{3,2},{4,5},{5,4},{6,7},{7,6},{8,9},{9,8},{10,11... | collective-permute-start | bytes 3145736 | tf_op jit(solution)/shard_map/ppermute | solution.py:24
  52.9 36.6 %collective-permute-start.20 = (bf16[1024,512]{1,0:T(8,128)(2,1)S(1)}, bf16[1024,512]{1,0:T(8,128)(2,1)S(1)}, u32[]{:S(2)}, u32[]{:S(2)}) collective-permute-start(bf16[1024,512]{1,0:T(8,128)(2,1)S(1)} %collective-permute-done.16.refs_6_.refs_34_), channel_id=1, source_target_pairs={{0,1},{1,0},{2,3},{3,2},{4,5},{5,4},{6,7},{7,6},{8,9},{9,8},{10,11... | collective-permute-start | bytes 3145736 | tf_op jit(solution)/shard_map/ppermute | solution.py:24
  53.2 38.1 %collective-permute-start.19 = (bf16[1024,512]{1,0:T(8,128)(2,1)S(1)}, bf16[1024,512]{1,0:T(8,128)(2,1)}, u32[]{:S(2)}, u32[]{:S(2)}) collective-permute-start(bf16[1024,512]{1,0:T(8,128)(2,1)S(1)} %collective-permute-done.15.refs_5_.refs_33_), channel_id=1, source_target_pairs={{0,1},{1,0},{2,3},{3,2},{4,5},{5,4},{6,7},{7,6},{8,9},{9,8},{10,11... | collective-permute-start | bytes 3145736 | tf_op jit(solution)/shard_map/ppermute | solution.py:24
  62.0 14.2 %collective-permute-start.1 = (bf16[2,32,2048]{2,1,0:T(8,128)(2,1)S(1)}, bf16[2,32,2048]{2,1,0:T(8,128)(2,1)S(1)}, u32[]{:S(2)}, u32[]{:S(2)}) collective-permute-start(bf16[2,32,2048]{2,1,0:T(8,128)(2,1)S(1)} %bitcast.51), channel_id=1, source_target_pairs={{0,4},{1,5},{2,6},{3,7},{4,0},{5,1},{6,2},{7,3},{8,12},{9,13},{10,... | collective-permute-start | bytes 786440 | tf_op jit(solution)/shard_map/ppermute | solution.py:24
  76.2 9.9 %collective-permute-start.2 = (bf16[2,32,2048]{2,1,0:T(8,128)(2,1)S(1)}, bf16[2,32,2048]{2,1,0:T(8,128)(2,1)S(1)}, u32[]{:S(2)}, u32[]{:S(2)}) collective-permute-start(bf16[2,32,2048]{2,1,0:T(8,128)(2,1)S(1)} %bitcast.50), channel_id=1, source_target_pairs={{0,6},{1,7},{2,4},{3,5},{4,2},{5,3},{6,0},{7,1},{8,14},{9,15},{10,... | collective-permute-start | bytes 786440 | tf_op jit(solution)/shard_map/ppermute | solution.py:24
  86.0 16.9 %collective-permute-start.11 = (bf16[2,32,2048]{2,1,0:T(8,128)(2,1)S(1)}, bf16[2,32,2048]{2,1,0:T(8,128)(2,1)}, u32[]{:S(2)}, u32[]{:S(2)}) collective-permute-start(bf16[2,32,2048]{2,1,0:T(8,128)(2,1)S(1)} %bitcast.33), channel_id=1, source_target_pairs={{0,24},{8,16},{16,8},{24,0},{1,25},{9,17},{17,9},{25,1},{2,26},{10... | collective-permute-start | bytes 786440 | tf_op jit(solution)/shard_map/ppermute | solution.py:24
  87.7 17.6 %collective-permute-start.7 = (bf16[2,32,2048]{2,1,0:T(8,128)(2,1)S(1)}, bf16[2,32,2048]{2,1,0:T(8,128)(2,1)}, u32[]{:S(2)}, u32[]{:S(2)}) collective-permute-start(bf16[2,32,2048]{2,1,0:T(8,128)(2,1)S(1)} %bitcast.34), channel_id=1, source_target_pairs={{0,16},{8,24},{16,0},{24,8},{1,17},{9,25},{17,1},{25,9},{2,18},{10... | collective-permute-start | bytes 786440 | tf_op jit(solution)/shard_map/ppermute | solution.py:24
  89.0 17.3 %collective-permute-start.3 = (bf16[2,32,2048]{2,1,0:T(8,128)(2,1)S(1)}, bf16[2,32,2048]{2,1,0:T(8,128)(2,1)}, u32[]{:S(2)}, u32[]{:S(2)}) collective-permute-start(bf16[2,32,2048]{2,1,0:T(8,128)(2,1)S(1)} %bitcast.35), channel_id=1, source_target_pairs={{0,8},{8,0},{16,24},{24,16},{1,9},{9,1},{17,25},{25,17},{2,10},{10... | collective-permute-start | bytes 786440 | tf_op jit(solution)/shard_map/ppermute | solution.py:24
  89.5 18.2 %collective-permute-start.12 = (bf16[2,32,2048]{2,1,0:T(8,128)(2,1)S(1)}, bf16[2,32,2048]{2,1,0:T(8,128)(2,1)}, u32[]{:S(2)}, u32[]{:S(2)}) collective-permute-start(bf16[2,32,2048]{2,1,0:T(8,128)(2,1)S(1)} %collective-permute-done.refs_1_), channel_id=1, source_target_pairs={{0,24},{8,16},{16,8},{24,0},{1,25},{9,17},{17,9},{25,1},{2,26},{10... | collective-permute-start | bytes 786440 | tf_op jit(solution)/shard_map/ppermute | solution.py:24
  99.4 10.9 %collective-permute-start.27 = (f32[4,128,128]{2,1,0:T(8,128)}, f32[4,128,128]{2,1,0:T(8,128)S(1)}, u32[]{:S(2)}, u32[]{:S(2)}) collective-permute-start(f32[4,128,128]{2,1,0:T(8,128)} %get-tuple-element.42), channel_id=1, source_target_pairs={{0,6},{1,7},{2,4},{3,5},{4,2},{5,3},{6,0},{7,1},{8,14},{9,15},{10,... | collective-permute-start | bytes 786440 | tf_op jit(solution)/shard_map/ppermute | solution.py:24
  103.0 21.5 %collective-permute-start.26 = (f32[4,128,128]{2,1,0:T(8,128)}, f32[4,128,128]{2,1,0:T(8,128)S(1)}, u32[]{:S(2)}, u32[]{:S(2)}) collective-permute-start(f32[4,128,128]{2,1,0:T(8,128)} %get-tuple-element.42), channel_id=1, source_target_pairs={{0,4},{1,5},{2,6},{3,7},{4,0},{5,1},{6,2},{7,3},{8,12},{9,13},{10,... | collective-permute-start | bytes 786440 | tf_op jit(solution)/shard_map/ppermute | solution.py:24
  105.3 20.0 %collective-permute-start.25 = (f32[4,128,128]{2,1,0:T(8,128)}, f32[4,128,128]{2,1,0:T(8,128)S(1)}, u32[]{:S(2)}, u32[]{:S(2)}) collective-permute-start(f32[4,128,128]{2,1,0:T(8,128)} %get-tuple-element.42), channel_id=1, source_target_pairs={{0,2},{1,3},{2,0},{3,1},{4,6},{5,7},{6,4},{7,5},{8,10},{9,11},{10,... | collective-permute-start | bytes 786440 | tf_op jit(solution)/shard_map/ppermute | solution.py:24
  106.3 23.3 %collective-permute-start.8 = (bf16[2,32,2048]{2,1,0:T(8,128)(2,1)}, bf16[2,32,2048]{2,1,0:T(8,128)(2,1)S(1)}, u32[]{:S(2)}, u32[]{:S(2)}) collective-permute-start(bf16[2,32,2048]{2,1,0:T(8,128)(2,1)} %copy-done.8), channel_id=1, source_target_pairs={{0,16},{8,24},{16,0},{24,8},{1,17},{9,25},{17,1},{25,9},{2,18},{10... | collective-permute-start | bytes 786440 | tf_op jit(solution)/shard_map/ppermute | solution.py:24
  107.8 23.1 %collective-permute-start.4 = (bf16[2,32,2048]{2,1,0:T(8,128)(2,1)}, bf16[2,32,2048]{2,1,0:T(8,128)(2,1)S(1)}, u32[]{:S(2)}, u32[]{:S(2)}) collective-permute-start(bf16[2,32,2048]{2,1,0:T(8,128)(2,1)} %copy-done.8), channel_id=1, source_target_pairs={{0,8},{8,0},{16,24},{24,16},{1,9},{9,1},{17,25},{25,17},{2,10},{10... | collective-permute-start | bytes 786440 | tf_op jit(solution)/shard_map/ppermute | solution.py:24
  110.4 22.0 %collective-permute-start.13 = (bf16[2,32,2048]{2,1,0:T(8,128)(2,1)}, bf16[2,32,2048]{2,1,0:T(8,128)(2,1)S(1)}, u32[]{:S(2)}, u32[]{:S(2)}) collective-permute-start(bf16[2,32,2048]{2,1,0:T(8,128)(2,1)} %copy-done.9), channel_id=1, source_target_pairs={{0,24},{8,16},{16,8},{24,0},{1,25},{9,17},{17,9},{25,1},{2,26},{10... | collective-permute-start | bytes 786440 | tf_op jit(solution)/shard_map/ppermute | solution.py:24
  124.5 16.5 %collective-permute-start.22 = (f32[4,32,640]{2,1,0:T(8,128)}, f32[4,32,640]{2,1,0:T(8,128)S(1)}, u32[]{:S(2)}, u32[]{:S(2)}) collective-permute-start(f32[4,32,640]{2,1,0:T(8,128)} %get-tuple-element.39), channel_id=1, source_target_pairs={{0,2},{1,3},{2,0},{3,1},{4,6},{5,7},{6,4},{7,5},{8,10},{9,11},{10,... | collective-permute-start | bytes 983048 | tf_op jit(solution)/shard_map/ppermute | solution.py:24
  125.3 18.3 %collective-permute-start.23 = (f32[4,32,640]{2,1,0:T(8,128)}, f32[4,32,640]{2,1,0:T(8,128)S(1)}, u32[]{:S(2)}, u32[]{:S(2)}) collective-permute-start(f32[4,32,640]{2,1,0:T(8,128)} %get-tuple-element.40), channel_id=1, source_target_pairs={{0,4},{1,5},{2,6},{3,7},{4,0},{5,1},{6,2},{7,3},{8,12},{9,13},{10,... | collective-permute-start | bytes 983048 | tf_op jit(solution)/shard_map/ppermute | solution.py:24
  129.6 14.0 %collective-permute-start.33 = (f32[4,128,128]{2,1,0:T(8,128)S(1)}, f32[4,128,128]{2,1,0:T(8,128)S(1)}, u32[]{:S(2)}, u32[]{:S(2)}) collective-permute-start(f32[4,128,128]{2,1,0:T(8,128)S(1)} %add_add_fusion.refs_7_), channel_id=1, source_target_pairs={{0,24},{8,16},{16,8},{24,0},{1,25},{9,17},{17,9},{25,1},{2,26},{10... | collective-permute-start | bytes 786440 | tf_op jit(solution)/shard_map/ppermute | solution.py:24
  130.9 13.3 %collective-permute-start.31 = (f32[4,128,128]{2,1,0:T(8,128)S(1)}, f32[4,128,128]{2,1,0:T(8,128)S(1)}, u32[]{:S(2)}, u32[]{:S(2)}) collective-permute-start(f32[4,128,128]{2,1,0:T(8,128)S(1)} %add_add_fusion.refs_7_), channel_id=1, source_target_pairs={{0,16},{8,24},{16,0},{24,8},{1,17},{9,25},{17,1},{25,9},{2,18},{10... | collective-permute-start | bytes 786440 | tf_op jit(solution)/shard_map/ppermute | solution.py:24
  132.4 11.9 %collective-permute-start.29 = (f32[4,128,128]{2,1,0:T(8,128)S(1)}, f32[4,128,128]{2,1,0:T(8,128)S(1)}, u32[]{:S(2)}, u32[]{:S(2)}) collective-permute-start(f32[4,128,128]{2,1,0:T(8,128)S(1)} %add_add_fusion.refs_7_), channel_id=1, source_target_pairs={{0,8},{8,0},{16,24},{24,16},{1,9},{9,1},{17,25},{25,17},{2,10},{10... | collective-permute-start | bytes 786440 | tf_op jit(solution)/shard_map/ppermute | solution.py:24
  141.0 10.8 %collective-permute-start.24 = (f32[4,32,640]{2,1,0:T(8,128)}, f32[4,32,640]{2,1,0:T(8,128)S(1)}, u32[]{:S(2)}, u32[]{:S(2)}) collective-permute-start(f32[4,32,640]{2,1,0:T(8,128)} %get-tuple-element.41), channel_id=1, source_target_pairs={{0,6},{1,7},{2,4},{3,5},{4,2},{5,3},{6,0},{7,1},{8,14},{9,15},{10,... | collective-permute-start | bytes 983048 | tf_op jit(solution)/shard_map/ppermute | solution.py:24
  143.7 9.4 %collective-permute-start.28 = (f32[4,128,128]{2,1,0:T(8,128)S(1)}, f32[4,128,128]{2,1,0:T(8,128)S(1)}, u32[]{:S(2)}, u32[]{:S(2)}) collective-permute-start(f32[4,128,128]{2,1,0:T(8,128)S(1)} %add_add_fusion.refs_7_), channel_id=1, source_target_pairs={{0,1},{1,0},{2,3},{3,2},{4,5},{5,4},{6,7},{7,6},{8,9},{9,8},{10,11... | collective-permute-start | bytes 786440 | tf_op jit(solution)/shard_map/ppermute | solution.py:24
  143.7 9.9 %collective-permute-start.34 = (f32[4,128,128]{2,1,0:T(8,128)S(1)}, f32[4,128,128]{2,1,0:T(8,128)S(1)}, u32[]{:S(2)}, u32[]{:S(2)}) collective-permute-start(f32[4,128,128]{2,1,0:T(8,128)S(1)} %collective-permute-done.33.refs_13_), channel_id=1, source_target_pairs={{0,1},{1,0},{2,3},{3,2},{4,5},{5,4},{6,7},{7,6},{8,9},{9,8},{10,11... | collective-permute-start | bytes 786440 | tf_op jit(solution)/shard_map/ppermute | solution.py:24
  144.2 11.2 %collective-permute-start.32 = (f32[4,128,128]{2,1,0:T(8,128)S(1)}, f32[4,128,128]{2,1,0:T(8,128)S(1)}, u32[]{:S(2)}, u32[]{:S(2)}) collective-permute-start(f32[4,128,128]{2,1,0:T(8,128)S(1)} %collective-permute-done.31.refs_11_), channel_id=1, source_target_pairs={{0,1},{1,0},{2,3},{3,2},{4,5},{5,4},{6,7},{7,6},{8,9},{9,8},{10,11... | collective-permute-start | bytes 786440 | tf_op jit(solution)/shard_map/ppermute | solution.py:24
  144.3 12.4 %collective-permute-start.30 = (f32[4,128,128]{2,1,0:T(8,128)S(1)}, f32[4,128,128]{2,1,0:T(8,128)S(1)}, u32[]{:S(2)}, u32[]{:S(2)}) collective-permute-start(f32[4,128,128]{2,1,0:T(8,128)S(1)} %collective-permute-done.29.refs_9_), channel_id=1, source_target_pairs={{0,1},{1,0},{2,3},{3,2},{4,5},{5,4},{6,7},{7,6},{8,9},{9,8},{10,11... | collective-permute-start | bytes 786440 | tf_op jit(solution)/shard_map/ppermute | solution.py:24
  151.8 17.5 %collective-permute-start.9 = (bf16[2,32,2048]{2,1,0:T(8,128)(2,1)}, bf16[2,32,2048]{2,1,0:T(8,128)(2,1)S(1)}, u32[]{:S(2)}, u32[]{:S(2)}) collective-permute-start(bf16[2,32,2048]{2,1,0:T(8,128)(2,1)} %copy-done.9), channel_id=1, source_target_pairs={{0,16},{8,24},{16,0},{24,8},{1,17},{9,25},{17,1},{25,9},{2,18},{10... | collective-permute-start | bytes 786440 | tf_op jit(solution)/shard_map/ppermute | solution.py:24
  153.0 18.0 %collective-permute-start.5 = (bf16[2,32,2048]{2,1,0:T(8,128)(2,1)}, bf16[2,32,2048]{2,1,0:T(8,128)(2,1)S(1)}, u32[]{:S(2)}, u32[]{:S(2)}) collective-permute-start(bf16[2,32,2048]{2,1,0:T(8,128)(2,1)} %copy-done.9), channel_id=1, source_target_pairs={{0,8},{8,0},{16,24},{24,16},{1,9},{9,1},{17,25},{25,17},{2,10},{10... | collective-permute-start | bytes 786440 | tf_op jit(solution)/shard_map/ppermute | solution.py:24
  153.5 19.7 %collective-permute-start.14 = (bf16[2,32,2048]{2,1,0:T(8,128)(2,1)}, bf16[2,32,2048]{2,1,0:T(8,128)(2,1)S(1)}, u32[]{:S(2)}, u32[]{:S(2)}) collective-permute-start(bf16[2,32,2048]{2,1,0:T(8,128)(2,1)} %copy-done.10), channel_id=1, source_target_pairs={{0,24},{8,16},{16,8},{24,0},{1,25},{9,17},{17,9},{25,1},{2,26},{10... | collective-permute-start | bytes 786440 | tf_op jit(solution)/shard_map/ppermute | solution.py:24
  155.3 19.2 %collective-permute-start.10 = (bf16[2,32,2048]{2,1,0:T(8,128)(2,1)}, bf16[2,32,2048]{2,1,0:T(8,128)(2,1)S(1)}, u32[]{:S(2)}, u32[]{:S(2)}) collective-permute-start(bf16[2,32,2048]{2,1,0:T(8,128)(2,1)} %copy-done.10), channel_id=1, source_target_pairs={{0,16},{8,24},{16,0},{24,8},{1,17},{9,25},{17,1},{25,9},{2,18},{10... | collective-permute-start | bytes 786440 | tf_op jit(solution)/shard_map/ppermute | solution.py:24
  156.7 18.5 %collective-permute-start.6 = (bf16[2,32,2048]{2,1,0:T(8,128)(2,1)}, bf16[2,32,2048]{2,1,0:T(8,128)(2,1)S(1)}, u32[]{:S(2)}, u32[]{:S(2)}) collective-permute-start(bf16[2,32,2048]{2,1,0:T(8,128)(2,1)} %copy-done.10), channel_id=1, source_target_pairs={{0,8},{8,0},{16,24},{24,16},{1,9},{9,1},{17,25},{25,17},{2,10},{10... | collective-permute-start | bytes 786440 | tf_op jit(solution)/shard_map/ppermute | solution.py:24
  169.3 11.4 %collective-permute-start.46 = (bf16[32,2176]{1,0:T(8,128)(2,1)}, bf16[32,2176]{1,0:T(8,128)(2,1)S(1)}, u32[]{:S(2)}, u32[]{:S(2)}) collective-permute-start(bf16[32,2176]{1,0:T(8,128)(2,1)} %chain.1.refs_16_), channel_id=1, source_target_pairs={{0,24},{8,16},{16,8},{24,0},{1,25},{9,17},{17,9},{25,1},{2,26},{10... | collective-permute-start | bytes 417800 | tf_op jit(solution)/shard_map/ppermute | solution.py:24
  171.0 12.2 %collective-permute-start.37 = (bf16[32,2176]{1,0:T(8,128)(2,1)}, bf16[32,2176]{1,0:T(8,128)(2,1)S(1)}, u32[]{:S(2)}, u32[]{:S(2)}) collective-permute-start(bf16[32,2176]{1,0:T(8,128)(2,1)} %chain.1.refs_16_), channel_id=1, source_target_pairs={{0,6},{1,7},{2,4},{3,5},{4,2},{5,3},{6,0},{7,1},{8,14},{9,15},{10,... | collective-permute-start | bytes 417800 | tf_op jit(solution)/shard_map/ppermute | solution.py:24
  173.3 11.3 %collective-permute-start.42 = (bf16[32,2176]{1,0:T(8,128)(2,1)}, bf16[32,2176]{1,0:T(8,128)(2,1)S(1)}, u32[]{:S(2)}, u32[]{:S(2)}) collective-permute-start(bf16[32,2176]{1,0:T(8,128)(2,1)} %chain.1.refs_16_), channel_id=1, source_target_pairs={{0,16},{8,24},{16,0},{24,8},{1,17},{9,25},{17,1},{25,9},{2,18},{10... | collective-permute-start | bytes 417800 | tf_op jit(solution)/shard_map/ppermute | solution.py:24
  174.5 11.4 %collective-permute-start.38 = (bf16[32,2176]{1,0:T(8,128)(2,1)}, bf16[32,2176]{1,0:T(8,128)(2,1)S(1)}, u32[]{:S(2)}, u32[]{:S(2)}) collective-permute-start(bf16[32,2176]{1,0:T(8,128)(2,1)} %chain.1.refs_16_), channel_id=1, source_target_pairs={{0,8},{8,0},{16,24},{24,16},{1,9},{9,1},{17,25},{25,17},{2,10},{10... | collective-permute-start | bytes 417800 | tf_op jit(solution)/shard_map/ppermute | solution.py:24
  175.2 11.9 %collective-permute-start.36 = (bf16[32,2176]{1,0:T(8,128)(2,1)}, bf16[32,2176]{1,0:T(8,128)(2,1)S(1)}, u32[]{:S(2)}, u32[]{:S(2)}) collective-permute-start(bf16[32,2176]{1,0:T(8,128)(2,1)} %chain.1.refs_16_), channel_id=1, source_target_pairs={{0,4},{1,5},{2,6},{3,7},{4,0},{5,1},{6,2},{7,3},{8,12},{9,13},{10,... | collective-permute-start | bytes 417800 | tf_op jit(solution)/shard_map/ppermute | solution.py:24
  187.1 9.8 %collective-permute-start.48 = (bf16[32,2176]{1,0:T(8,128)(2,1)S(1)}, bf16[32,2176]{1,0:T(8,128)(2,1)S(1)}, u32[]{:S(2)}, u32[]{:S(2)}) collective-permute-start(bf16[32,2176]{1,0:T(8,128)(2,1)S(1)} %collective-permute-done.36.refs_18_), channel_id=1, source_target_pairs={{0,24},{8,16},{16,8},{24,0},{1,25},{9,17},{17,9},{25,1},{2,26},{10... | collective-permute-start | bytes 417800 | tf_op jit(solution)/shard_map/ppermute | solution.py:24
  188.3 9.9 %collective-permute-start.44 = (bf16[32,2176]{1,0:T(8,128)(2,1)S(1)}, bf16[32,2176]{1,0:T(8,128)(2,1)S(1)}, u32[]{:S(2)}, u32[]{:S(2)}) collective-permute-start(bf16[32,2176]{1,0:T(8,128)(2,1)S(1)} %collective-permute-done.36.refs_18_), channel_id=1, source_target_pairs={{0,16},{8,24},{16,0},{24,8},{1,17},{9,25},{17,1},{25,9},{2,18},{10... | collective-permute-start | bytes 417800 | tf_op jit(solution)/shard_map/ppermute | solution.py:24
  213.9 49.9 %collective-permute-start.56 = (f32[1024,512]{1,0:T(8,128)}, f32[1024,512]{1,0:T(8,128)S(1)}, u32[]{:S(2)}, u32[]{:S(2)}) collective-permute-start(f32[1024,512]{1,0:T(8,128)} %get-tuple-element.52), channel_id=1, source_target_pairs={{0,1},{1,0},{2,3},{3,2},{4,5},{5,4},{6,7},{7,6},{8,9},{9,8},{10,11... | collective-permute-start | bytes 6291464 | tf_op jit(solution)/shard_map/ppermute | solution.py:24
  213.9 16.8 %collective-permute-start.51 = (bf16[128,1024]{1,0:T(8,128)(2,1)}, bf16[128,1024]{1,0:T(8,128)(2,1)S(1)}, u32[]{:S(2)}, u32[]{:S(2)}) collective-permute-start(bf16[128,1024]{1,0:T(8,128)(2,1)} %bitcast.46), channel_id=1, source_target_pairs={{0,2},{1,3},{2,0},{3,1},{4,6},{5,7},{6,4},{7,5},{8,10},{9,11},{10,... | collective-permute-start | bytes 786440 | tf_op jit(solution)/shard_map/ppermute | solution.py:24
  216.2 21.6 %collective-permute-start.53 = (bf16[128,1024]{1,0:T(8,128)(2,1)}, bf16[128,1024]{1,0:T(8,128)(2,1)S(1)}, u32[]{:S(2)}, u32[]{:S(2)}) collective-permute-start(bf16[128,1024]{1,0:T(8,128)(2,1)} %bitcast.45), channel_id=1, source_target_pairs={{0,4},{1,5},{2,6},{3,7},{4,0},{5,1},{6,2},{7,3},{8,12},{9,13},{10,... | collective-permute-start | bytes 786440 | tf_op jit(solution)/shard_map/ppermute | solution.py:24
  216.6 22.9 %collective-permute-start.55 = (bf16[128,1024]{1,0:T(8,128)(2,1)}, bf16[128,1024]{1,0:T(8,128)(2,1)S(1)}, u32[]{:S(2)}, u32[]{:S(2)}) collective-permute-start(bf16[128,1024]{1,0:T(8,128)(2,1)} %bitcast.44), channel_id=1, source_target_pairs={{0,6},{1,7},{2,4},{3,5},{4,2},{5,3},{6,0},{7,1},{8,14},{9,15},{10,... | collective-permute-start | bytes 786440 | tf_op jit(solution)/shard_map/ppermute | solution.py:24
  229.6 12.9 %collective-permute-start.50 = (bf16[128,1024]{1,0:T(8,128)(2,1)}, bf16[128,1024]{1,0:T(8,128)(2,1)S(1)}, u32[]{:S(2)}, u32[]{:S(2)}) collective-permute-start(bf16[128,1024]{1,0:T(8,128)(2,1)} %bitcast.49), channel_id=1, source_target_pairs={{0,2},{1,3},{2,0},{3,1},{4,6},{5,7},{6,4},{7,5},{8,10},{9,11},{10,... | collective-permute-start | bytes 786440 | tf_op jit(solution)/shard_map/ppermute | solution.py:24
  230.7 29.5 %collective-permute-start.52 = (bf16[128,1024]{1,0:T(8,128)(2,1)}, bf16[128,1024]{1,0:T(8,128)(2,1)S(1)}, u32[]{:S(2)}, u32[]{:S(2)}) collective-permute-start(bf16[128,1024]{1,0:T(8,128)(2,1)} %bitcast.48), channel_id=1, source_target_pairs={{0,4},{1,5},{2,6},{3,7},{4,0},{5,1},{6,2},{7,3},{8,12},{9,13},{10,... | collective-permute-start | bytes 786440 | tf_op jit(solution)/shard_map/ppermute | solution.py:24
  237.7 22.5 %collective-permute-start.54 = (bf16[128,1024]{1,0:T(8,128)(2,1)}, bf16[128,1024]{1,0:T(8,128)(2,1)}, u32[]{:S(2)}, u32[]{:S(2)}) collective-permute-start(bf16[128,1024]{1,0:T(8,128)(2,1)} %bitcast.47), channel_id=1, source_target_pairs={{0,6},{1,7},{2,4},{3,5},{4,2},{5,3},{6,0},{7,1},{8,14},{9,15},{10,... | collective-permute-start | bytes 786440 | tf_op jit(solution)/shard_map/ppermute | solution.py:24
  (66 other events, 1342.0 us)

commit v2 on v1

v2 whole, which is shorter than its diff:
```python
import functools

import jax
import jax.numpy as jnp
from jax import lax
from jax.experimental import pallas as pl
from jax.experimental.pallas import tpu as pltpu
from jax.sharding import PartitionSpec as P

BF = jnp.bfloat16
F32 = jnp.float32
NN = (((1,), (0,)), ((), ()))
NT = (((1,), (1,)), ((), ()))
TN = (((0,), (0,)), ((), ()))
VMEM_BYTES = 56 * 2**20
CORES = 2


def dot(a, b, dims=NN):
    return lax.dot_general(a, b, dims, preferred_element_type=F32)


def hop(block, axis, step):
    return lax.ppermute(block, axis, [(i, i ^ step) for i in range(lax.axis_size(axis))])


def place():
    b = lax.axis_index("dp")
    return lax.axis_index("pipe"), b // CORES, b % CORES


def cost(flops, moved):
    return pl.CostEstimate(flops=int(flops), bytes_accessed=int(moved), transcendentals=0)


def vmem(count):
    return [pl.BlockSpec(memory_space=pltpu.VMEM)] * count


def anywhere(count):
    return [pl.BlockSpec(memory_space=pl.ANY)] * count


def across(block, chips):
    groups = [[z * CORES + c for z in range(chips)] for c in range(CORES)]
    return lax.all_to_all(block, "dp", 0, 0, axis_index_groups=groups, tiled=True)


def after(values, *others):
    return lax.optimization_barrier((values, others))[0]


def sides(block):
    return hop(block, "pipe", 1), hop(block, "pipe", 2)


def corner(one, two):
    cut = one.shape[0] // 2
    return hop(one[:cut], "pipe", 2), hop(two[cut:], "pipe", 1)


def fan(block):
    sections = lax.axis_size("pipe")
    if sections != 4:
        return [block] + [hop(block, "pipe", j) for j in range(1, sections)]
    one, two = sides(block)
    return [block, one, two, jnp.concatenate(corner(one, two), axis=0)]


def pack(features, cots, chips):
    _, total, seq, width = features.shape
    group = total // lax.axis_size("pipe")
    eighth = width // (chips * CORES)

    def kernel(x_ref, g_ref, out, squares, sems):
        p, _, c = place()
        copies = []
        for z in range(chips):
            for h in range(CORES):
                start = pl.multiple_of((z * CORES + (c ^ h)) * eighth, eighth)
                for a, ref in enumerate((x_ref, g_ref)):
                    copies.append(
                        pltpu.make_async_copy(
                            ref.at[0, pl.ds(p * group, group), :, pl.ds(start, eighth)],
                            out.at[z, a, :, :, pl.ds(h * eighth, eighth)],
                            sems.at[len(copies)],
                        )
                    )
        for copy in copies:
            copy.start()
        for copy in copies:
            copy.wait()
        for i in range(group):
            total = jnp.zeros((seq, 1), F32)
            for z in range(chips):
                block = out[z, 0, i].astype(F32)
                total = total + jnp.sum(block * block, axis=-1, keepdims=True)
            squares[i * seq : (i + 1) * seq, :] = total

    out, squares = pl.pallas_call(
        kernel,
        name="pack",
        out_shape=(
            jax.ShapeDtypeStruct((chips, 2, group, seq, CORES * eighth), BF),
            jax.ShapeDtypeStruct((group * seq, 1), F32),
        ),
        in_specs=anywhere(2),
        out_specs=tuple(vmem(2)),
        scratch_shapes=[pltpu.SemaphoreType.DMA((chips * CORES * 2,))],
        cost_estimate=cost(0, 8 * group * seq * width * 2),
    )(features, cots)
    return out.reshape(chips, 2, group * seq, CORES * eighth), squares


def unpack(pieces, chips, width):
    rows, eighth = pieces[0].shape

    def kernel(*refs):
        ins, out, sems = refs[:-2], refs[-2], refs[-1]
        _, z, c = place()
        copies = []
        for k in range(chips):
            for h in range(CORES):
                start = pl.multiple_of(((z ^ k) * CORES + (c ^ h)) * eighth, eighth)
                copies.append(
                    pltpu.make_async_copy(
                        ins[k * CORES + h], out.at[:, pl.ds(start, eighth)], sems.at[len(copies)]
                    )
                )
        for copy in copies:
            copy.start()
        for copy in copies:
            copy.wait()

    return pl.pallas_call(
        kernel,
        name="unpack",
        out_shape=jax.ShapeDtypeStruct((rows, width), BF),
        in_specs=vmem(len(pieces)),
        out_specs=pl.BlockSpec(memory_space=pl.ANY),
        scratch_shapes=[pltpu.SemaphoreType.DMA((len(pieces),))],
        cost_estimate=cost(0, 4 * rows * width * 2),
    )(*pieces)


def project(tokens, own, other, wanted, head, apart):
    chips, _, rows, _ = tokens.shape
    given, first = len(own), len(own) - len(wanted)
    half = own[0].shape[0]
    tall = head // rows
    blocks = len(wanted) * (5 + tall)

    def kernel(*refs):
        tok = refs[0]
        ws = refs[1 : 1 + given]
        vs = refs[1 + given : 1 + 2 * given]
        outs = refs[1 + 2 * given :]
        p, z, c = place()
        order = [z ^ k if apart else k for k in range(chips)]
        outs = outs if apart else [outs[0].at[k] for k in range(chips)]
        h = jnp.concatenate([tok[k, 0] for k in order], axis=0)
        g = jnp.concatenate([tok[k, 1] for k in order], axis=0)
        for n in range(len(wanted)):
            w, v = ws[first + n], vs[first + n]
            a = dot(h[:, :half], w[...]) + dot(h[:, half:], v[...])
            b = dot(g[:, :half], w[:, 3 * head :]) + dot(g[:, half:], v[:, 3 * head :])
            for k in range(chips):
                at = slice(k * rows, (k + 1) * rows)
                for i in range(4):
                    part = a[at, i * head : (i + 1) * head]
                    outs[k][n * 5 + i] = part.astype(BF)
                outs[k][n * 5 + 4] = b[at].astype(BF)

        def put(n, low, high, block):
            cols = slice(block * head, (block + 1) * head)
            gram = sum(dot(w[low][:, 3 * head :], w[high][:, cols], TN) for w in (ws, vs))
            for k in range(chips):
                for i in range(tall):
                    part = gram[i * rows : (i + 1) * rows]
                    outs[k][len(wanted) * 5 + n * tall + i] = part.astype(BF)

        for n, j in enumerate(wanted):
            if j == 0:
                put(n, 0, 0, 3)
                continue
            below = p < (p ^ j)
            at = first + n
            for core in range(CORES):
                pl.when(below & (c == core))(functools.partial(put, n, 0, at, core))
                pl.when(jnp.logical_not(below) & (c == core))(
                    functools.partial(put, n, at, 0, CORES + core)
                )

    return pl.pallas_call(
        kernel,
        name="project",
        out_shape=[jax.ShapeDtypeStruct((blocks, rows, head), BF)] * chips
        if apart
        else [jax.ShapeDtypeStruct((chips, blocks, rows, head), BF)],
        in_specs=vmem(1 + 2 * given),
        out_specs=vmem(chips if apart else 1),
        cost_estimate=cost(len(wanted) * 2**31, 4 * given * half * head * 8),
        compiler_params=pltpu.CompilerParams(vmem_limit_bytes=VMEM_BYTES),
    )(tokens, *own, *other)


def chain(rounds, squares, docs, head, width, seq):
    sections = sum(len(wanted) for wanted, _, _ in rounds)
    rows = squares.shape[0]
    lanes = sections * 4 * head
    flat = []
    for _, partials, grams in rounds:
        flat += [*partials] + [g for pair in grams for g in pair]

    def kernel(*refs):
        sq_ref, doc_ref = refs[:2]
        out, a_all, gram = refs[-3:]
        p, _, c = place()
        left = list(refs[2:-3])
        for wanted, partials, grams in rounds:
            a_refs = [left.pop(0) for _ in partials]
            for n, j in enumerate(wanted):
                for i in range(5):
                    at = n * 5 + i
                    if len(a_refs) > 1:
                        parts = [ref[at].astype(F32) for ref in a_refs]
                    else:
                        count = a_refs[0].shape[0]
                        parts = [a_refs[0][z, at].astype(F32) for z in range(count)]
                    a_all[p ^ j, i] = sum(parts)
            for i in range(sections):
                for h in range(CORES):
                    g_ref = left.pop(0)
                    for n, j in enumerate(wanted):
                        one, two = p ^ i, p ^ i ^ j
                        low, high = jnp.minimum(one, two), jnp.maximum(one, two)
                        if j > 0:
                            kind = jnp.where(one < two, 0, CORES) + (c ^ h)
                            gram[low, high, kind] = g_ref[n]
                        elif h == 0:
                            gram[low, high, 3] = g_ref[n]

        def times(m, low, high, kind, dims=NN):
            return dot(m, gram[low, high, kind], dims)

        places_r = lax.broadcasted_iota(jnp.int32, (rows, rows), 0)
        places_c = lax.broadcasted_iota(jnp.int32, (rows, rows), 1)
        across_docs = jnp.broadcast_to(doc_ref[p], (rows, rows))
        down = jnp.sum(jnp.where(places_r == places_c, across_docs, 0), axis=-1, keepdims=True)
        allowed = (places_r >= places_c) & (down == across_docs)
        if rows > seq:
            allowed = allowed & (places_r // seq == places_c // seq)
        scale = head ** (-0.5)

        x = [[a_all[s, i] for i in range(3)] for s in range(sections)]
        ho = [a_all[s, 3] for s in range(sections)]
        bo = [a_all[s, 4] for s in range(sections)]
        norm = sq_ref[...]
        saved = []
        for s in range(sections):
            inv = lax.rsqrt(jnp.maximum(norm, 0.0) / width + 1e-05)
            q, k, v = ((part * inv).astype(BF) for part in x[s])
            scores = jnp.where(allowed, dot(q, k, NT) * scale, -1e30)
            highest = jnp.max(scores, axis=-1, keepdims=True)
            exponent = jnp.where(allowed, jnp.exp(scores - highest), 0.0)
            soft = exponent / jnp.sum(exponent, axis=-1, keepdims=True)
            attend = soft.astype(BF)
            mixed = dot(attend, v).astype(BF)
            saved.append((inv, q, k, v, soft, attend, mixed, list(ho)))
            if s < sections - 1:
                before = ho[s]
                for t in range(s + 1, sections):
                    x[t] = [x[t][i] + times(mixed, s, t, i) for i in range(3)]
                for t in range(sections - 1):
                    if t >= s:
                        ho[t] = ho[t] + times(mixed, s, t, 3)
                    else:
                        ho[t] = ho[t] + times(mixed, t, s, 3, NT)
                wide = mixed.astype(F32)
                norm = norm + jnp.sum(wide * (before + ho[s]), axis=-1, keepdims=True)

        lane = lax.broadcasted_iota(jnp.int32, (rows, head), 1)
        scalars = jnp.zeros((rows, head), F32)
        for s in reversed(range(sections)):
            inv, q, k, v, soft, attend, mixed, along = saved[s]
            d_mixed = bo[s].astype(BF)
            d_attend = dot(d_mixed, v, NT).astype(BF).astype(F32)
            d_values = dot(attend, d_mixed, TN)
            inner = jnp.sum(soft * d_attend, axis=-1, keepdims=True)
            d_scores = (soft * (d_attend - inner) * scale).astype(BF)
            d_query = dot(d_scores, k)
            d_keys = dot(d_scores, q, TN)
            y = [(part * inv).astype(BF) for part in (d_query, d_keys, d_values)]
            inner = sum(y[i].astype(F32) * x[s][i] for i in range(3))
            coef = inv * inv * jnp.sum(inner, axis=-1, keepdims=True) / width
            for t in range(s):
                add = sum(times(y[i], t, s, i, NT) for i in range(3))
                bo[t] = bo[t] + add - coef * along[t]
            at = s * 4 * head
            for i in range(3):
                out[:, at + i * head : at + (i + 1) * head] = y[i]
            out[:, at + 3 * head : at + 4 * head] = mixed
            coarse = coef.astype(BF).astype(F32)
            scalars = jnp.where(lane == 2 * s, coarse, scalars)
            scalars = jnp.where(lane == 2 * s + 1, coef - coarse, scalars)
        out[:, lanes:] = scalars.astype(BF)

    return pl.pallas_call(
        kernel,
        name="chain",
        out_shape=jax.ShapeDtypeStruct((rows, lanes + head), BF),
        in_specs=vmem(2 + len(flat)),
        out_specs=pl.BlockSpec(memory_space=pltpu.VMEM),
        scratch_shapes=[
            pltpu.VMEM((sections, 5, rows, head), F32),
            pltpu.VMEM((sections, sections, 4, head, head), BF),
        ],
        cost_estimate=cost(sections * 2**31, 2**22),
        compiler_params=pltpu.CompilerParams(vmem_limit_bytes=VMEM_BYTES),
    )(squares, docs, *flat)


def rebuild(tokens, coefs, weights, column, head):
    groups, sections = len(tokens), len(weights)
    chips, rows, lanes = coefs[0].shape
    half = weights[0].shape[0]
    some = chips * rows
    count = groups * some
    block = min(256, half)

    def kernel(*refs):
        t_refs, c_refs = refs[:groups], refs[groups : 2 * groups]
        w_refs = refs[2 * groups : 2 * groups + sections]
        outs = refs[2 * groups + sections : 2 * groups + sections + chips]
        grads, left, own_m, edge, h_all, g_all = refs[2 * groups + sections + chips :]
        p, z, _ = place()
        out_w = slice(3 * head, 4 * head)
        qkv_w = slice(0, 3 * head)

        @pl.when(pl.program_id(0) == 0)
        def _():
            for i in range(groups):
                at = pl.ds(i * some, some)
                scalars = c_refs[i][:, :, lanes - head :].reshape(some, head).astype(F32)
                side = lax.broadcasted_iota(jnp.int32, scalars.shape, 1) // 2
                here = jnp.where(side == p, scalars, 0.0)
                here = jnp.sum(here, axis=-1, keepdims=True)
                edge[1, at, :] = jnp.broadcast_to(here, (some, head))
                for j in range(sections):
                    s = p ^ j
                    start = pl.multiple_of(s * 4 * head, 4 * head)
                    both = c_refs[i][:, :, pl.ds(start, 4 * head)].reshape(some, 4 * head)
                    left[j, at, :] = both
                    m = both[:, out_w]

                    def weigh(j=j, s=s, m=m):
                        after = jnp.where((side > s) & (side < sections), scalars, 0.0)
                        share = jnp.sum(after, axis=-1, keepdims=True)
                        left[j, at, out_w] = (-share * m.astype(F32)).astype(BF)
                        if j == 0:
                            edge[0, at, :] = jnp.broadcast_to(share, (some, head))

                    if j == 0:
                        own_m[at, :] = m
                        weigh()
                    else:
                        pl.when(s > p)(weigh)

        for i in range(groups):
            for k in range(chips):
                at = pl.ds(i * some + k * rows, rows)
                h_all[at, :] = t_refs[i][z ^ k, 0].astype(F32)
                g_all[at, :] = t_refs[i][z ^ k, 1].astype(F32)
        for j in range(1, sections):

            @pl.when((p ^ j) < p)
            def _():
                h_all[...] += dot(left[j, :, out_w], w_refs[j][:, out_w], NT)

            @pl.when((p ^ j) > p)
            def _():
                g_all[...] += dot(left[j], w_refs[j][...], NT)

        h = h_all[...]
        y = left[0, :, qkv_w]
        g = g_all[...] + dot(left[0, :, out_w], w_refs[0][:, out_w], NT)
        g = g - edge[0][:, :1] * h
        grads[:, qkv_w] = dot(h.astype(BF), y, TN)
        grads[:, out_w] = dot(g.astype(BF), own_m[...], TN)
        result = (g + dot(y, w_refs[0][:, qkv_w], NT) - edge[1][:, :1] * h).astype(BF)
        for i in range(groups):
            for k in range(chips):
                at = i * some + k * rows
                outs[k][p ^ i] = result[at : at + rows]

    outs = pl.pallas_call(
        kernel,
        name="rebuild",
        grid=(half // block,),
        out_shape=[jax.ShapeDtypeStruct((groups, rows, half), BF)] * chips
        + [jax.ShapeDtypeStruct((half, 4 * head), F32)],
        in_specs=[
            pl.BlockSpec((chips, 2, rows, block), lambda i: (0, 0, 0, i + column // block))
        ]
        * groups
        + vmem(groups)
        + [pl.BlockSpec((block, 4 * head), lambda i: (i, 0))] * sections,
        out_specs=[pl.BlockSpec((groups, rows, block), lambda i: (0, 0, i))] * chips
        + [pl.BlockSpec((block, 4 * head), lambda i: (i, 0))],
        scratch_shapes=[
            pltpu.VMEM((sections, count, 4 * head), BF),
            pltpu.VMEM((count, head), BF),
            pltpu.VMEM((2, count, head), F32),
            pltpu.VMEM((count, block), F32),
            pltpu.VMEM((count, block), F32),
        ],
        cost_estimate=cost(12 * count * half * head * 4 * sections, 2**24),
        compiler_params=pltpu.CompilerParams(vmem_limit_bytes=VMEM_BYTES),
    )(*tokens, *coefs, *weights)
    return outs[:chips], outs[chips]


def rebuild_wide(tokens, coefs, weights, column, head):
    sections = len(weights)
    chips, rows, lanes = coefs[0].shape
    half = weights[0].shape[0]
    p, z, _ = place()
    grads = jnp.zeros((half, 4 * head), F32)
    results = []
    for both, coef in zip(tokens, coefs):
        both, coef, grads = lax.optimization_barrier((both, coef, grads))
        both = jnp.take(both[..., column : column + half], jnp.arange(chips) ^ z, axis=0)
        coef = coef.reshape(chips * rows, lanes)
        scalars = coef[:, lanes - head :].astype(F32)
        side = lax.broadcasted_iota(jnp.int32, scalars.shape, 1) // 2

        def share(s, scalars=scalars, side=side):
            after = jnp.where((side > s) & (side < sections), scalars, 0.0)
            return jnp.sum(after, axis=-1, keepdims=True)

        h = both[:, 0].reshape(chips * rows, half).astype(F32)
        g = both[:, 1].reshape(chips * rows, half).astype(F32)
        for j in range(sections):
            s = p ^ j
            part = lax.dynamic_slice_in_dim(coef, s * 4 * head, 4 * head, axis=1)
            y, m = part[:, : 3 * head], part[:, 3 * head :]
            out_w = weights[j][:, 3 * head :]
            if j == 0:
                own = part
            h = h + dot(jnp.where(s < p, m, jnp.zeros_like(m)), out_w, NT)
            g = g + dot(jnp.where(s > p, y, jnp.zeros_like(y)), weights[j][:, : 3 * head], NT)
            late = jnp.where(s >= p, -share(s) * m.astype(F32), 0.0).astype(BF)
            g = g + dot(late, out_w, NT)
        g = g - share(p) * h
        y, m = own[:, : 3 * head], own[:, 3 * head :]
        here = jnp.sum(jnp.where(side == p, scalars, 0.0), axis=-1, keepdims=True)
        grads = grads + jnp.concatenate(
            [dot(h.astype(BF), y, TN), dot(g.astype(BF), m, TN)], axis=1
        )
        result = (g + dot(y, weights[0][:, : 3 * head], NT) - here * h).astype(BF)
        results.append(result.reshape(chips, rows, half))
    result = jnp.take(jnp.stack(results), jnp.arange(len(tokens)) ^ p, axis=0)
    return [result[:, k] for k in range(chips)], grads


def shards(inputs, segments, cotangent, w_query, w_key, w_value, w_out):
    sections = lax.axis_size("pipe")
    chips = lax.axis_size("dp") // CORES
    head = w_query.shape[2]
    _, batches, seq, width = inputs.shape
    short = -batches % sections
    if short:
        fill = ((0, 0), (0, short), (0, 0), (0, 0))
        inputs, cotangent = jnp.pad(inputs, fill), jnp.pad(cotangent, fill)
        segments = jnp.pad(segments, fill[:3])
    group = inputs.shape[1] // sections
    rows = group * seq

    pieces, squares = pack(inputs, cotangent, chips)
    mine = jnp.concatenate([w_query[0], w_key[0], w_value[0], w_out[0]], axis=1)
    pieces, mine = lax.optimization_barrier((pieces, mine))
    def summed(wanted, part):
        low = len(wanted) * 5
        if len(part) > 1:
            gram = sum(one[low:].astype(F32) for one in part)
        else:
            gram = jnp.sum(part[0][:, low:].astype(F32), axis=0)
        gram = gram.astype(BF).reshape(len(wanted), head, head)
        close = [gram] + [hop(gram, "pipe", j) for j in range(1, sections)]
        return wanted, part, [(g, hop(g, "dp", 1)) for g in close]

    tokens = across(pieces, chips)
    if sections == 4:
        near = hop(mine, "dp", 1)
        one, two = sides(mine)
        low, high = corner(one, two)
        near_one, near_two = (hop(w, "dp", 1) for w in after((one, two), tokens))
        ours, theirs = [mine, one, two], [near, near_one, near_two]
        early = project(tokens, ours, theirs, (0, 1, 2), head, False)
        low, high = after((low, high), *early)
        ours.append(jnp.concatenate([low, high], axis=0))
        theirs.append(hop(ours[3], "dp", 1))
        late = project(tokens, [mine, ours[3]], [near, theirs[3]], (3,), head, True)
        spread = sides(after(tokens, ours[3]))
        spread = [tokens, *spread, jnp.concatenate(corner(*after(spread, late[0])), axis=0)]
        early = summed((0, 1, 2), [across(early[0], chips)])
        late = [late[0]] + [hop(late[k], "dp", k * CORES) for k in range(1, chips)]
        rounds = [early, summed((3,), late)]
    else:
        ours = fan(mine)
        theirs = [hop(w, "dp", 1) for w in ours]
        spread = fan(tokens)
        wanted = tuple(range(sections))
        part = project(tokens, ours, theirs, wanted, head, False)
        rounds = [summed(wanted, [across(part[0], chips)])]

    docs = segments.reshape(sections, 1, rows)
    squares, *spread = lax.optimization_barrier((squares, *spread))
    coef = chain(rounds, squares, docs, head, width, seq)
    coef = jnp.stack([coef] + [hop(coef, "dp", k * CORES) for k in range(1, chips)])
    coefs = fan(coef)

    half = mine.shape[0]
    form = rebuild if sections * chips * rows <= 1024 else rebuild_wide
    far, far_grads = form(spread, coefs, theirs, half, head)
    close, grads = form(spread, coefs, ours, 0, head)
    grads = grads + hop(far_grads, "dp", 1)
    grads = [grads[None, :, i * head : (i + 1) * head] for i in range(4)]
    def sent(pieces):
        pieces = [part.reshape(sections * rows, half) for part in pieces]
        return [pieces[0]] + [hop(pieces[k], "dp", k * CORES) for k in range(1, chips)]

    far = sent(far)
    close = sent(after(close, far))
    out = [part for pair in zip(close, far) for part in pair]
    out, grads = lax.optimization_barrier((out, grads))
    stored = unpack(out, chips, width)[: batches * seq]
    return (stored.reshape(1, 1, batches, seq, width), *grads)


def solution(mesh):
    wide = P("dp", None, None, None)
    weight = P("pipe", "dp", None)
    return jax.shard_map(
        shards,
        mesh=mesh,
        in_specs=(wide, P("dp", None, None), wide, weight, weight, weight, weight),
        out_specs=(P("pipe", "dp", None, None, None), weight, weight, weight, weight),
        check_vma=False,
    )
```

time: 269 us -> 222 us (0.83)
  waiting for transfers between devices: 133 us -> 103 us
  starting transfers between devices: 79.1 us -> 54.2 us
  Pallas kernels: 43.5 us -> 47.5 us
  local copies, waits for them, and re-layouts: 5.63 us -> 9.56 us
    ppermute x57 -> x43, starting transfers between devices: 79.1 us -> 43.8 us  [hop(): lax.ppermute(block, axis, [(i, i ^ step) for i in range(lax.axis_size(axi...]
    ppermute x57 -> x43, waiting for transfers between devices: 133 us -> 103 us  [hop(): lax.ppermute(block, axis, [(i, i ^ step) for i in range(lax.axis_size(axi...]
    all_to_all x0 -> x2, starting transfers between devices: none -> 10.4 us  [across(): lax.all_to_all(block, 'dp', 0, 0, axis_index_groups=groups, tiled=True)]
    pallas_call x4 -> x5, Pallas kernels: 32.5 us -> 37.4 us  [the longest x2 24.3 us: rebuild(): pl.pallas_call(kernel, name='rebuild', grid=(half // block,), out_shape=[...]
    unnamed x114 -> x84, local copies, waits for them, and re-layouts: 1.64 us -> 5.04 us
  transfers between devices with their start and end apart: 57 -> 45, of which waited for: 21 -> 20; matrix products, arithmetic and copies ran while one was open for 2% -> 4% of each run, Pallas kernels for 11% -> 10%
where the time goes in v2:
time: 222 us; the launch traced here: 220 us
  waiting for transfers between devices  103 us (46%)
  starting transfers between devices  54.2 us (24%)
  Pallas kernels  47.5 us (21%)
  local copies, waits for them, and re-layouts  9.56 us (4%)
  other arithmetic  5.16 us (2%)
    ppermute x43, waiting for transfers between devices, hop(): lax.ppermute(block, axis, [(i, i ^ step) for i in range(lax.axis_size(axi...  103 us
    ppermute x43, starting transfers between devices, hop(): lax.ppermute(block, axis, [(i, i ^ step) for i in range(lax.axis_size(axi...  43.8 us
    pallas_call x2, Pallas kernels, rebuild(): pl.pallas_call(kernel, name='rebuild', grid=(half // block,), out_shape=[...  24.3 us
    pallas_call x2, Pallas kernels, project(): pl.pallas_call(kernel, name='project', out_shape=[jax.ShapeDtypeStruct((b...  10.6 us
    all_to_all x2, starting transfers between devices, across(): lax.all_to_all(block, 'dp', 0, 0, axis_index_groups=groups, tiled=True)  10.4 us
    pallas_call x1, Pallas kernels, chain(): pl.pallas_call(kernel, name='chain', out_shape=jax.ShapeDtypeStruct((rows...  7.22 us
    unnamed x84, local copies, waits for them, and re-layouts  5.04 us
  transfers between devices with their start and end apart: 45, of which 20 were waited for; matrix products, arithmetic and copies ran while one was open for 4% of the time, Pallas kernels for 10%

profile of v2, /device:TPU:0, one launch (start us, length us, event | category | flops | bytes accessed | tf_op | source)
XLA Modules:
  0.0 220.3 jit_solution(8831744827045632030)
XLA Ops:
  0.7 2.4 %pack.1 = (bf16[4,2,1,32,2048]{4,3,2,1,0:T(8,128)(2,1)}, f32[32,1]{1,0:T(8,128)}) custom-call(bf16[1,4,32,8192]{3,2,1,0:T(8,128)(2,1)} %x_ref.1, bf16[1,4,32,8192]{3,2,1,0:T(8,128)(2,1)} %g_ref.1), custom_call_target="tpu_custom_call" | custom-call | bytes 4194304 | tf_op jit(solution)/shard_map/pack/pallas_call | solution.py:100
  3.3 6.3 %all-to-all-start = ((bf16[4,2,32,2048]{3,2,1,0:T(8,128)(2,1)}), bf16[4,2,32,2048]{3,2,1,0:T(8,128)(2,1)S(1)}, u32[]{:S(2)}, u32[]{:S(2)}) async-start(bf16[4,2,32,2048]{3,2,1,0:T(8,128)(2,1)} %bitcast), calls=%async_computation | async-start | bytes 2097152 | tf_op jit(solution)/shard_map/all_to_all | solution.py:46
  9.6 1.5 collective-permute-start.2
  11.1 1.5 collective-permute-start
  12.6 21.6 %collective-permute-done.2.refs_3_.refs_10_ = bf16[1024,512]{1,0:T(8,128)(2,1)S(1)} collective-permute-done((bf16[1024,512]{1,0:T(8,128)(2,1)S(1)}, bf16[1024,512]{1,0:T(8,128)(2,1)S(1)}, u32[]{:S(2)}, u32[]{:S(2)}) %collective-permute-start.2) | collective-permute-done | bytes 1048608 | tf_op jit(solution)/shard_map/ppermute | solution.py:24
  34.2 1.3 collective-permute-done.refs_2_.refs_9_
  36.1 1.6 collective-permute-start.3
  37.7 1.1 slice.60
  38.8 1.3 collective-permute-start.1
  42.1 6.3 %project.2 = bf16[4,27,32,128]{3,2,1,0:T(8,128)(2,1)} custom-call(bf16[4,2,32,2048]{3,2,1,0:T(8,128)(2,1)} %copy-done.2, bf16[1024,512]{1,0:T(8,128)(2,1)} %copy-done.1, bf16[1024,512]{1,0:T(8,128)(2,1)} %collective-permute-done.refs_2_.refs_9_, bf16[1024,512]{1,0:T(8,128)(2,1)} %copy-done.11, ...), custom_call_target="tpu_custom_call" | custom-call | flops 6442450944 | bytes 12582912 | tf_op jit(solution)/shard_map/project/pallas_call | solution.py:194
  48.4 1.7 collective-permute-done.3
  50.1 2.4 %collective-permute-done.1 = bf16[512,512]{1,0:T(8,128)(2,1)S(1)} collective-permute-done((bf16[512,512]{1,0:T(8,128)(2,1)S(1)}, bf16[512,512]{1,0:T(8,128)(2,1)S(1)}, u32[]{:S(2)}, u32[]{:S(2)}) %collective-permute-start.1) | collective-permute-done | bytes 524320 | tf_op jit(solution)/shard_map/ppermute | solution.py:24
  54.2 1.2 collective-permute-start.8
  55.9 4.1 %all-to-all-start.1 = ((bf16[4,27,32,128]{3,2,1,0:T(8,128)(2,1)}), bf16[4,27,32,128]{3,2,1,0:T(8,128)(2,1)S(1)}, u32[]{:S(2)}, u32[]{:S(2)}) async-start(bf16[4,27,32,128]{3,2,1,0:T(8,128)(2,1)} %project.2), calls=%async_computation.1 | async-start | bytes 1769472 | tf_op jit(solution)/shard_map/all_to_all | solution.py:46
  60.0 4.3 %project.3 = (bf16[9,32,128]{2,1,0:T(8,128)(2,1)}, bf16[9,32,128]{2,1,0:T(8,128)(2,1)}, bf16[9,32,128]{2,1,0:T(8,128)(2,1)}, bf16[9,32,128]{2,1,0:T(8,128)(2,1)}) custom-call(bf16[4,2,32,2048]{3,2,1,0:T(8,128)(2,1)} %copy-done.2, bf16[1024,512]{1,0:T(8,128)(2,1)} %copy-done.1, bf16[1024,512]{1,0:T(8,128)(2,1)} %constant_dynamic-update-slice_fusion.refs_2_.refs_11_, ...), custom_call_target="tpu_custom_call" | custom-call | flops 2147483648 | bytes 8388608 | tf_op jit(solution)/shard_map/project/pallas_call | solution.py:194
  64.3 2.0 collective-permute-start.19
  66.4 2.4 %collective-permute-start.20 = (bf16[9,32,128]{2,1,0:T(8,128)(2,1)}, bf16[9,32,128]{2,1,0:T(8,128)(2,1)S(1)}, u32[]{:S(2)}, u32[]{:S(2)}) collective-permute-start(bf16[9,32,128]{2,1,0:T(8,128)(2,1)} %get-tuple-element.69), channel_id=1, source_target_pairs={{0,4},{1,5},{2,6},{3,7},{4,0},{5,1},{6,2},{7,3},{8,12},{9,13},{10,... | collective-permute-start | bytes 221192 | tf_op jit(solution)/shard_map/ppermute | solution.py:24
  68.7 11.0 %collective-permute-done.8.refs_2_ = bf16[4,2,32,2048]{3,2,1,0:T(8,128)(2,1)S(1)} collective-permute-done((bf16[4,2,32,2048]{3,2,1,0:T(8,128)(2,1)S(1)}, bf16[4,2,32,2048]{3,2,1,0:T(8,128)(2,1)S(1)}, u32[]{:S(2)}, u32[]{:S(2)}) %collective-permute-start.8) | collective-permute-done | bytes 1048608 | tf_op jit(solution)/shard_map/ppermute | solution.py:24
  79.7 1.0 collective-permute-done.7.refs_1_
  81.5 1.1 slice.47
  82.5 1.3 collective-permute-start.10
  83.8 4.1 %collective-permute-done.20.refs_13_ = bf16[9,32,128]{2,1,0:T(8,128)(2,1)S(1)} collective-permute-done((bf16[9,32,128]{2,1,0:T(8,128)(2,1)}, bf16[9,32,128]{2,1,0:T(8,128)(2,1)S(1)}, u32[]{:S(2)}, u32[]{:S(2)}) %collective-permute-start.20) | collective-permute-done | bytes 73760 | tf_op jit(solution)/shard_map/ppermute | solution.py:24
  88.7 2.5 %collective-permute-start.27 = (bf16[1,128,128]{2,1,0:T(8,128)(2,1)S(1)}, bf16[1,128,128]{2,1,0:T(8,128)(2,1)S(1)}, u32[]{:S(2)}, u32[]{:S(2)}) collective-permute-start(bf16[1,128,128]{2,1,0:T(8,128)(2,1)S(1)} %bitcast.47), channel_id=1, source_target_pairs={{0,24},{8,16},{16,8},{24,0},{1,25},{9,17},{17,9},{25,1},{2,26},{10... | collective-permute-start | bytes 98312 | tf_op jit(solution)/shard_map/ppermute | solution.py:24
  92.3 4.1 %collective-permute-done.27.refs_21_ = bf16[1,128,128]{2,1,0:T(8,128)(2,1)S(1)} collective-permute-done((bf16[1,128,128]{2,1,0:T(8,128)(2,1)S(1)}, bf16[1,128,128]{2,1,0:T(8,128)(2,1)S(1)}, u32[]{:S(2)}, u32[]{:S(2)}) %collective-permute-start.27) | collective-permute-done | bytes 32800 | tf_op jit(solution)/shard_map/ppermute | solution.py:24
  98.0 2.2 collective-permute-start.17
  101.6 2.3 %collective-permute-done.17.refs_9_ = bf16[3,128,128]{2,1,0:T(8,128)(2,1)S(1)} collective-permute-done((bf16[3,128,128]{2,1,0:T(8,128)(2,1)S(1)}, bf16[3,128,128]{2,1,0:T(8,128)(2,1)S(1)}, u32[]{:S(2)}, u32[]{:S(2)}) %collective-permute-start.17) | collective-permute-done | bytes 98336 | tf_op jit(solution)/shard_map/ppermute | solution.py:24
  103.8 2.0 collective-permute-done.15.refs_7_
  106.9 1.1 pad_maximum_fusion.1.refs_3_
  108.7 7.2 %chain.1 = bf16[32,2176]{1,0:T(8,128)(2,1)} custom-call(f32[32,1]{1,0:T(8,128)} %get-tuple-element.67.refs_0_, s32[4,1,32]{2,1,0:T(1,128)} %bitcast.58, bf16[4,27,32,128]{3,2,1,0:T(8,128)(2,1)} %copy-done, bf16[3,128,128]{2,1,0:T(8,128)(2,1)} %bitcast.46, bf16[3,128,128]{2,1,0:T(8,128)(2,1)} %copy-done.30, bf16[3,128,128]{2,1,0:T(8,128)(2,1)} %copy-done.29, ...), custom_call_target="tpu_custom_call" | custom-call | flops 8589934592 | bytes 4194304 | tf_op jit(solution)/shard_map/chain/pallas_call | solution.py:308
  116.0 3.5 %collective-permute-start.31 = (bf16[32,2176]{1,0:T(8,128)(2,1)}, bf16[32,2176]{1,0:T(8,128)(2,1)S(1)}, u32[]{:S(2)}, u32[]{:S(2)}) collective-permute-start(bf16[32,2176]{1,0:T(8,128)(2,1)} %chain.1), channel_id=1, source_target_pairs={{0,6},{1,7},{2,4},{3,5},{4,2},{5,3},{6,0},{7,1},{8,14},{9,15},{10,... | collective-permute-start | bytes 417800 | tf_op jit(solution)/shard_map/ppermute | solution.py:24
  120.4 4.2 %collective-permute-done.31 = bf16[32,2176]{1,0:T(8,128)(2,1)S(1)} collective-permute-done((bf16[32,2176]{1,0:T(8,128)(2,1)}, bf16[32,2176]{1,0:T(8,128)(2,1)S(1)}, u32[]{:S(2)}, u32[]{:S(2)}) %collective-permute-start.31) | collective-permute-done | bytes 139296 | tf_op jit(solution)/shard_map/ppermute | solution.py:24
  124.6 7.4 %collective-permute-done.30 = bf16[32,2176]{1,0:T(8,128)(2,1)S(1)} collective-permute-done((bf16[32,2176]{1,0:T(8,128)(2,1)}, bf16[32,2176]{1,0:T(8,128)(2,1)S(1)}, u32[]{:S(2)}, u32[]{:S(2)}) %collective-permute-start.30) | collective-permute-done | bytes 139296 | tf_op jit(solution)/shard_map/ppermute | solution.py:24
  133.0 1.3 collective-permute-start.32
  135.1 11.9 %collective-permute-done.32.refs_5_ = bf16[4,32,2176]{2,1,0:T(8,128)(2,1)S(1)} collective-permute-done((bf16[4,32,2176]{2,1,0:T(8,128)(2,1)S(1)}, bf16[4,32,2176]{2,1,0:T(8,128)(2,1)S(1)}, u32[]{:S(2)}, u32[]{:S(2)}) %collective-permute-start.32) | collective-permute-done | bytes 557088 | tf_op jit(solution)/shard_map/ppermute | solution.py:24
  147.8 1.3 collective-permute-start.35
  149.0 5.1 %collective-permute-done.34 = bf16[2,32,2176]{2,1,0:T(8,128)(2,1)S(1)} collective-permute-done((bf16[2,32,2176]{2,1,0:T(8,128)(2,1)S(1)}, bf16[2,32,2176]{2,1,0:T(8,128)(2,1)S(1)}, u32[]{:S(2)}, u32[]{:S(2)}) %collective-permute-start.34) | collective-permute-done | bytes 278560 | tf_op jit(solution)/shard_map/ppermute | solution.py:24
  155.3 12.2 %rebuild.3 = (bf16[4,32,1024]{2,1,0:T(8,128)(2,1)}, bf16[4,32,1024]{2,1,0:T(8,128)(2,1)}, bf16[4,32,1024]{2,1,0:T(8,128)(2,1)}, bf16[4,32,1024]{2,1,0:T(8,128)(2,1)}, f32[1024,512]{1,0:T(8,128)}) custom-call(bf16[4,2,32,2048]{3,2,1,0:T(8,128)(2,1)} %copy-done.2, bf16[4,2,32,2048]{3,2,1,0:T(8,128)(2,1)} %collective-permute-done.7.refs_1_, ...), custom_call_target="tpu_custom_call" | custom-call | flops 12884901888 | bytes 16777216 | tf_op jit(solution)/shard_map/rebuild/pallas_call | solution.py:396
  167.6 2.9 %collective-permute-start.37 = (bf16[128,1024]{1,0:T(8,128)(2,1)}, bf16[128,1024]{1,0:T(8,128)(2,1)S(1)}, u32[]{:S(2)}, u32[]{:S(2)}) collective-permute-start(bf16[128,1024]{1,0:T(8,128)(2,1)} %bitcast.56), channel_id=1, source_target_pairs={{0,4},{1,5},{2,6},{3,7},{4,0},{5,1},{6,2},{7,3},{8,12},{9,13},{10,... | collective-permute-start | bytes 786440 | tf_op jit(solution)/shard_map/ppermute | solution.py:24
  170.6 1.4 collective-permute-start.38
  172.0 12.2 %rebuild.2 = (bf16[4,32,1024]{2,1,0:T(8,128)(2,1)}, bf16[4,32,1024]{2,1,0:T(8,128)(2,1)}, bf16[4,32,1024]{2,1,0:T(8,128)(2,1)}, bf16[4,32,1024]{2,1,0:T(8,128)(2,1)}, f32[1024,512]{1,0:T(8,128)}) custom-call(bf16[4,2,32,2048]{3,2,1,0:T(8,128)(2,1)} %copy-done.2, bf16[4,2,32,2048]{3,2,1,0:T(8,128)(2,1)} %collective-permute-done.7.refs_1_, ...), custom_call_target="tpu_custom_call" | custom-call | flops 12884901888 | bytes 16777216 | tf_op jit(solution)/shard_map/rebuild/pallas_call | solution.py:396
  184.2 5.0 %collective-permute-done.37.refs_5_ = bf16[128,1024]{1,0:T(8,128)(2,1)S(1)} collective-permute-done((bf16[128,1024]{1,0:T(8,128)(2,1)}, bf16[128,1024]{1,0:T(8,128)(2,1)S(1)}, u32[]{:S(2)}, u32[]{:S(2)}) %collective-permute-start.37) | collective-permute-done | bytes 262176 | tf_op jit(solution)/shard_map/ppermute | solution.py:24
  189.2 5.6 %collective-permute-start.39 = (bf16[128,1024]{1,0:T(8,128)(2,1)}, bf16[128,1024]{1,0:T(8,128)(2,1)S(1)}, u32[]{:S(2)}, u32[]{:S(2)}) collective-permute-start(bf16[128,1024]{1,0:T(8,128)(2,1)} %bitcast.54), channel_id=1, source_target_pairs={{0,2},{1,3},{2,0},{3,1},{4,6},{5,7},{6,4},{7,5},{8,10},{9,11},{10,... | collective-permute-start | bytes 786440 | tf_op jit(solution)/shard_map/ppermute | solution.py:24
  195.8 1.5 collective-permute-start.41
  197.3 2.1 add.15
  199.4 1.4 slice_bitcast_fusion
  200.7 5.0 %collective-permute-done.39.refs_2_ = bf16[128,1024]{1,0:T(8,128)(2,1)S(1)} collective-permute-done((bf16[128,1024]{1,0:T(8,128)(2,1)}, bf16[128,1024]{1,0:T(8,128)(2,1)S(1)}, u32[]{:S(2)}, u32[]{:S(2)}) %collective-permute-start.39) | collective-permute-done | bytes 262176 | tf_op jit(solution)/shard_map/ppermute | solution.py:24
  205.8 10.7 %collective-permute-done.40.refs_4_ = bf16[128,1024]{1,0:T(8,128)(2,1)S(1)} collective-permute-done((bf16[128,1024]{1,0:T(8,128)(2,1)}, bf16[128,1024]{1,0:T(8,128)(2,1)S(1)}, u32[]{:S(2)}, u32[]{:S(2)}) %collective-permute-start.40) | collective-permute-done | bytes 262176 | tf_op jit(solution)/shard_map/ppermute | solution.py:24
  217.3 2.9 %unpack.1 = bf16[128,8192]{1,0:T(8,128)(2,1)} custom-call(bf16[128,1024]{1,0:T(8,128)(2,1)} %bitcast.33, bf16[128,1024]{1,0:T(8,128)(2,1)} %bitcast.32, bf16[128,1024]{1,0:T(8,128)(2,1)} %copy-done.8, bf16[128,1024]{1,0:T(8,128)(2,1)} %copy-done.5, bf16[128,1024]{1,0:T(8,128)(2,1)} %copy-done.9, bf16[128,1024]{1,0:T(8,128)(2,1)} %copy-done.6, ...), custom_call_target="tpu_custom_call" | custom-call | bytes 8388608 | tf_op jit(solution)/shard_map/unpack/pallas_call | solution.py:135
  (148 shorter events, 18.3 us)
Async XLA Ops:
  3.3 35.5 %copy-start.1 = (bf16[1024,512]{1,0:T(8,128)(2,1)}, bf16[1024,512]{1,0:T(8,128)(2,1)S(1)}, u32[]{:S(2)}) copy-start(bf16[1024,512]{1,0:T(8,128)(2,1)S(1)} %pad_maximum_fusion.refs_1_.refs_8_) | copy-start | bytes 3145732
  3.3 32.3 %all-to-all-start = ((bf16[4,2,32,2048]{3,2,1,0:T(8,128)(2,1)}), bf16[4,2,32,2048]{3,2,1,0:T(8,128)(2,1)S(1)}, u32[]{:S(2)}, u32[]{:S(2)}) async-start(bf16[4,2,32,2048]{3,2,1,0:T(8,128)(2,1)} %bitcast), calls=%async_computation | async-start | bytes 2097152 | tf_op jit(solution)/shard_map/all_to_all | solution.py:46
  9.6 24.6 %collective-permute-start.2 = (bf16[1024,512]{1,0:T(8,128)(2,1)S(1)}, bf16[1024,512]{1,0:T(8,128)(2,1)S(1)}, u32[]{:S(2)}, u32[]{:S(2)}) collective-permute-start(bf16[1024,512]{1,0:T(8,128)(2,1)S(1)} %pad_maximum_fusion.refs_1_.refs_8_), channel_id=1, source_target_pairs={{0,16},{8,24},{16,0},{24,8},{1,17},{9,25},{17,1},{25,9},{2,18},{10... | collective-permute-start | bytes 3145736 | tf_op jit(solution)/shard_map/ppermute | solution.py:24
  11.1 24.4 %collective-permute-start = (bf16[1024,512]{1,0:T(8,128)(2,1)S(1)}, bf16[1024,512]{1,0:T(8,128)(2,1)}, u32[]{:S(2)}, u32[]{:S(2)}) collective-permute-start(bf16[1024,512]{1,0:T(8,128)(2,1)S(1)} %pad_maximum_fusion.refs_1_.refs_8_), channel_id=1, source_target_pairs={{0,8},{8,0},{16,24},{24,16},{1,9},{9,1},{17,25},{25,17},{2,10},{10... | collective-permute-start | bytes 3145736 | tf_op jit(solution)/shard_map/ppermute | solution.py:24
  12.6 27.5 %collective-permute-start.4 = (bf16[1024,512]{1,0:T(8,128)(2,1)S(1)}, bf16[1024,512]{1,0:T(8,128)(2,1)}, u32[]{:S(2)}, u32[]{:S(2)}) collective-permute-start(bf16[1024,512]{1,0:T(8,128)(2,1)S(1)} %pad_maximum_fusion.refs_1_.refs_8_), channel_id=1, source_target_pairs={{0,1},{1,0},{2,3},{3,2},{4,5},{5,4},{6,7},{7,6},{8,9},{9,8},{10,11... | collective-permute-start | bytes 3145736 | tf_op jit(solution)/shard_map/ppermute | solution.py:24
  35.6 4.5 %collective-permute-start.5 = (bf16[1024,512]{1,0:T(8,128)(2,1)}, bf16[1024,512]{1,0:T(8,128)(2,1)S(1)}, u32[]{:S(2)}, u32[]{:S(2)}) collective-permute-start(bf16[1024,512]{1,0:T(8,128)(2,1)} %collective-permute-done.refs_2_.refs_9_), channel_id=1, source_target_pairs={{0,1},{1,0},{2,3},{3,2},{4,5},{5,4},{6,7},{7,6},{8,9},{9,8},{10,11... | collective-permute-start | bytes 3145736 | tf_op jit(solution)/shard_map/ppermute | solution.py:24
  35.6 4.5 %collective-permute-start.6 = (bf16[1024,512]{1,0:T(8,128)(2,1)S(1)}, bf16[1024,512]{1,0:T(8,128)(2,1)S(1)}, u32[]{:S(2)}, u32[]{:S(2)}) collective-permute-start(bf16[1024,512]{1,0:T(8,128)(2,1)S(1)} %collective-permute-done.2.refs_3_.refs_10_), channel_id=1, source_target_pairs={{0,1},{1,0},{2,3},{3,2},{4,5},{5,4},{6,7},{7,6},{8,9},{9,8},{10,11... | collective-permute-start | bytes 3145736 | tf_op jit(solution)/shard_map/ppermute | solution.py:24
  36.1 14.0 %collective-permute-start.3 = (bf16[512,512]{1,0:T(8,128)(2,1)S(1)}, bf16[512,512]{1,0:T(8,128)(2,1)S(1)}, u32[]{:S(2)}, u32[]{:S(2)}) collective-permute-start(bf16[512,512]{1,0:T(8,128)(2,1)S(1)} %slice.61), channel_id=1, source_target_pairs={{0,8},{8,0},{16,24},{24,16},{1,9},{9,1},{17,25},{25,17},{2,10},{10... | collective-permute-start | bytes 1572872 | tf_op jit(solution)/shard_map/ppermute | solution.py:24
  38.8 13.7 %collective-permute-start.1 = (bf16[512,512]{1,0:T(8,128)(2,1)S(1)}, bf16[512,512]{1,0:T(8,128)(2,1)S(1)}, u32[]{:S(2)}, u32[]{:S(2)}) collective-permute-start(bf16[512,512]{1,0:T(8,128)(2,1)S(1)} %slice.60), channel_id=1, source_target_pairs={{0,16},{8,24},{16,0},{24,8},{1,17},{9,25},{17,1},{25,9},{2,18},{10... | collective-permute-start | bytes 1572872 | tf_op jit(solution)/shard_map/ppermute | solution.py:24
  54.2 5.9 %collective-permute-start.9 = (bf16[1024,512]{1,0:T(8,128)(2,1)}, bf16[1024,512]{1,0:T(8,128)(2,1)}, u32[]{:S(2)}, u32[]{:S(2)}) collective-permute-start(bf16[1024,512]{1,0:T(8,128)(2,1)} %constant_dynamic-update-slice_fusion.refs_2_.refs_11_), channel_id=1, source_target_pairs={{0,1},{1,0},{2,3},{3,2},{4,5},{5,4},{6,7},{7,6},{8,9},{9,8},{10,11... | collective-permute-start | bytes 3145736 | tf_op jit(solution)/shard_map/ppermute | solution.py:24
  54.2 25.6 %collective-permute-start.8 = (bf16[4,2,32,2048]{3,2,1,0:T(8,128)(2,1)S(1)}, bf16[4,2,32,2048]{3,2,1,0:T(8,128)(2,1)S(1)}, u32[]{:S(2)}, u32[]{:S(2)}) collective-permute-start(bf16[4,2,32,2048]{3,2,1,0:T(8,128)(2,1)S(1)} %copy-done.3), channel_id=1, source_target_pairs={{0,16},{8,24},{16,0},{24,8},{1,17},{9,25},{17,1},{25,9},{2,18},{10... | collective-permute-start | bytes 3145736 | tf_op jit(solution)/shard_map/ppermute | solution.py:24
  55.4 25.4 %collective-permute-start.7 = (bf16[4,2,32,2048]{3,2,1,0:T(8,128)(2,1)S(1)}, bf16[4,2,32,2048]{3,2,1,0:T(8,128)(2,1)}, u32[]{:S(2)}, u32[]{:S(2)}) collective-permute-start(bf16[4,2,32,2048]{3,2,1,0:T(8,128)(2,1)S(1)} %copy-done.3), channel_id=1, source_target_pairs={{0,8},{8,0},{16,24},{24,16},{1,9},{9,1},{17,25},{25,17},{2,10},{10... | collective-permute-start | bytes 3145736 | tf_op jit(solution)/shard_map/ppermute | solution.py:24
  55.9 42.0 %all-to-all-start.1 = ((bf16[4,27,32,128]{3,2,1,0:T(8,128)(2,1)}), bf16[4,27,32,128]{3,2,1,0:T(8,128)(2,1)S(1)}, u32[]{:S(2)}, u32[]{:S(2)}) async-start(bf16[4,27,32,128]{3,2,1,0:T(8,128)(2,1)} %project.2), calls=%async_computation.1 | async-start | bytes 1769472 | tf_op jit(solution)/shard_map/all_to_all | solution.py:46
  64.3 19.5 %collective-permute-start.19 = (bf16[9,32,128]{2,1,0:T(8,128)(2,1)}, bf16[9,32,128]{2,1,0:T(8,128)(2,1)S(1)}, u32[]{:S(2)}, u32[]{:S(2)}) collective-permute-start(bf16[9,32,128]{2,1,0:T(8,128)(2,1)} %get-tuple-element.68), channel_id=1, source_target_pairs={{0,2},{1,3},{2,0},{3,1},{4,6},{5,7},{6,4},{7,5},{8,10},{9,11},{10,... | collective-permute-start | bytes 221192 | tf_op jit(solution)/shard_map/ppermute | solution.py:24
  66.4 21.5 %collective-permute-start.20 = (bf16[9,32,128]{2,1,0:T(8,128)(2,1)}, bf16[9,32,128]{2,1,0:T(8,128)(2,1)S(1)}, u32[]{:S(2)}, u32[]{:S(2)}) collective-permute-start(bf16[9,32,128]{2,1,0:T(8,128)(2,1)} %get-tuple-element.69), channel_id=1, source_target_pairs={{0,4},{1,5},{2,6},{3,7},{4,0},{5,1},{6,2},{7,3},{8,12},{9,13},{10,... | collective-permute-start | bytes 221192 | tf_op jit(solution)/shard_map/ppermute | solution.py:24
  68.7 19.1 %collective-permute-start.21 = (bf16[9,32,128]{2,1,0:T(8,128)(2,1)}, bf16[9,32,128]{2,1,0:T(8,128)(2,1)S(1)}, u32[]{:S(2)}, u32[]{:S(2)}) collective-permute-start(bf16[9,32,128]{2,1,0:T(8,128)(2,1)} %get-tuple-element.70), channel_id=1, source_target_pairs={{0,6},{1,7},{2,4},{3,5},{4,2},{5,3},{6,0},{7,1},{8,14},{9,15},{10,... | collective-permute-start | bytes 221192 | tf_op jit(solution)/shard_map/ppermute | solution.py:24
  80.9 25.5 %collective-permute-start.11 = (bf16[2,2,32,2048]{3,2,1,0:T(8,128)(2,1)S(1)}, bf16[2,2,32,2048]{3,2,1,0:T(8,128)(2,1)S(1)}, u32[]{:S(2)}, u32[]{:S(2)}) collective-permute-start(bf16[2,2,32,2048]{3,2,1,0:T(8,128)(2,1)S(1)} %slice.48), channel_id=1, source_target_pairs={{0,8},{8,0},{16,24},{24,16},{1,9},{9,1},{17,25},{25,17},{2,10},{10... | collective-permute-start | bytes 1572872 | tf_op jit(solution)/shard_map/ppermute | solution.py:24
  82.5 23.9 %collective-permute-start.10 = (bf16[2,2,32,2048]{3,2,1,0:T(8,128)(2,1)S(1)}, bf16[2,2,32,2048]{3,2,1,0:T(8,128)(2,1)S(1)}, u32[]{:S(2)}, u32[]{:S(2)}) collective-permute-start(bf16[2,2,32,2048]{3,2,1,0:T(8,128)(2,1)S(1)} %slice.47), channel_id=1, source_target_pairs={{0,16},{8,24},{16,0},{24,8},{1,17},{9,25},{17,1},{25,9},{2,18},{10... | collective-permute-start | bytes 1572872 | tf_op jit(solution)/shard_map/ppermute | solution.py:24
  83.8 24.3 %copy-start.22 = (bf16[9,32,128]{2,1,0:T(8,128)(2,1)}, bf16[9,32,128]{2,1,0:T(8,128)(2,1)S(1)}, u32[]{:S(2)}) copy-start(bf16[9,32,128]{2,1,0:T(8,128)(2,1)S(1)} %collective-permute-done.19.refs_12_) | copy-start | bytes 221188
  88.7 7.7 %collective-permute-start.27 = (bf16[1,128,128]{2,1,0:T(8,128)(2,1)S(1)}, bf16[1,128,128]{2,1,0:T(8,128)(2,1)S(1)}, u32[]{:S(2)}, u32[]{:S(2)}) collective-permute-start(bf16[1,128,128]{2,1,0:T(8,128)(2,1)S(1)} %bitcast.47), channel_id=1, source_target_pairs={{0,24},{8,16},{16,8},{24,0},{1,25},{9,17},{17,9},{25,1},{2,26},{10... | collective-permute-start | bytes 98312 | tf_op jit(solution)/shard_map/ppermute | solution.py:24
  91.2 6.2 %collective-permute-start.25 = (bf16[1,128,128]{2,1,0:T(8,128)(2,1)S(1)}, bf16[1,128,128]{2,1,0:T(8,128)(2,1)S(1)}, u32[]{:S(2)}, u32[]{:S(2)}) collective-permute-start(bf16[1,128,128]{2,1,0:T(8,128)(2,1)S(1)} %bitcast.48), channel_id=1, source_target_pairs={{0,16},{8,24},{16,0},{24,8},{1,17},{9,25},{17,1},{25,9},{2,18},{10... | collective-permute-start | bytes 98312 | tf_op jit(solution)/shard_map/ppermute | solution.py:24
  91.7 5.7 %collective-permute-start.23 = (bf16[1,128,128]{2,1,0:T(8,128)(2,1)S(1)}, bf16[1,128,128]{2,1,0:T(8,128)(2,1)S(1)}, u32[]{:S(2)}, u32[]{:S(2)}) collective-permute-start(bf16[1,128,128]{2,1,0:T(8,128)(2,1)S(1)} %bitcast.49), channel_id=1, source_target_pairs={{0,8},{8,0},{16,24},{24,16},{1,9},{9,1},{17,25},{25,17},{2,10},{10... | collective-permute-start | bytes 98312 | tf_op jit(solution)/shard_map/ppermute | solution.py:24
  96.4 1.6 collective-permute-start.22
  97.4 2.8 %collective-permute-start.28 = (bf16[1,128,128]{2,1,0:T(8,128)(2,1)S(1)}, bf16[1,128,128]{2,1,0:T(8,128)(2,1)S(1)}, u32[]{:S(2)}, u32[]{:S(2)}) collective-permute-start(bf16[1,128,128]{2,1,0:T(8,128)(2,1)S(1)} %collective-permute-done.27.refs_21_), channel_id=1, source_target_pairs={{0,1},{1,0},{2,3},{3,2},{4,5},{5,4},{6,7},{7,6},{8,9},{9,8},{10,11... | collective-permute-start | bytes 98312 | tf_op jit(solution)/shard_map/ppermute | solution.py:24
  97.4 3.6 %collective-permute-start.26 = (bf16[1,128,128]{2,1,0:T(8,128)(2,1)S(1)}, bf16[1,128,128]{2,1,0:T(8,128)(2,1)S(1)}, u32[]{:S(2)}, u32[]{:S(2)}) collective-permute-start(bf16[1,128,128]{2,1,0:T(8,128)(2,1)S(1)} %collective-permute-done.25.refs_19_), channel_id=1, source_target_pairs={{0,1},{1,0},{2,3},{3,2},{4,5},{5,4},{6,7},{7,6},{8,9},{9,8},{10,11... | collective-permute-start | bytes 98312 | tf_op jit(solution)/shard_map/ppermute | solution.py:24
  98.0 5.8 %collective-permute-start.17 = (bf16[3,128,128]{2,1,0:T(8,128)(2,1)S(1)}, bf16[3,128,128]{2,1,0:T(8,128)(2,1)S(1)}, u32[]{:S(2)}, u32[]{:S(2)}) collective-permute-start(bf16[3,128,128]{2,1,0:T(8,128)(2,1)S(1)} %bitcast.42), channel_id=1, source_target_pairs={{0,24},{8,16},{16,8},{24,0},{1,25},{9,17},{17,9},{25,1},{2,26},{10... | collective-permute-start | bytes 294920 | tf_op jit(solution)/shard_map/ppermute | solution.py:24
  100.2 5.6 %collective-permute-start.15 = (bf16[3,128,128]{2,1,0:T(8,128)(2,1)S(1)}, bf16[3,128,128]{2,1,0:T(8,128)(2,1)S(1)}, u32[]{:S(2)}, u32[]{:S(2)}) collective-permute-start(bf16[3,128,128]{2,1,0:T(8,128)(2,1)S(1)} %bitcast.43), channel_id=1, source_target_pairs={{0,16},{8,24},{16,0},{24,8},{1,17},{9,25},{17,1},{25,9},{2,18},{10... | collective-permute-start | bytes 294920 | tf_op jit(solution)/shard_map/ppermute | solution.py:24
  101.0 4.8 %collective-permute-start.13 = (bf16[3,128,128]{2,1,0:T(8,128)(2,1)S(1)}, bf16[3,128,128]{2,1,0:T(8,128)(2,1)S(1)}, u32[]{:S(2)}, u32[]{:S(2)}) collective-permute-start(bf16[3,128,128]{2,1,0:T(8,128)(2,1)S(1)} %bitcast.44), channel_id=1, source_target_pairs={{0,8},{8,0},{16,24},{24,16},{1,9},{9,1},{17,25},{25,17},{2,10},{10... | collective-permute-start | bytes 294920 | tf_op jit(solution)/shard_map/ppermute | solution.py:24
  103.8 4.2 %collective-permute-start.24 = (bf16[1,128,128]{2,1,0:T(8,128)(2,1)S(1)}, bf16[1,128,128]{2,1,0:T(8,128)(2,1)S(1)}, u32[]{:S(2)}, u32[]{:S(2)}) collective-permute-start(bf16[1,128,128]{2,1,0:T(8,128)(2,1)S(1)} %collective-permute-done.23.refs_17_), channel_id=1, source_target_pairs={{0,1},{1,0},{2,3},{3,2},{4,5},{5,4},{6,7},{7,6},{8,9},{9,8},{10,11... | collective-permute-start | bytes 98312 | tf_op jit(solution)/shard_map/ppermute | solution.py:24
  105.8 2.2 collective-permute-start.12
  105.9 2.2 collective-permute-start.18
  106.4 1.7 collective-permute-start.16
  106.5 1.6 collective-permute-start.14
  116.0 8.6 %collective-permute-start.31 = (bf16[32,2176]{1,0:T(8,128)(2,1)}, bf16[32,2176]{1,0:T(8,128)(2,1)S(1)}, u32[]{:S(2)}, u32[]{:S(2)}) collective-permute-start(bf16[32,2176]{1,0:T(8,128)(2,1)} %chain.1), channel_id=1, source_target_pairs={{0,6},{1,7},{2,4},{3,5},{4,2},{5,3},{6,0},{7,1},{8,14},{9,15},{10,... | collective-permute-start | bytes 417800 | tf_op jit(solution)/shard_map/ppermute | solution.py:24
  119.5 12.5 %collective-permute-start.30 = (bf16[32,2176]{1,0:T(8,128)(2,1)}, bf16[32,2176]{1,0:T(8,128)(2,1)S(1)}, u32[]{:S(2)}, u32[]{:S(2)}) collective-permute-start(bf16[32,2176]{1,0:T(8,128)(2,1)} %chain.1), channel_id=1, source_target_pairs={{0,4},{1,5},{2,6},{3,7},{4,0},{5,1},{6,2},{7,3},{8,12},{9,13},{10,... | collective-permute-start | bytes 417800 | tf_op jit(solution)/shard_map/ppermute | solution.py:24
  119.5 12.5 %collective-permute-start.29 = (bf16[32,2176]{1,0:T(8,128)(2,1)}, bf16[32,2176]{1,0:T(8,128)(2,1)S(1)}, u32[]{:S(2)}, u32[]{:S(2)}) collective-permute-start(bf16[32,2176]{1,0:T(8,128)(2,1)} %chain.1), channel_id=1, source_target_pairs={{0,2},{1,3},{2,0},{3,1},{4,6},{5,7},{6,4},{7,5},{8,10},{9,11},{10,... | collective-permute-start | bytes 417800 | tf_op jit(solution)/shard_map/ppermute | solution.py:24
  133.0 21.5 %copy-start.4 = (bf16[4,32,2176]{2,1,0:T(8,128)(2,1)}, bf16[4,32,2176]{2,1,0:T(8,128)(2,1)S(1)}, u32[]{:S(2)}) copy-start(bf16[4,32,2176]{2,1,0:T(8,128)(2,1)S(1)} %pad_maximum_fusion.2.refs_4_) | copy-start | bytes 1671172
  133.0 14.0 %collective-permute-start.32 = (bf16[4,32,2176]{2,1,0:T(8,128)(2,1)S(1)}, bf16[4,32,2176]{2,1,0:T(8,128)(2,1)S(1)}, u32[]{:S(2)}, u32[]{:S(2)}) collective-permute-start(bf16[4,32,2176]{2,1,0:T(8,128)(2,1)S(1)} %pad_maximum_fusion.2.refs_4_), channel_id=1, source_target_pairs={{0,8},{8,0},{16,24},{24,16},{1,9},{9,1},{17,25},{25,17},{2,10},{10... | collective-permute-start | bytes 1671176 | tf_op jit(solution)/shard_map/ppermute | solution.py:24
  134.3 13.5 %collective-permute-start.33 = (bf16[4,32,2176]{2,1,0:T(8,128)(2,1)S(1)}, bf16[4,32,2176]{2,1,0:T(8,128)(2,1)S(1)}, u32[]{:S(2)}, u32[]{:S(2)}) collective-permute-start(bf16[4,32,2176]{2,1,0:T(8,128)(2,1)S(1)} %pad_maximum_fusion.2.refs_4_), channel_id=1, source_target_pairs={{0,16},{8,24},{16,0},{24,8},{1,17},{9,25},{17,1},{25,9},{2,18},{10... | collective-permute-start | bytes 1671176 | tf_op jit(solution)/shard_map/ppermute | solution.py:24
  147.0 7.1 %collective-permute-start.34 = (bf16[2,32,2176]{2,1,0:T(8,128)(2,1)S(1)}, bf16[2,32,2176]{2,1,0:T(8,128)(2,1)S(1)}, u32[]{:S(2)}, u32[]{:S(2)}) collective-permute-start(bf16[2,32,2176]{2,1,0:T(8,128)(2,1)S(1)} %slice.66), channel_id=1, source_target_pairs={{0,16},{8,24},{16,0},{24,8},{1,17},{9,25},{17,1},{25,9},{2,18},{10... | collective-permute-start | bytes 835592 | tf_op jit(solution)/shard_map/ppermute | solution.py:24
  147.8 6.7 %collective-permute-start.35 = (bf16[2,32,2176]{2,1,0:T(8,128)(2,1)S(1)}, bf16[2,32,2176]{2,1,0:T(8,128)(2,1)S(1)}, u32[]{:S(2)}, u32[]{:S(2)}) collective-permute-start(bf16[2,32,2176]{2,1,0:T(8,128)(2,1)S(1)} %slice.67), channel_id=1, source_target_pairs={{0,8},{8,0},{16,24},{24,16},{1,9},{9,1},{17,25},{25,17},{2,10},{10... | collective-permute-start | bytes 835592 | tf_op jit(solution)/shard_map/ppermute | solution.py:24
  167.5 29.8 %collective-permute-start.42 = (f32[1024,512]{1,0:T(8,128)}, f32[1024,512]{1,0:T(8,128)S(1)}, u32[]{:S(2)}, u32[]{:S(2)}) collective-permute-start(f32[1024,512]{1,0:T(8,128)} %get-tuple-element.84), channel_id=1, source_target_pairs={{0,1},{1,0},{2,3},{3,2},{4,5},{5,4},{6,7},{7,6},{8,9},{9,8},{10,11... | collective-permute-start | bytes 6291464 | tf_op jit(solution)/shard_map/ppermute | solution.py:24
  167.6 16.6 %collective-permute-start.36 = (bf16[128,1024]{1,0:T(8,128)(2,1)}, bf16[128,1024]{1,0:T(8,128)(2,1)S(1)}, u32[]{:S(2)}, u32[]{:S(2)}) collective-permute-start(bf16[128,1024]{1,0:T(8,128)(2,1)} %bitcast.57), channel_id=1, source_target_pairs={{0,2},{1,3},{2,0},{3,1},{4,6},{5,7},{6,4},{7,5},{8,10},{9,11},{10,... | collective-permute-start | bytes 786440 | tf_op jit(solution)/shard_map/ppermute | solution.py:24
  167.6 21.6 %collective-permute-start.37 = (bf16[128,1024]{1,0:T(8,128)(2,1)}, bf16[128,1024]{1,0:T(8,128)(2,1)S(1)}, u32[]{:S(2)}, u32[]{:S(2)}) collective-permute-start(bf16[128,1024]{1,0:T(8,128)(2,1)} %bitcast.56), channel_id=1, source_target_pairs={{0,4},{1,5},{2,6},{3,7},{4,0},{5,1},{6,2},{7,3},{8,12},{9,13},{10,... | collective-permute-start | bytes 786440 | tf_op jit(solution)/shard_map/ppermute | solution.py:24
  170.6 18.7 %collective-permute-start.38 = (bf16[128,1024]{1,0:T(8,128)(2,1)}, bf16[128,1024]{1,0:T(8,128)(2,1)S(1)}, u32[]{:S(2)}, u32[]{:S(2)}) collective-permute-start(bf16[128,1024]{1,0:T(8,128)(2,1)} %bitcast.55), channel_id=1, source_target_pairs={{0,6},{1,7},{2,4},{3,5},{4,2},{5,3},{6,0},{7,1},{8,14},{9,15},{10,... | collective-permute-start | bytes 786440 | tf_op jit(solution)/shard_map/ppermute | solution.py:24
  189.2 16.5 %collective-permute-start.39 = (bf16[128,1024]{1,0:T(8,128)(2,1)}, bf16[128,1024]{1,0:T(8,128)(2,1)S(1)}, u32[]{:S(2)}, u32[]{:S(2)}) collective-permute-start(bf16[128,1024]{1,0:T(8,128)(2,1)} %bitcast.54), channel_id=1, source_target_pairs={{0,2},{1,3},{2,0},{3,1},{4,6},{5,7},{6,4},{7,5},{8,10},{9,11},{10,... | collective-permute-start | bytes 786440 | tf_op jit(solution)/shard_map/ppermute | solution.py:24
  194.9 21.6 %collective-permute-start.40 = (bf16[128,1024]{1,0:T(8,128)(2,1)}, bf16[128,1024]{1,0:T(8,128)(2,1)S(1)}, u32[]{:S(2)}, u32[]{:S(2)}) collective-permute-start(bf16[128,1024]{1,0:T(8,128)(2,1)} %bitcast.53), channel_id=1, source_target_pairs={{0,4},{1,5},{2,6},{3,7},{4,0},{5,1},{6,2},{7,3},{8,12},{9,13},{10,... | collective-permute-start | bytes 786440 | tf_op jit(solution)/shard_map/ppermute | solution.py:24
  195.8 20.7 %collective-permute-start.41 = (bf16[128,1024]{1,0:T(8,128)(2,1)}, bf16[128,1024]{1,0:T(8,128)(2,1)S(1)}, u32[]{:S(2)}, u32[]{:S(2)}) collective-permute-start(bf16[128,1024]{1,0:T(8,128)(2,1)} %bitcast.52), channel_id=1, source_target_pairs={{0,6},{1,7},{2,4},{3,5},{4,2},{5,3},{6,0},{7,1},{8,14},{9,15},{10,... | collective-permute-start | bytes 786440 | tf_op jit(solution)/shard_map/ppermute | solution.py:24
  (38 other events, 243.1 us)

commit v3 on v2

--- a/solution.py
+++ b/solution.py
@@ -112,21 +112,31 @@
     return out.reshape(chips, 2, group * seq, CORES * eighth), squares
 
 
-def unpack(pieces, chips, width):
-    rows, eighth = pieces[0].shape
+def unpack(parts, width):
+    flat = [array for arrays, _, _ in parts for array in arrays]
+    rows, chips = flat[0].shape[-2], lax.axis_size("dp") // CORES
+    eighth = width // (chips * CORES)
+    sections = sum(len(groups) * len(halves) for _, groups, halves in parts) // CORES
 
     def kernel(*refs):
-        ins, out, sems = refs[:-2], refs[-2], refs[-1]
-        _, z, c = place()
+        ins, out, sems = list(refs[:-2]), refs[-2], refs[-1]
+        p, z, c = place()
         copies = []
-        for k in range(chips):
-            for h in range(CORES):
-                start = pl.multiple_of(((z ^ k) * CORES + (c ^ h)) * eighth, eighth)
-                copies.append(
-                    pltpu.make_async_copy(
-                        ins[k * CORES + h], out.at[:, pl.ds(start, eighth)], sems.at[len(copies)]
-                    )
-                )
+        for arrays, groups, halves in parts:
+            held = [ins.pop(0) for _ in arrays]
+            for k in range(chips):
+                chip, ref = (z ^ k, held[k]) if len(held) > 1 else (k, held[0].at[k])
+                for n, group in enumerate(groups):
+                    row = pl.multiple_of((p ^ group) * rows, rows)
+                    for i, h in enumerate(halves):
+                        start = pl.multiple_of((chip * CORES + (c ^ h)) * eighth, eighth)
+                        copies.append(
+                            pltpu.make_async_copy(
+                                ref.at[n, :, pl.ds(i * eighth, eighth)],
+                                out.at[pl.ds(row, rows), pl.ds(start, eighth)],
+                                sems.at[len(copies)],
+                            )
+                        )
         for copy in copies:
             copy.start()
         for copy in copies:
@@ -135,12 +145,12 @@
     return pl.pallas_call(
         kernel,
         name="unpack",
-        out_shape=jax.ShapeDtypeStruct((rows, width), BF),
-        in_specs=vmem(len(pieces)),
+        out_shape=jax.ShapeDtypeStruct((sections * rows, width), BF),
+        in_specs=vmem(len(flat)),
         out_specs=pl.BlockSpec(memory_space=pl.ANY),
-        scratch_shapes=[pltpu.SemaphoreType.DMA((len(pieces),))],
-        cost_estimate=cost(0, 4 * rows * width * 2),
-    )(*pieces)
+        scratch_shapes=[pltpu.SemaphoreType.DMA((sections * chips * CORES,))],
+        cost_estimate=cost(0, 4 * sections * rows * width * 2),
+    )(*flat)
 
 
 def project(tokens, own, other, wanted, head, apart):
@@ -320,20 +330,24 @@
     )(squares, docs, *flat)
 
 
-def rebuild(tokens, coefs, weights, column, head):
-    groups, sections = len(tokens), len(weights)
+def rebuild(tokens, coefs, weights, halves, head, apart):
+    groups, sections = len(coefs), len(weights[0])
     chips, rows, lanes = coefs[0].shape
-    half = weights[0].shape[0]
+    half = weights[0][0].shape[0]
     some = chips * rows
     count = groups * some
-    block = min(256, half)
+    block = min(512, half)
+    steps = half // block
+    wide = len(halves) * half
+    chosen = [weights[h] for h in halves]
 
     def kernel(*refs):
         t_refs, c_refs = refs[:groups], refs[groups : 2 * groups]
-        w_refs = refs[2 * groups : 2 * groups + sections]
-        outs = refs[2 * groups + sections : 2 * groups + sections + chips]
-        grads, left, own_m, edge, h_all, g_all = refs[2 * groups + sections + chips :]
+        w_refs = refs[2 * groups : 2 * groups + len(halves) * sections]
+        outs = refs[2 * groups + len(halves) * sections : -7]
+        h_out, g_out, left, edge, h_all, g_all, kept = refs[-7:]
         p, z, _ = place()
+        outs = outs if apart else [outs[0].at[z ^ k] for k in range(chips)]
         out_w = slice(3 * head, 4 * head)
         qkv_w = slice(0, 3 * head)
 
@@ -354,14 +368,13 @@
                     m = both[:, out_w]
 
                     def weigh(j=j, s=s, m=m):
-                        after = jnp.where((side > s) & (side < sections), scalars, 0.0)
-                        share = jnp.sum(after, axis=-1, keepdims=True)
+                        later = jnp.where((side > s) & (side < sections), scalars, 0.0)
+                        share = jnp.sum(later, axis=-1, keepdims=True)
                         left[j, at, out_w] = (-share * m.astype(F32)).astype(BF)
                         if j == 0:
                             edge[0, at, :] = jnp.broadcast_to(share, (some, head))
 
                     if j == 0:
-                        own_m[at, :] = m
                         weigh()
                     else:
                         pl.when(s > p)(weigh)
@@ -371,53 +384,104 @@
                 at = pl.ds(i * some + k * rows, rows)
                 h_all[at, :] = t_refs[i][z ^ k, 0].astype(F32)
                 g_all[at, :] = t_refs[i][z ^ k, 1].astype(F32)
-        for j in range(1, sections):
-
-            @pl.when((p ^ j) < p)
-            def _():
-                h_all[...] += dot(left[j, :, out_w], w_refs[j][:, out_w], NT)
-
-            @pl.when((p ^ j) > p)
-            def _():
-                g_all[...] += dot(left[j], w_refs[j][...], NT)
+
+        def add(held):
+            for j in range(1, sections):
+
+                @pl.when((p ^ j) < p)
+                def _():
+                    h_all[...] += dot(left[j, :, out_w], held[j][:, out_w], NT)
+
+                @pl.when((p ^ j) > p)
+                def _():
+                    g_all[...] += dot(left[j], held[j][...], NT)
+
+            g_all[...] += dot(left[0, :, out_w], held[0][:, out_w], NT)
+            kept[...] = dot(left[0, :, qkv_w], held[0][:, qkv_w], NT)
+
+        for n in range(len(halves)):
+            held = w_refs[n * sections : (n + 1) * sections]
+            if len(halves) == 1:
+                add(held)
+            else:
+                pl.when(pl.program_id(0) // steps == n)(functools.partial(add, held))
 
         h = h_all[...]
-        y = left[0, :, qkv_w]
-        g = g_all[...] + dot(left[0, :, out_w], w_refs[0][:, out_w], NT)
-        g = g - edge[0][:, :1] * h
-        grads[:, qkv_w] = dot(h.astype(BF), y, TN)
-        grads[:, out_w] = dot(g.astype(BF), own_m[...], TN)
-        result = (g + dot(y, w_refs[0][:, qkv_w], NT) - edge[1][:, :1] * h).astype(BF)
+        g = g_all[...] - edge[0][:, :1] * h
+        h_out[...] = h.astype(BF)
+        g_out[...] = g.astype(BF)
+        result = (g + kept[...] - edge[1][:, :1] * h).astype(BF)
         for i in range(groups):
             for k in range(chips):
                 at = i * some + k * rows
-                outs[k][p ^ i] = result[at : at + rows]
-
+                outs[k][i] = result[at : at + rows]
+
+    if apart:
+        shapes = [(groups, rows, wide)] * chips
+        specs = [pl.BlockSpec((groups, rows, block), lambda i: (0, 0, i))] * chips
+    else:
+        shapes = [(chips, groups, rows, wide)]
+        specs = [pl.BlockSpec((chips, groups, rows, block), lambda i: (0, 0, 0, i))]
+    first = halves[0] * steps
     outs = pl.pallas_call(
         kernel,
         name="rebuild",
-        grid=(half // block,),
-        out_shape=[jax.ShapeDtypeStruct((groups, rows, half), BF)] * chips
-        + [jax.ShapeDtypeStruct((half, 4 * head), F32)],
-        in_specs=[
-            pl.BlockSpec((chips, 2, rows, block), lambda i: (0, 0, 0, i + column // block))
-        ]
-        * groups
+        grid=(wide // block,),
+        out_shape=[jax.ShapeDtypeStruct(shape, BF) for shape in [*shapes] + [(count, wide)] * 2],
+        in_specs=[pl.BlockSpec((chips, 2, rows, block), lambda i: (0, 0, 0, i + first))] * groups
         + vmem(groups)
-        + [pl.BlockSpec((block, 4 * head), lambda i: (i, 0))] * sections,
-        out_specs=[pl.BlockSpec((groups, rows, block), lambda i: (0, 0, i))] * chips
-        + [pl.BlockSpec((block, 4 * head), lambda i: (i, 0))],
+        + [
+            pl.BlockSpec(
+                (block, 4 * head), lambda i, n=n: (jnp.clip(i - n * steps, 0, steps - 1), 0)
+            )
+            for n in range(len(halves))
+            for _ in range(sections)
+        ],
+        out_specs=specs + [pl.BlockSpec((count, block), lambda i: (0, i))] * 2,
         scratch_shapes=[
             pltpu.VMEM((sections, count, 4 * head), BF),
-            pltpu.VMEM((count, head), BF),
             pltpu.VMEM((2, count, head), F32),
             pltpu.VMEM((count, block), F32),
             pltpu.VMEM((count, block), F32),
+            pltpu.VMEM((count, block), F32),
         ],
-        cost_estimate=cost(12 * count * half * head * 4 * sections, 2**24),
+        cost_estimate=cost(12 * count * wide * head * 4 * sections, 2**24),
         compiler_params=pltpu.CompilerParams(vmem_limit_bytes=VMEM_BYTES),
-    )(*tokens, *coefs, *weights)
-    return outs[:chips], outs[chips]
+    )(*tokens, *coefs, *[w for held in chosen for w in held])
+    return outs[:-2], outs[-2], outs[-1]
+
+
+def gradients(built, coefs, order, half, h, head, dtype):
+    chips, rows, lanes = coefs[0].shape
+    some = chips * rows
+    block = min(512, half)
+    taken = [(hs, gs, halves.index(h)) for hs, gs, halves in built if h in halves]
+
+    def kernel(*refs):
+        n = len(taken)
+        h_refs, g_refs, c_refs, out = refs[:n], refs[n : 2 * n], refs[2 * n : -1], refs[-1]
+        start = pl.multiple_of(lax.axis_index("pipe") * 4 * head, 4 * head)
+        own = [c_refs[i][:, :, pl.ds(start, 4 * head)].reshape(some, 4 * head) for i in order]
+        own = jnp.concatenate(own, axis=0)
+        hs = jnp.concatenate([ref[...] for ref in h_refs], axis=0)
+        gs = jnp.concatenate([ref[...] for ref in g_refs], axis=0)
+        out[:, : 3 * head] = dot(hs, own[:, : 3 * head], TN).astype(dtype)
+        out[:, 3 * head :] = dot(gs, own[:, 3 * head :], TN).astype(dtype)
+
+    specs = [
+        pl.BlockSpec((hs.shape[0], block), lambda i, at=at: (0, i + at * (half // block)))
+        for hs, _, at in taken
+    ]
+    return pl.pallas_call(
+        kernel,
+        name="gradients",
+        grid=(half // block,),
+        out_shape=jax.ShapeDtypeStruct((half, 4 * head), dtype),
+        in_specs=specs * 2 + vmem(len(coefs)),
+        out_specs=pl.BlockSpec((block, 4 * head), lambda i: (i, 0)),
+        cost_estimate=cost(2**33, 2**23),
+        compiler_params=pltpu.CompilerParams(vmem_limit_bytes=VMEM_BYTES),
+    )(*[hs for hs, _, _ in taken], *[gs for _, gs, _ in taken], *coefs)
 
 
 def rebuild_wide(tokens, coefs, weights, column, head):
@@ -459,8 +523,8 @@
         )
         result = (g + dot(y, weights[0][:, : 3 * head], NT) - here * h).astype(BF)
         results.append(result.reshape(chips, rows, half))
-    result = jnp.take(jnp.stack(results), jnp.arange(len(tokens)) ^ p, axis=0)
-    return [result[:, k] for k in range(chips)], grads
+    result = jnp.stack(results, axis=1)
+    return jnp.take(result, jnp.arange(chips) ^ z, axis=0), grads
 
 
 def shards(inputs, segments, cotangent, w_query, w_key, w_value, w_out):
@@ -500,12 +564,14 @@
         low, high = after((low, high), *early)
         ours.append(jnp.concatenate([low, high], axis=0))
         theirs.append(hop(ours[3], "dp", 1))
-        late = project(tokens, [mine, ours[3]], [near, theirs[3]], (3,), head, True)
+        late = project(tokens, [mine, ours[3]], [near, theirs[3]], (3,), head, False)
         spread = sides(after(tokens, ours[3]))
-        spread = [tokens, *spread, jnp.concatenate(corner(*after(spread, late[0])), axis=0)]
         early = summed((0, 1, 2), [across(early[0], chips)])
-        late = [late[0]] + [hop(late[k], "dp", k * CORES) for k in range(1, chips)]
-        rounds = [early, summed((3,), late)]
+        late = across(after(late[0], early[1]), chips)
+        late = summed((3,), [after(late, early[2][0])])
+        rounds = [early, late]
+        plane = [pair[0] for pair in early[2]]
+        spread = [tokens, *spread, jnp.concatenate(corner(*after(spread, plane)), axis=0)]
     else:
         ours = fan(mine)
         theirs = [hop(w, "dp", 1) for w in ours]
@@ -515,26 +581,50 @@
         rounds = [summed(wanted, [across(part[0], chips)])]
 
     docs = segments.reshape(sections, 1, rows)
-    squares, *spread = lax.optimization_barrier((squares, *spread))
     coef = chain(rounds, squares, docs, head, width, seq)
     coef = jnp.stack([coef] + [hop(coef, "dp", k * CORES) for k in range(1, chips)])
-    coefs = fan(coef)
 
     half = mine.shape[0]
-    form = rebuild if sections * chips * rows <= 1024 else rebuild_wide
-    far, far_grads = form(spread, coefs, theirs, half, head)
-    close, grads = form(spread, coefs, ours, 0, head)
-    grads = grads + hop(far_grads, "dp", 1)
+    if sections == 4:
+        sent, built, raw = [], [], []
+
+        def task(groups, halves, apart, before=(), between=()):
+            token, scale = [spread[i] for i in groups], [coefs[i] for i in groups]
+            token, scale = after((token, scale), *before)
+            part, hs, gs = rebuild(token, scale, (ours, theirs), halves, head, apart)
+            built.append((hs, gs, halves))
+            raw.append(part)
+            part = after(part, *between)
+            if apart:
+                part = [part[0]] + [hop(part[k], "dp", k * CORES) for k in range(1, chips)]
+            else:
+                part = [across(part[0], chips)]
+            sent.append((part, groups, halves))
+
+        coefs = [coef]
+        task((0,), (0, 1), False)
+        coefs += sides(after(coef, spread[3]))
+        task((1, 2), (1,), True)
+        task((1, 2), (0,), False, before=sent[0][0])
+        coefs.append(jnp.concatenate(corner(*coefs[1:]), axis=0))
+        task((3,), (0, 1), True, before=(sent[1][0], raw[2]), between=sent[1][0])
+        halves_of = [halves for _, _, halves in built]
+        token = hop(raw[3][0][:1, :8, :head], "dp", 1)
+        arrays = after([pair[:2] for pair in built], sent[2][0], token)
+        built = [(*pair, halves) for pair, halves in zip(arrays, halves_of)]
+        far_grads = gradients(built, coefs, range(4), half, 1, head, BF)
+        grads = gradients(built, coefs, range(4), half, 0, head, F32)
+    else:
+        coefs = fan(coef)
+        far, far_grads = rebuild_wide(spread, coefs, theirs, half, head)
+        close, grads = rebuild_wide(spread, coefs, ours, 0, head)
+        order = tuple(range(sections))
+        sent = [([across(far, chips)], order, (1,)), ([across(close, chips)], order, (0,))]
+    grads = grads + hop(far_grads, "dp", 1).astype(F32)
     grads = [grads[None, :, i * head : (i + 1) * head] for i in range(4)]
-    def sent(pieces):
-        pieces = [part.reshape(sections * rows, half) for part in pieces]
-        return [pieces[0]] + [hop(pieces[k], "dp", k * CORES) for k in range(1, chips)]
-
-    far = sent(far)
-    close = sent(after(close, far))
-    out = [part for pair in zip(close, far) for part in pair]
-    out, grads = lax.optimization_barrier((out, grads))
-    stored = unpack(out, chips, width)[: batches * seq]
+    arrays, grads = lax.optimization_barrier(([part for part, _, _ in sent], grads))
+    sent = [(part, groups, halves) for part, (_, groups, halves) in zip(arrays, sent)]
+    stored = unpack(sent, width)[: batches * seq]
     return (stored.reshape(1, 1, batches, seq, width), *grads)
 
 

time: 222 us -> 202 us (0.910)
  waiting for transfers between devices: 103 us -> 61.1 us
  Pallas kernels: 47.5 us -> 65.8 us
  local copies, waits for them, and re-layouts: 9.56 us -> 15 us
  other arithmetic: 5.16 us -> 2.18 us
    ppermute x43 -> x40, waiting for transfers between devices: 103 us -> 45 us  [hop(): lax.ppermute(block, axis, [(i, i ^ step) for i in range(lax.axis_size(axi...]
    pallas_call x3 -> x7, Pallas kernels: 27.2 us -> 45.8 us  [the longest x4 33.9 us: rebuild(): pl.pallas_call(kernel, name='rebuild', grid=(wide // block,), out_shape=[...]
    all_to_all x2 -> x5, waiting for transfers between devices: 0.01 us -> 16.1 us  [across(): lax.all_to_all(block, 'dp', 0, 0, axis_index_groups=groups, tiled=True)]
    all_to_all x2 -> x5, starting transfers between devices: 10.4 us -> 21.5 us  [across(): lax.all_to_all(block, 'dp', 0, 0, axis_index_groups=groups, tiled=True)]
    ppermute x43 -> x40, starting transfers between devices: 43.8 us -> 34 us  [hop(): lax.ppermute(block, axis, [(i, i ^ step) for i in range(lax.axis_size(axi...]
    slice x6, local copies, waits for them, and re-layouts: 2.27 us -> 6.8 us  [corner(): return (hop(one[:cut], 'pipe', 2), hop(two[cut:], 'pipe', 1))]
    unnamed x84 -> x85, local copies, waits for them, and re-layouts: 5.04 us -> 6.73 us
  transfers between devices with their start and end apart: 45 -> 45, of which waited for: 20 -> 16; matrix products, arithmetic and copies ran while one was open for 4% -> 5% of each run, Pallas kernels for 10% -> 28%
where the time goes in v3:
time: 202 us; the launch traced here: 201 us
  Pallas kernels  65.8 us (33%)
  waiting for transfers between devices  61.1 us (30%)
  starting transfers between devices  55.5 us (27%)
  local copies, waits for them, and re-layouts  15 us (7%)
  other arithmetic  2.18 us (1%)
    ppermute x40, waiting for transfers between devices, hop(): lax.ppermute(block, axis, [(i, i ^ step) for i in range(lax.axis_size(axi...  45 us
    ppermute x40, starting transfers between devices, hop(): lax.ppermute(block, axis, [(i, i ^ step) for i in range(lax.axis_size(axi...  34 us
    pallas_call x4, Pallas kernels, rebuild(): pl.pallas_call(kernel, name='rebuild', grid=(wide // block,), out_shape=[...  33.9 us
    all_to_all x5, starting transfers between devices, across(): lax.all_to_all(block, 'dp', 0, 0, axis_index_groups=groups, tiled=True)  21.5 us
    all_to_all x5, waiting for transfers between devices, across(): lax.all_to_all(block, 'dp', 0, 0, axis_index_groups=groups, tiled=True)  16.1 us
    pallas_call x2, Pallas kernels, project(): pl.pallas_call(kernel, name='project', out_shape=[jax.ShapeDtypeStruct((b...  10.4 us
    pallas_call x2, Pallas kernels, gradients(): pl.pallas_call(kernel, name='gradients', grid=(half // block,), out_shape...  8.75 us
    pallas_call x1, Pallas kernels, chain(): pl.pallas_call(kernel, name='chain', out_shape=jax.ShapeDtypeStruct((rows...  7.2 us
  transfers between devices with their start and end apart: 45, of which 16 were waited for; matrix products, arithmetic and copies ran while one was open for 5% of the time, Pallas kernels for 28%

profile of v3, /device:TPU:0, one launch (start us, length us, event | category | flops | bytes accessed | tf_op | source)
XLA Modules:
  0.0 201.0 jit_solution(11229892675427409727)
XLA Ops:
  0.7 2.4 %pack.1 = (bf16[4,2,1,32,2048]{4,3,2,1,0:T(8,128)(2,1)}, f32[32,1]{1,0:T(8,128)}) custom-call(bf16[1,4,32,8192]{3,2,1,0:T(8,128)(2,1)} %x_ref.1, bf16[1,4,32,8192]{3,2,1,0:T(8,128)(2,1)} %g_ref.1), custom_call_target="tpu_custom_call" | custom-call | bytes 4194304 | tf_op jit(solution)/shard_map/pack/pallas_call | solution.py:100
  3.3 6.3 %all-to-all-start = ((bf16[4,2,32,2048]{3,2,1,0:T(8,128)(2,1)}), bf16[4,2,32,2048]{3,2,1,0:T(8,128)(2,1)S(1)}, u32[]{:S(2)}, u32[]{:S(2)}) async-start(bf16[4,2,32,2048]{3,2,1,0:T(8,128)(2,1)} %bitcast), calls=%async_computation | async-start | bytes 2097152 | tf_op jit(solution)/shard_map/all_to_all | solution.py:46
  9.6 1.5 collective-permute-start
  11.1 1.5 collective-permute-start.1
  12.6 21.7 %collective-permute-done.refs_2_.refs_3_.refs_5_ = bf16[1024,512]{1,0:T(8,128)(2,1)} collective-permute-done((bf16[1024,512]{1,0:T(8,128)(2,1)S(1)}, bf16[1024,512]{1,0:T(8,128)(2,1)}, u32[]{:S(2)}, u32[]{:S(2)}) %collective-permute-start) | collective-permute-done | bytes 1048608 | tf_op jit(solution)/shard_map/ppermute | solution.py:24
  34.3 1.2 collective-permute-done.1.refs_3_.refs_4_.refs_6_
  36.1 1.9 slice.50
  37.9 1.5 collective-permute-start.12
  39.5 1.9 slice.51
  41.3 1.3 collective-permute-start.13
  44.6 6.3 %project.2 = bf16[4,27,32,128]{3,2,1,0:T(8,128)(2,1)} custom-call(bf16[4,2,32,2048]{3,2,1,0:T(8,128)(2,1)} %copy-done.4, bf16[1024,512]{1,0:T(8,128)(2,1)} %copy-done.3, bf16[1024,512]{1,0:T(8,128)(2,1)} %collective-permute-done.refs_2_.refs_3_.refs_5_, bf16[1024,512]{1,0:T(8,128)(2,1)} %collective-permute-done.1.refs_3_.refs_4_.refs_6_, ...), custom_call_target="tpu_custom_call" | custom-call | flops 6442450944 | bytes 12582912 | tf_op jit(solution)/shard_map/project/pallas_call | solution.py:204
  50.8 4.2 %all-to-all-start.1 = ((bf16[4,27,32,128]{3,2,1,0:T(8,128)(2,1)}), bf16[4,27,32,128]{3,2,1,0:T(8,128)(2,1)S(1)}, u32[]{:S(2)}, u32[]{:S(2)}) async-start(bf16[4,27,32,128]{3,2,1,0:T(8,128)(2,1)} %project.2), calls=%async_computation.1 | async-start | bytes 1769472 | tf_op jit(solution)/shard_map/all_to_all | solution.py:46
  55.3 1.5 collective-permute-start.25
  58.0 1.1 copy-done.29
  59.1 4.1 %project.3 = bf16[4,9,32,128]{3,2,1,0:T(8,128)(2,1)} custom-call(bf16[4,2,32,2048]{3,2,1,0:T(8,128)(2,1)} %copy-done.4, bf16[1024,512]{1,0:T(8,128)(2,1)} %copy-done.3, bf16[1024,512]{1,0:T(8,128)(2,1)} %copy-done.10, bf16[1024,512]{1,0:T(8,128)(2,1)} %collective-permute-done.2.refs_4_.refs_3_.refs_6_, bf16[1024,512]{1,0:T(8,128)(2,1)} %copy-done.29), custom_call_target="tpu_custom_call" | custom-call | flops 2147483648 | bytes 8388608 | tf_op jit(solution)/shard_map/project/pallas_call | solution.py:204
  63.2 13.7 %all-to-all-done.1.refs_2_ = bf16[4,27,32,128]{3,2,1,0:T(8,128)(2,1)S(1)} async-done(((bf16[4,27,32,128]{3,2,1,0:T(8,128)(2,1)}), bf16[4,27,32,128]{3,2,1,0:T(8,128)(2,1)S(1)}, u32[]{:S(2)}, u32[]{:S(2)}) %all-to-all-start.1) | async-done | bytes 884768 | tf_op jit(solution)/shard_map/all_to_all | solution.py:46
  76.9 3.6 %all-to-all-start.2 = ((bf16[4,9,32,128]{3,2,1,0:T(8,128)(2,1)}), bf16[4,9,32,128]{3,2,1,0:T(8,128)(2,1)S(1)}, u32[]{:S(2)}, u32[]{:S(2)}) async-start(bf16[4,9,32,128]{3,2,1,0:T(8,128)(2,1)} %project.3), calls=%async_computation.2 | async-start | bytes 589824 | tf_op jit(solution)/shard_map/all_to_all | solution.py:46
  80.7 1.6 collective-permute-start.6
  82.8 1.5 collective-permute-start.10
  84.3 1.8 collective-permute-done.6.refs_5_
  86.1 3.3 %collective-permute-done.8.refs_7_ = bf16[3,128,128]{2,1,0:T(8,128)(2,1)} collective-permute-done((bf16[3,128,128]{2,1,0:T(8,128)(2,1)S(1)}, bf16[3,128,128]{2,1,0:T(8,128)(2,1)}, u32[]{:S(2)}, u32[]{:S(2)}) %collective-permute-start.8) | collective-permute-done | bytes 98336 | tf_op jit(solution)/shard_map/ppermute | solution.py:24
  89.9 1.1 collective-permute-start.16
  91.6 1.9 collective-permute-start.20
  94.0 1.3 collective-permute-done.18.refs_16_
  95.3 1.1 collective-permute-done.20.refs_18_
  96.4 1.1 slice.42
  97.5 1.6 collective-permute-start.27
  100.7 7.2 %chain.1 = bf16[32,2176]{1,0:T(8,128)(2,1)} custom-call(f32[32,1]{1,0:T(8,128)} %get-tuple-element.81.refs_0_, s32[4,1,32]{2,1,0:T(1,128)} %bitcast.42, bf16[4,27,32,128]{3,2,1,0:T(8,128)(2,1)} %copy-done.2, bf16[3,128,128]{2,1,0:T(8,128)(2,1)} %bitcast.36, bf16[3,128,128]{2,1,0:T(8,128)(2,1)} %copy-done.33, ...), custom_call_target="tpu_custom_call" | custom-call | flops 8589934592 | bytes 4194304 | tf_op jit(solution)/shard_map/chain/pallas_call | solution.py:318
  108.0 3.7 %collective-permute-start.24 = (bf16[32,2176]{1,0:T(8,128)(2,1)}, bf16[32,2176]{1,0:T(8,128)(2,1)S(1)}, u32[]{:S(2)}, u32[]{:S(2)}) collective-permute-start(bf16[32,2176]{1,0:T(8,128)(2,1)} %chain.1), channel_id=1, source_target_pairs={{0,6},{1,7},{2,4},{3,5},{4,2},{5,3},{6,0},{7,1},{8,14},{9,15},{10,... | collective-permute-start | bytes 417800 | tf_op jit(solution)/shard_map/ppermute | solution.py:24
  113.2 3.5 %collective-permute-done.24 = bf16[32,2176]{1,0:T(8,128)(2,1)S(1)} collective-permute-done((bf16[32,2176]{1,0:T(8,128)(2,1)}, bf16[32,2176]{1,0:T(8,128)(2,1)S(1)}, u32[]{:S(2)}, u32[]{:S(2)}) %collective-permute-start.24) | collective-permute-done | bytes 139296 | tf_op jit(solution)/shard_map/ppermute | solution.py:24
  116.7 7.3 %collective-permute-done.23 = bf16[32,2176]{1,0:T(8,128)(2,1)S(1)} collective-permute-done((bf16[32,2176]{1,0:T(8,128)(2,1)}, bf16[32,2176]{1,0:T(8,128)(2,1)S(1)}, u32[]{:S(2)}, u32[]{:S(2)}) %collective-permute-start.23) | collective-permute-done | bytes 139296 | tf_op jit(solution)/shard_map/ppermute | solution.py:24
  125.4 9.8 %rebuild.4 = (bf16[4,1,32,2048]{3,2,1,0:T(8,128)(2,1)}, bf16[128,2048]{1,0:T(8,128)(2,1)}, bf16[128,2048]{1,0:T(8,128)(2,1)}) custom-call(bf16[4,2,32,2048]{3,2,1,0:T(8,128)(2,1)} %copy-done.4, bf16[4,32,2176]{2,1,0:T(8,128)(2,1)} %copy-done.7, bf16[1024,512]{1,0:T(8,128)(2,1)} %copy-done.3, bf16[1024,512]{1,0:T(8,128)(2,1)} %collective-permute-done.refs_2_.refs_3_.refs_5_, ...), custom_call_target="tpu_custom_call" | custom-call | flops 6442450944 | bytes 16777216 | tf_op jit(solution)/shard_map/rebuild/pallas_call | solution.py:426
  135.2 3.6 %all-to-all-start.3 = ((bf16[4,1,32,2048]{3,2,1,0:T(8,128)(2,1)}), bf16[4,1,32,2048]{3,2,1,0:T(8,128)(2,1)S(1)}, u32[]{:S(2)}, u32[]{:S(2)}) async-start(bf16[4,1,32,2048]{3,2,1,0:T(8,128)(2,1)} %get-tuple-element.91), calls=%async_computation.3 | async-start | bytes 1048576 | tf_op jit(solution)/shard_map/all_to_all | solution.py:46
  140.4 6.9 %rebuild.5 = (bf16[2,32,1024]{2,1,0:T(8,128)(2,1)}, bf16[2,32,1024]{2,1,0:T(8,128)(2,1)}, bf16[2,32,1024]{2,1,0:T(8,128)(2,1)}, bf16[2,32,1024]{2,1,0:T(8,128)(2...) custom-call(bf16[4,2,32,2048]{3,2,1,0:T(8,128)(2,1)} %copy-done.8, ...), custom_call_target="tpu_custom_call" | custom-call | flops 6442450944 | bytes 16777216 | tf_op jit(solution)/shard_map/rebuild/pallas_call | solution.py:426
  147.3 2.1 %collective-permute-start.31 = (bf16[2,32,1024]{2,1,0:T(8,128)(2,1)}, bf16[2,32,1024]{2,1,0:T(8,128)(2,1)S(1)}, u32[]{:S(2)}, u32[]{:S(2)}) collective-permute-start(bf16[2,32,1024]{2,1,0:T(8,128)(2,1)} %get-tuple-element.105), channel_id=1, source_target_pairs={{0,2},{1,3},{2,0},{3,1},{4,6},{5,7},{6,4},{7,5},{8,10},{9,11},{10,... | collective-permute-start | bytes 393224 | tf_op jit(solution)/shard_map/ppermute | solution.py:24
  149.4 2.4 %collective-permute-start.32 = (bf16[2,32,1024]{2,1,0:T(8,128)(2,1)}, bf16[2,32,1024]{2,1,0:T(8,128)(2,1)S(1)}, u32[]{:S(2)}, u32[]{:S(2)}) collective-permute-start(bf16[2,32,1024]{2,1,0:T(8,128)(2,1)} %get-tuple-element.106), channel_id=1, source_target_pairs={{0,4},{1,5},{2,6},{3,7},{4,0},{5,1},{6,2},{7,3},{8,12},{9,13},{10,... | collective-permute-start | bytes 393224 | tf_op jit(solution)/shard_map/ppermute | solution.py:24
  154.3 1.4 all-to-all-done.3.refs_0_
  155.7 7.1 %rebuild.6 = (bf16[4,2,32,1024]{3,2,1,0:T(8,128)(2,1)}, bf16[256,1024]{1,0:T(8,128)(2,1)}, bf16[256,1024]{1,0:T(8,128)(2,1)}) custom-call(bf16[4,2,32,2048]{3,2,1,0:T(8,128)(2,1)} %copy-done.8, bf16[4,2,32,2048]{3,2,1,0:T(8,128)(2,1)} %collective-permute-done.26.refs_1_, bf16[4,32,2176]{2,1,0:T(8,128)(2,1)} %copy-done.16, bf16[4,32,2176]{2,1,0:T(8,128)(2,1)} %copy-done.17, ...), custom_call_target="tpu_custom_call" | custom-call | flops 6442450944 | bytes 16777216 | tf_op jit(solution)/shard_map/rebuild/pallas_call | solution.py:426
  162.8 3.7 %all-to-all-start.4 = ((bf16[4,2,32,1024]{3,2,1,0:T(8,128)(2,1)}), bf16[4,2,32,1024]{3,2,1,0:T(8,128)(2,1)S(1)}, u32[]{:S(2)}, u32[]{:S(2)}) async-start(bf16[4,2,32,1024]{3,2,1,0:T(8,128)(2,1)} %get-tuple-element.112), calls=%async_computation.4 | async-start | bytes 1048576 | tf_op jit(solution)/shard_map/all_to_all | solution.py:46
  167.4 10.0 %rebuild.7 = (bf16[1,32,2048]{2,1,0:T(8,128)(2,1)}, bf16[1,32,2048]{2,1,0:T(8,128)(2,1)}, bf16[1,32,2048]{2,1,0:T(8,128)(2,1)}, bf16[1,32,2048]{2,1,0:T(8,128)(2...) custom-call(bf16[4,2,32,2048]{3,2,1,0:T(8,128)(2,1)} %copy-done.9, bf16[4,32,2176]{2,1,0:T(8,128)(2,1)} %copy-done.18, ...), custom_call_target="tpu_custom_call" | custom-call | flops 6442450944 | bytes 16777216 | tf_op jit(solution)/shard_map/rebuild/pallas_call | solution.py:426
  178.5 4.4 %gradients.3 = bf16[1024,512]{1,0:T(8,128)(2,1)} custom-call(bf16[128,2048]{1,0:T(8,128)(2,1)} %get-tuple-element.131.refs_0_, bf16[256,1024]{1,0:T(8,128)(2,1)} %get-tuple-element.137.refs_1_, bf16[128,2048]{1,0:T(8,128)(2,1)} %get-tuple-element.133.refs_2_, bf16[128,2048]{1,0:T(8,128)(2,1)} %get-tuple-element.134.refs_3_, ...), custom_call_target="tpu_custom_call" | custom-call | flops 8589934592 | bytes 8388608 | tf_op jit(solution)/shard_map/gradients/pallas_call | solution.py:475
  183.0 1.2 collective-permute-start.36
  184.1 2.4 %collective-permute-start.37 = (bf16[1,32,2048]{2,1,0:T(8,128)(2,1)S(1)}, bf16[1,32,2048]{2,1,0:T(8,128)(2,1)S(1)}, u32[]{:S(2)}, u32[]{:S(2)}) collective-permute-start(bf16[1,32,2048]{2,1,0:T(8,128)(2,1)S(1)} %copy-done.31), channel_id=1, source_target_pairs={{0,4},{1,5},{2,6},{3,7},{4,0},{5,1},{6,2},{7,3},{8,12},{9,13},{10,... | collective-permute-start | bytes 393224 | tf_op jit(solution)/shard_map/ppermute | solution.py:24
  187.4 4.3 %gradients.2 = f32[1024,512]{1,0:T(8,128)} custom-call(bf16[128,2048]{1,0:T(8,128)(2,1)} %get-tuple-element.131.refs_0_, bf16[256,1024]{1,0:T(8,128)(2,1)} %get-tuple-element.132.refs_1_, bf16[128,2048]{1,0:T(8,128)(2,1)} %get-tuple-element.133.refs_2_, bf16[128,2048]{1,0:T(8,128)(2,1)} %get-tuple-element.134.refs_3_, ...), custom_call_target="tpu_custom_call" | custom-call | flops 8589934592 | bytes 8388608 | tf_op jit(solution)/shard_map/gradients/pallas_call | solution.py:475
  191.8 1.9 convert_add_fusion
  193.7 1.4 slice_bitcast_fusion
  195.1 2.0 collective-permute-done.37.refs_8_
  197.8 3.1 %unpack.1 = bf16[128,8192]{1,0:T(8,128)(2,1)} custom-call(bf16[4,1,32,2048]{3,2,1,0:T(8,128)(2,1)} %copy-done, bf16[2,32,1024]{2,1,0:T(8,128)(2,1)} %get-tuple-element.140.refs_1_, bf16[2,32,1024]{2,1,0:T(8,128)(2,1)} %copy-done.19, bf16[2,32,1024]{2,1,0:T(8,128)(2,1)} %copy-done.20, bf16[2,32,1024]{2,1,0:T(8,128)(2,1)} %copy-done.21, ...), custom_call_target="tpu_custom_call" | custom-call | bytes 8388608 | tf_op jit(solution)/shard_map/unpack/pallas_call | solution.py:145
  (153 shorter events, 18.4 us)
Async XLA Ops:
  3.3 38.1 %copy-start.3 = (bf16[1024,512]{1,0:T(8,128)(2,1)}, bf16[1024,512]{1,0:T(8,128)(2,1)S(1)}, u32[]{:S(2)}) copy-start(bf16[1024,512]{1,0:T(8,128)(2,1)S(1)} %pad_maximum_fusion.refs_1_.refs_2_.refs_4_) | copy-start | bytes 3145732
  3.3 32.3 %all-to-all-start = ((bf16[4,2,32,2048]{3,2,1,0:T(8,128)(2,1)}), bf16[4,2,32,2048]{3,2,1,0:T(8,128)(2,1)S(1)}, u32[]{:S(2)}, u32[]{:S(2)}) async-start(bf16[4,2,32,2048]{3,2,1,0:T(8,128)(2,1)} %bitcast), calls=%async_computation | async-start | bytes 2097152 | tf_op jit(solution)/shard_map/all_to_all | solution.py:46
  9.6 24.7 %collective-permute-start = (bf16[1024,512]{1,0:T(8,128)(2,1)S(1)}, bf16[1024,512]{1,0:T(8,128)(2,1)}, u32[]{:S(2)}, u32[]{:S(2)}) collective-permute-start(bf16[1024,512]{1,0:T(8,128)(2,1)S(1)} %pad_maximum_fusion.refs_1_.refs_2_.refs_4_), channel_id=1, source_target_pairs={{0,8},{8,0},{16,24},{24,16},{1,9},{9,1},{17,25},{25,17},{2,10},{10... | collective-permute-start | bytes 3145736 | tf_op jit(solution)/shard_map/ppermute | solution.py:24
  11.1 24.4 %collective-permute-start.1 = (bf16[1024,512]{1,0:T(8,128)(2,1)S(1)}, bf16[1024,512]{1,0:T(8,128)(2,1)}, u32[]{:S(2)}, u32[]{:S(2)}) collective-permute-start(bf16[1024,512]{1,0:T(8,128)(2,1)S(1)} %pad_maximum_fusion.refs_1_.refs_2_.refs_4_), channel_id=1, source_target_pairs={{0,16},{8,24},{16,0},{24,8},{1,17},{9,25},{17,1},{25,9},{2,18},{10... | collective-permute-start | bytes 3145736 | tf_op jit(solution)/shard_map/ppermute | solution.py:24
  12.6 30.0 %collective-permute-start.2 = (bf16[1024,512]{1,0:T(8,128)(2,1)S(1)}, bf16[1024,512]{1,0:T(8,128)(2,1)}, u32[]{:S(2)}, u32[]{:S(2)}) collective-permute-start(bf16[1024,512]{1,0:T(8,128)(2,1)S(1)} %pad_maximum_fusion.refs_1_.refs_2_.refs_4_), channel_id=1, source_target_pairs={{0,1},{1,0},{2,3},{3,2},{4,5},{5,4},{6,7},{7,6},{8,9},{9,8},{10,11... | collective-permute-start | bytes 3145736 | tf_op jit(solution)/shard_map/ppermute | solution.py:24
  35.6 7.1 %collective-permute-start.3 = (bf16[1024,512]{1,0:T(8,128)(2,1)}, bf16[1024,512]{1,0:T(8,128)(2,1)S(1)}, u32[]{:S(2)}, u32[]{:S(2)}) collective-permute-start(bf16[1024,512]{1,0:T(8,128)(2,1)} %collective-permute-done.refs_2_.refs_3_.refs_5_), channel_id=1, source_target_pairs={{0,1},{1,0},{2,3},{3,2},{4,5},{5,4},{6,7},{7,6},{8,9},{9,8},{10,11... | collective-permute-start | bytes 3145736 | tf_op jit(solution)/shard_map/ppermute | solution.py:24
  35.6 7.1 %collective-permute-start.4 = (bf16[1024,512]{1,0:T(8,128)(2,1)}, bf16[1024,512]{1,0:T(8,128)(2,1)S(1)}, u32[]{:S(2)}, u32[]{:S(2)}) collective-permute-start(bf16[1024,512]{1,0:T(8,128)(2,1)} %collective-permute-done.1.refs_3_.refs_4_.refs_6_), channel_id=1, source_target_pairs={{0,1},{1,0},{2,3},{3,2},{4,5},{5,4},{6,7},{7,6},{8,9},{9,8},{10,11... | collective-permute-start | bytes 3145736 | tf_op jit(solution)/shard_map/ppermute | solution.py:24
  37.9 17.1 %collective-permute-start.12 = (bf16[512,512]{1,0:T(8,128)(2,1)}, bf16[512,512]{1,0:T(8,128)(2,1)S(1)}, u32[]{:S(2)}, u32[]{:S(2)}) collective-permute-start(bf16[512,512]{1,0:T(8,128)(2,1)} %slice.50), channel_id=1, source_target_pairs={{0,16},{8,24},{16,0},{24,8},{1,17},{9,25},{17,1},{25,9},{2,18},{10... | collective-permute-start | bytes 1572872 | tf_op jit(solution)/shard_map/ppermute | solution.py:24
  41.3 13.8 %collective-permute-start.13 = (bf16[512,512]{1,0:T(8,128)(2,1)}, bf16[512,512]{1,0:T(8,128)(2,1)S(1)}, u32[]{:S(2)}, u32[]{:S(2)}) collective-permute-start(bf16[512,512]{1,0:T(8,128)(2,1)} %slice.51), channel_id=1, source_target_pairs={{0,8},{8,0},{16,24},{24,16},{1,9},{9,1},{17,25},{25,17},{2,10},{10... | collective-permute-start | bytes 1572872 | tf_op jit(solution)/shard_map/ppermute | solution.py:24
  50.8 26.1 %all-to-all-start.1 = ((bf16[4,27,32,128]{3,2,1,0:T(8,128)(2,1)}), bf16[4,27,32,128]{3,2,1,0:T(8,128)(2,1)S(1)}, u32[]{:S(2)}, u32[]{:S(2)}) async-start(bf16[4,27,32,128]{3,2,1,0:T(8,128)(2,1)} %project.2), calls=%async_computation.1 | async-start | bytes 1769472 | tf_op jit(solution)/shard_map/all_to_all | solution.py:46
  55.3 2.7 %collective-permute-start.14 = (bf16[1024,512]{1,0:T(8,128)(2,1)S(1)}, bf16[1024,512]{1,0:T(8,128)(2,1)S(1)}, u32[]{:S(2)}, u32[]{:S(2)}) collective-permute-start(bf16[1024,512]{1,0:T(8,128)(2,1)S(1)} %constant_dynamic-update-slice_fusion.refs_2_.refs_5_.refs_7_), channel_id=1, source_target_pairs={{0,1},{1,0},{2,3},{3,2},{4,5},{5,4},{6,7},{7,6},{8,9},{9,8},{10,11... | collective-permute-start | bytes 3145736 | tf_op jit(solution)/shard_map/ppermute | solution.py:24
  55.3 34.6 %collective-permute-start.25 = (bf16[4,2,32,2048]{3,2,1,0:T(8,128)(2,1)S(1)}, bf16[4,2,32,2048]{3,2,1,0:T(8,128)(2,1)S(1)}, u32[]{:S(2)}, u32[]{:S(2)}) collective-permute-start(bf16[4,2,32,2048]{3,2,1,0:T(8,128)(2,1)S(1)} %copy-done.5), channel_id=1, source_target_pairs={{0,8},{8,0},{16,24},{24,16},{1,9},{9,1},{17,25},{25,17},{2,10},{10... | collective-permute-start | bytes 3145736 | tf_op jit(solution)/shard_map/ppermute | solution.py:24
  56.8 34.2 %collective-permute-start.26 = (bf16[4,2,32,2048]{3,2,1,0:T(8,128)(2,1)S(1)}, bf16[4,2,32,2048]{3,2,1,0:T(8,128)(2,1)}, u32[]{:S(2)}, u32[]{:S(2)}) collective-permute-start(bf16[4,2,32,2048]{3,2,1,0:T(8,128)(2,1)S(1)} %copy-done.5), channel_id=1, source_target_pairs={{0,16},{8,24},{16,0},{24,8},{1,17},{9,25},{17,1},{25,9},{2,18},{10... | collective-permute-start | bytes 3145736 | tf_op jit(solution)/shard_map/ppermute | solution.py:24
  76.9 23.2 %copy-start.2 = (bf16[4,27,32,128]{3,2,1,0:T(8,128)(2,1)}, bf16[4,27,32,128]{3,2,1,0:T(8,128)(2,1)S(1)}, u32[]{:S(2)}) copy-start(bf16[4,27,32,128]{3,2,1,0:T(8,128)(2,1)S(1)} %all-to-all-done.1.refs_2_) | copy-start | bytes 2654212
  76.9 12.9 %all-to-all-start.2 = ((bf16[4,9,32,128]{3,2,1,0:T(8,128)(2,1)}), bf16[4,9,32,128]{3,2,1,0:T(8,128)(2,1)S(1)}, u32[]{:S(2)}, u32[]{:S(2)}) async-start(bf16[4,9,32,128]{3,2,1,0:T(8,128)(2,1)} %project.3), calls=%async_computation.2 | async-start | bytes 589824 | tf_op jit(solution)/shard_map/all_to_all | solution.py:46
  80.7 2.2 %collective-permute-start.5 = (bf16[3,128,128]{2,1,0:T(8,128)(2,1)S(1)}, bf16[3,128,128]{2,1,0:T(8,128)(2,1)S(1)}, u32[]{:S(2)}, u32[]{:S(2)}) collective-permute-start(bf16[3,128,128]{2,1,0:T(8,128)(2,1)S(1)} %bitcast.32), channel_id=1, source_target_pairs={{0,1},{1,0},{2,3},{3,2},{4,5},{5,4},{6,7},{7,6},{8,9},{9,8},{10,11... | collective-permute-start | bytes 294920 | tf_op jit(solution)/shard_map/ppermute | solution.py:24
  80.7 5.3 %collective-permute-start.6 = (bf16[3,128,128]{2,1,0:T(8,128)(2,1)S(1)}, bf16[3,128,128]{2,1,0:T(8,128)(2,1)}, u32[]{:S(2)}, u32[]{:S(2)}) collective-permute-start(bf16[3,128,128]{2,1,0:T(8,128)(2,1)S(1)} %bitcast.33), channel_id=1, source_target_pairs={{0,8},{8,0},{16,24},{24,16},{1,9},{9,1},{17,25},{25,17},{2,10},{10... | collective-permute-start | bytes 294920 | tf_op jit(solution)/shard_map/ppermute | solution.py:24
  82.3 7.1 %collective-permute-start.8 = (bf16[3,128,128]{2,1,0:T(8,128)(2,1)S(1)}, bf16[3,128,128]{2,1,0:T(8,128)(2,1)}, u32[]{:S(2)}, u32[]{:S(2)}) collective-permute-start(bf16[3,128,128]{2,1,0:T(8,128)(2,1)S(1)} %bitcast.34), channel_id=1, source_target_pairs={{0,16},{8,24},{16,0},{24,8},{1,17},{9,25},{17,1},{25,9},{2,18},{10... | collective-permute-start | bytes 294920 | tf_op jit(solution)/shard_map/ppermute | solution.py:24
  82.8 6.6 %collective-permute-start.10 = (bf16[3,128,128]{2,1,0:T(8,128)(2,1)S(1)}, bf16[3,128,128]{2,1,0:T(8,128)(2,1)}, u32[]{:S(2)}, u32[]{:S(2)}) collective-permute-start(bf16[3,128,128]{2,1,0:T(8,128)(2,1)S(1)} %bitcast.35), channel_id=1, source_target_pairs={{0,24},{8,16},{16,8},{24,0},{1,25},{9,17},{17,9},{25,1},{2,26},{10... | collective-permute-start | bytes 294920 | tf_op jit(solution)/shard_map/ppermute | solution.py:24
  86.0 5.5 %collective-permute-start.7 = (bf16[3,128,128]{2,1,0:T(8,128)(2,1)}, bf16[3,128,128]{2,1,0:T(8,128)(2,1)}, u32[]{:S(2)}, u32[]{:S(2)}) collective-permute-start(bf16[3,128,128]{2,1,0:T(8,128)(2,1)} %collective-permute-done.6.refs_5_), channel_id=1, source_target_pairs={{0,1},{1,0},{2,3},{3,2},{4,5},{5,4},{6,7},{7,6},{8,9},{9,8},{10,11... | collective-permute-start | bytes 294920 | tf_op jit(solution)/shard_map/ppermute | solution.py:24
  89.4 4.1 %collective-permute-start.9 = (bf16[3,128,128]{2,1,0:T(8,128)(2,1)}, bf16[3,128,128]{2,1,0:T(8,128)(2,1)}, u32[]{:S(2)}, u32[]{:S(2)}) collective-permute-start(bf16[3,128,128]{2,1,0:T(8,128)(2,1)} %collective-permute-done.8.refs_7_), channel_id=1, source_target_pairs={{0,1},{1,0},{2,3},{3,2},{4,5},{5,4},{6,7},{7,6},{8,9},{9,8},{10,11... | collective-permute-start | bytes 294920 | tf_op jit(solution)/shard_map/ppermute | solution.py:24
  89.4 8.2 %collective-permute-start.11 = (bf16[3,128,128]{2,1,0:T(8,128)(2,1)}, bf16[3,128,128]{2,1,0:T(8,128)(2,1)}, u32[]{:S(2)}, u32[]{:S(2)}) collective-permute-start(bf16[3,128,128]{2,1,0:T(8,128)(2,1)} %collective-permute-done.10.refs_9_), channel_id=1, source_target_pairs={{0,1},{1,0},{2,3},{3,2},{4,5},{5,4},{6,7},{7,6},{8,9},{9,8},{10,11... | collective-permute-start | bytes 294920 | tf_op jit(solution)/shard_map/ppermute | solution.py:24
  89.9 4.0 %collective-permute-start.16 = (bf16[1,128,128]{2,1,0:T(8,128)(2,1)S(1)}, bf16[1,128,128]{2,1,0:T(8,128)(2,1)S(1)}, u32[]{:S(2)}, u32[]{:S(2)}) collective-permute-start(bf16[1,128,128]{2,1,0:T(8,128)(2,1)S(1)} %bitcast.37), channel_id=1, source_target_pairs={{0,8},{8,0},{16,24},{24,16},{1,9},{9,1},{17,25},{25,17},{2,10},{10... | collective-permute-start | bytes 98312 | tf_op jit(solution)/shard_map/ppermute | solution.py:24
  91.0 4.3 %collective-permute-start.18 = (bf16[1,128,128]{2,1,0:T(8,128)(2,1)S(1)}, bf16[1,128,128]{2,1,0:T(8,128)(2,1)S(1)}, u32[]{:S(2)}, u32[]{:S(2)}) collective-permute-start(bf16[1,128,128]{2,1,0:T(8,128)(2,1)S(1)} %bitcast.38), channel_id=1, source_target_pairs={{0,16},{8,24},{16,0},{24,8},{1,17},{9,25},{17,1},{25,9},{2,18},{10... | collective-permute-start | bytes 98312 | tf_op jit(solution)/shard_map/ppermute | solution.py:24
  91.6 4.8 %collective-permute-start.20 = (bf16[1,128,128]{2,1,0:T(8,128)(2,1)S(1)}, bf16[1,128,128]{2,1,0:T(8,128)(2,1)S(1)}, u32[]{:S(2)}, u32[]{:S(2)}) collective-permute-start(bf16[1,128,128]{2,1,0:T(8,128)(2,1)S(1)} %bitcast.39), channel_id=1, source_target_pairs={{0,24},{8,16},{16,8},{24,0},{1,25},{9,17},{17,9},{25,1},{2,26},{10... | collective-permute-start | bytes 98312 | tf_op jit(solution)/shard_map/ppermute | solution.py:24
  93.5 5.6 %collective-permute-start.15 = (bf16[1,128,128]{2,1,0:T(8,128)(2,1)S(1)}, bf16[1,128,128]{2,1,0:T(8,128)(2,1)S(1)}, u32[]{:S(2)}, u32[]{:S(2)}) collective-permute-start(bf16[1,128,128]{2,1,0:T(8,128)(2,1)S(1)} %bitcast.40), channel_id=1, source_target_pairs={{0,1},{1,0},{2,3},{3,2},{4,5},{5,4},{6,7},{7,6},{8,9},{9,8},{10,11... | collective-permute-start | bytes 98312 | tf_op jit(solution)/shard_map/ppermute | solution.py:24
  93.9 6.2 %collective-permute-start.17 = (bf16[1,128,128]{2,1,0:T(8,128)(2,1)S(1)}, bf16[1,128,128]{2,1,0:T(8,128)(2,1)S(1)}, u32[]{:S(2)}, u32[]{:S(2)}) collective-permute-start(bf16[1,128,128]{2,1,0:T(8,128)(2,1)S(1)} %collective-permute-done.16.refs_14_), channel_id=1, source_target_pairs={{0,1},{1,0},{2,3},{3,2},{4,5},{5,4},{6,7},{7,6},{8,9},{9,8},{10,11... | collective-permute-start | bytes 98312 | tf_op jit(solution)/shard_map/ppermute | solution.py:24
  95.3 4.8 %collective-permute-start.19 = (bf16[1,128,128]{2,1,0:T(8,128)(2,1)S(1)}, bf16[1,128,128]{2,1,0:T(8,128)(2,1)S(1)}, u32[]{:S(2)}, u32[]{:S(2)}) collective-permute-start(bf16[1,128,128]{2,1,0:T(8,128)(2,1)S(1)} %collective-permute-done.18.refs_16_), channel_id=1, source_target_pairs={{0,1},{1,0},{2,3},{3,2},{4,5},{5,4},{6,7},{7,6},{8,9},{9,8},{10,11... | collective-permute-start | bytes 98312 | tf_op jit(solution)/shard_map/ppermute | solution.py:24
  96.4 3.7 %collective-permute-start.21 = (bf16[1,128,128]{2,1,0:T(8,128)(2,1)S(1)}, bf16[1,128,128]{2,1,0:T(8,128)(2,1)S(1)}, u32[]{:S(2)}, u32[]{:S(2)}) collective-permute-start(bf16[1,128,128]{2,1,0:T(8,128)(2,1)S(1)} %collective-permute-done.20.refs_18_), channel_id=1, source_target_pairs={{0,1},{1,0},{2,3},{3,2},{4,5},{5,4},{6,7},{7,6},{8,9},{9,8},{10,11... | collective-permute-start | bytes 98312 | tf_op jit(solution)/shard_map/ppermute | solution.py:24
  97.5 14.9 %collective-permute-start.27 = (bf16[2,2,32,2048]{3,2,1,0:T(8,128)(2,1)S(1)}, bf16[2,2,32,2048]{3,2,1,0:T(8,128)(2,1)S(1)}, u32[]{:S(2)}, u32[]{:S(2)}) collective-permute-start(bf16[2,2,32,2048]{3,2,1,0:T(8,128)(2,1)S(1)} %slice.41), channel_id=1, source_target_pairs={{0,16},{8,24},{16,0},{24,8},{1,17},{9,25},{17,1},{25,9},{2,18},{10... | collective-permute-start | bytes 1572872 | tf_op jit(solution)/shard_map/ppermute | solution.py:24
  99.1 14.1 %collective-permute-start.28 = (bf16[2,2,32,2048]{3,2,1,0:T(8,128)(2,1)S(1)}, bf16[2,2,32,2048]{3,2,1,0:T(8,128)(2,1)S(1)}, u32[]{:S(2)}, u32[]{:S(2)}) collective-permute-start(bf16[2,2,32,2048]{3,2,1,0:T(8,128)(2,1)S(1)} %slice.42), channel_id=1, source_target_pairs={{0,8},{8,0},{16,24},{24,16},{1,9},{9,1},{17,25},{25,17},{2,10},{10... | collective-permute-start | bytes 1572872 | tf_op jit(solution)/shard_map/ppermute | solution.py:24
  108.0 8.7 %collective-permute-start.24 = (bf16[32,2176]{1,0:T(8,128)(2,1)}, bf16[32,2176]{1,0:T(8,128)(2,1)S(1)}, u32[]{:S(2)}, u32[]{:S(2)}) collective-permute-start(bf16[32,2176]{1,0:T(8,128)(2,1)} %chain.1), channel_id=1, source_target_pairs={{0,6},{1,7},{2,4},{3,5},{4,2},{5,3},{6,0},{7,1},{8,14},{9,15},{10,... | collective-permute-start | bytes 417800 | tf_op jit(solution)/shard_map/ppermute | solution.py:24
  111.6 12.3 %collective-permute-start.23 = (bf16[32,2176]{1,0:T(8,128)(2,1)}, bf16[32,2176]{1,0:T(8,128)(2,1)S(1)}, u32[]{:S(2)}, u32[]{:S(2)}) collective-permute-start(bf16[32,2176]{1,0:T(8,128)(2,1)} %chain.1), channel_id=1, source_target_pairs={{0,4},{1,5},{2,6},{3,7},{4,0},{5,1},{6,2},{7,3},{8,12},{9,13},{10,... | collective-permute-start | bytes 417800 | tf_op jit(solution)/shard_map/ppermute | solution.py:24
  111.6 12.3 %collective-permute-start.22 = (bf16[32,2176]{1,0:T(8,128)(2,1)}, bf16[32,2176]{1,0:T(8,128)(2,1)S(1)}, u32[]{:S(2)}, u32[]{:S(2)}) collective-permute-start(bf16[32,2176]{1,0:T(8,128)(2,1)} %chain.1), channel_id=1, source_target_pairs={{0,2},{1,3},{2,0},{3,1},{4,6},{5,7},{6,4},{7,5},{8,10},{9,11},{10,... | collective-permute-start | bytes 417800 | tf_op jit(solution)/shard_map/ppermute | solution.py:24
  113.2 22.0 %copy-start.9 = (bf16[4,2,32,2048]{3,2,1,0:T(8,128)(2,1)}, bf16[4,2,32,2048]{3,2,1,0:T(8,128)(2,1)S(1)}, u32[]{:S(2)}) copy-start(bf16[4,2,32,2048]{3,2,1,0:T(8,128)(2,1)S(1)} %constant_dynamic-update-slice_fusion.2.refs_0_) | copy-start | bytes 3145732
  124.0 14.8 %collective-permute-start.29 = (bf16[4,32,2176]{2,1,0:T(8,128)(2,1)S(1)}, bf16[4,32,2176]{2,1,0:T(8,128)(2,1)S(1)}, u32[]{:S(2)}, u32[]{:S(2)}) collective-permute-start(bf16[4,32,2176]{2,1,0:T(8,128)(2,1)S(1)} %pad_maximum_fusion.1.refs_1_.refs_6_), channel_id=1, source_target_pairs={{0,8},{8,0},{16,24},{24,16},{1,9},{9,1},{17,25},{25,17},{2,10},{10... | collective-permute-start | bytes 1671176 | tf_op jit(solution)/shard_map/ppermute | solution.py:24
  124.7 14.2 %collective-permute-start.30 = (bf16[4,32,2176]{2,1,0:T(8,128)(2,1)S(1)}, bf16[4,32,2176]{2,1,0:T(8,128)(2,1)S(1)}, u32[]{:S(2)}, u32[]{:S(2)}) collective-permute-start(bf16[4,32,2176]{2,1,0:T(8,128)(2,1)S(1)} %pad_maximum_fusion.1.refs_1_.refs_6_), channel_id=1, source_target_pairs={{0,16},{8,24},{16,0},{24,8},{1,17},{9,25},{17,1},{25,9},{2,18},{10... | collective-permute-start | bytes 1671176 | tf_op jit(solution)/shard_map/ppermute | solution.py:24
  135.2 20.5 %all-to-all-start.3 = ((bf16[4,1,32,2048]{3,2,1,0:T(8,128)(2,1)}), bf16[4,1,32,2048]{3,2,1,0:T(8,128)(2,1)S(1)}, u32[]{:S(2)}, u32[]{:S(2)}) async-start(bf16[4,1,32,2048]{3,2,1,0:T(8,128)(2,1)} %get-tuple-element.91), calls=%async_computation.3 | async-start | bytes 1048576 | tf_op jit(solution)/shard_map/all_to_all | solution.py:46
  147.3 19.3 %collective-permute-start.31 = (bf16[2,32,1024]{2,1,0:T(8,128)(2,1)}, bf16[2,32,1024]{2,1,0:T(8,128)(2,1)S(1)}, u32[]{:S(2)}, u32[]{:S(2)}) collective-permute-start(bf16[2,32,1024]{2,1,0:T(8,128)(2,1)} %get-tuple-element.105), channel_id=1, source_target_pairs={{0,2},{1,3},{2,0},{3,1},{4,6},{5,7},{6,4},{7,5},{8,10},{9,11},{10,... | collective-permute-start | bytes 393224 | tf_op jit(solution)/shard_map/ppermute | solution.py:24
  149.4 17.3 %collective-permute-start.32 = (bf16[2,32,1024]{2,1,0:T(8,128)(2,1)}, bf16[2,32,1024]{2,1,0:T(8,128)(2,1)S(1)}, u32[]{:S(2)}, u32[]{:S(2)}) collective-permute-start(bf16[2,32,1024]{2,1,0:T(8,128)(2,1)} %get-tuple-element.106), channel_id=1, source_target_pairs={{0,4},{1,5},{2,6},{3,7},{4,0},{5,1},{6,2},{7,3},{8,12},{9,13},{10,... | collective-permute-start | bytes 393224 | tf_op jit(solution)/shard_map/ppermute | solution.py:24
  151.8 14.9 %collective-permute-start.33 = (bf16[2,32,1024]{2,1,0:T(8,128)(2,1)}, bf16[2,32,1024]{2,1,0:T(8,128)(2,1)S(1)}, u32[]{:S(2)}, u32[]{:S(2)}) collective-permute-start(bf16[2,32,1024]{2,1,0:T(8,128)(2,1)} %get-tuple-element.107), channel_id=1, source_target_pairs={{0,6},{1,7},{2,4},{3,5},{4,2},{5,3},{6,0},{7,1},{8,14},{9,15},{10,... | collective-permute-start | bytes 393224 | tf_op jit(solution)/shard_map/ppermute | solution.py:24
  152.8 13.7 %collective-permute-start.34 = (bf16[2,32,2176]{2,1,0:T(8,128)(2,1)S(1)}, bf16[2,32,2176]{2,1,0:T(8,128)(2,1)S(1)}, u32[]{:S(2)}, u32[]{:S(2)}) collective-permute-start(bf16[2,32,2176]{2,1,0:T(8,128)(2,1)S(1)} %slice.52), channel_id=1, source_target_pairs={{0,16},{8,24},{16,0},{24,8},{1,17},{9,25},{17,1},{25,9},{2,18},{10... | collective-permute-start | bytes 835592 | tf_op jit(solution)/shard_map/ppermute | solution.py:24
  153.9 12.7 %collective-permute-start.35 = (bf16[2,32,2176]{2,1,0:T(8,128)(2,1)S(1)}, bf16[2,32,2176]{2,1,0:T(8,128)(2,1)S(1)}, u32[]{:S(2)}, u32[]{:S(2)}) collective-permute-start(bf16[2,32,2176]{2,1,0:T(8,128)(2,1)S(1)} %slice.53), channel_id=1, source_target_pairs={{0,8},{8,0},{16,24},{24,16},{1,9},{9,1},{17,25},{25,17},{2,10},{10... | collective-permute-start | bytes 835592 | tf_op jit(solution)/shard_map/ppermute | solution.py:24
  162.8 15.6 %all-to-all-start.4 = ((bf16[4,2,32,1024]{3,2,1,0:T(8,128)(2,1)}), bf16[4,2,32,1024]{3,2,1,0:T(8,128)(2,1)S(1)}, u32[]{:S(2)}, u32[]{:S(2)}) async-start(bf16[4,2,32,1024]{3,2,1,0:T(8,128)(2,1)} %get-tuple-element.112), calls=%async_computation.4 | async-start | bytes 1048576 | tf_op jit(solution)/shard_map/all_to_all | solution.py:46
  182.9 8.9 %collective-permute-start.39 = (bf16[1024,512]{1,0:T(8,128)(2,1)}, bf16[1024,512]{1,0:T(8,128)(2,1)S(1)}, u32[]{:S(2)}, u32[]{:S(2)}) collective-permute-start(bf16[1024,512]{1,0:T(8,128)(2,1)} %gradients.3), channel_id=1, source_target_pairs={{0,1},{1,0},{2,3},{3,2},{4,5},{5,4},{6,7},{7,6},{8,9},{9,8},{10,11... | collective-permute-start | bytes 3145736 | tf_op jit(solution)/shard_map/ppermute | solution.py:24
  183.0 12.1 %collective-permute-start.36 = (bf16[1,32,2048]{2,1,0:T(8,128)(2,1)S(1)}, bf16[1,32,2048]{2,1,0:T(8,128)(2,1)S(1)}, u32[]{:S(2)}, u32[]{:S(2)}) collective-permute-start(bf16[1,32,2048]{2,1,0:T(8,128)(2,1)S(1)} %copy-done.32), channel_id=1, source_target_pairs={{0,2},{1,3},{2,0},{3,1},{4,6},{5,7},{6,4},{7,5},{8,10},{9,11},{10,... | collective-permute-start | bytes 393224 | tf_op jit(solution)/shard_map/ppermute | solution.py:24
  184.1 12.9 %collective-permute-start.37 = (bf16[1,32,2048]{2,1,0:T(8,128)(2,1)S(1)}, bf16[1,32,2048]{2,1,0:T(8,128)(2,1)S(1)}, u32[]{:S(2)}, u32[]{:S(2)}) collective-permute-start(bf16[1,32,2048]{2,1,0:T(8,128)(2,1)S(1)} %copy-done.31), channel_id=1, source_target_pairs={{0,4},{1,5},{2,6},{3,7},{4,0},{5,1},{6,2},{7,3},{8,12},{9,13},{10,... | collective-permute-start | bytes 393224 | tf_op jit(solution)/shard_map/ppermute | solution.py:24
  186.5 10.5 %collective-permute-start.38 = (bf16[1,32,2048]{2,1,0:T(8,128)(2,1)S(1)}, bf16[1,32,2048]{2,1,0:T(8,128)(2,1)S(1)}, u32[]{:S(2)}, u32[]{:S(2)}) collective-permute-start(bf16[1,32,2048]{2,1,0:T(8,128)(2,1)S(1)} %copy-done.30), channel_id=1, source_target_pairs={{0,6},{1,7},{2,4},{3,5},{4,2},{5,3},{6,0},{7,1},{8,14},{9,15},{10,... | collective-permute-start | bytes 393224 | tf_op jit(solution)/shard_map/ppermute | solution.py:24
  (38 other events, 205.3 us)

commit v4 on v3

--- a/solution.py
+++ b/solution.py
@@ -336,7 +336,7 @@
     half = weights[0][0].shape[0]
     some = chips * rows
     count = groups * some
-    block = min(512, half)
+    block = min(1024 if len(halves) > 1 else 512, half)
     steps = half // block
     wide = len(halves) * half
     chosen = [weights[h] for h in halves]
@@ -620,8 +620,11 @@
         close, grads = rebuild_wide(spread, coefs, ours, 0, head)
         order = tuple(range(sections))
         sent = [([across(far, chips)], order, (1,)), ([across(close, chips)], order, (0,))]
-    grads = grads + hop(far_grads, "dp", 1).astype(F32)
-    grads = [grads[None, :, i * head : (i + 1) * head] for i in range(4)]
+    far_grads = hop(far_grads, "dp", 1)
+    grads = [
+        (grads[:, at : at + head] + far_grads[:, at : at + head].astype(F32))[None]
+        for at in range(0, 4 * head, head)
+    ]
     arrays, grads = lax.optimization_barrier(([part for part, _, _ in sent], grads))
     sent = [(part, groups, halves) for part, (_, groups, halves) in zip(arrays, sent)]
     stored = unpack(sent, width)[: batches * seq]

time: 202 us -> 201 us (level)
    broadcast_in_dim x0 -> x1, other arithmetic: none -> 2.92 us  [shards(): (grads[:, at:at + head] + far_grads[:, at:at + head].astype(F32))[None]]
  transfers between devices with their start and end apart: 45 -> 45, of which waited for: 16 -> 16; matrix products, arithmetic and copies ran while one was open for 5% -> 5% of each run, Pallas kernels for 28% -> 27%
where the time goes in v4:
time: 201 us; the launch traced here: 200 us
  Pallas kernels  64.8 us (32%)
  waiting for transfers between devices  61.5 us (31%)
  starting transfers between devices  55.4 us (28%)
  local copies, waits for them, and re-layouts  13.6 us (7%)
  other arithmetic  3.19 us (2%)
    ppermute x40, waiting for transfers between devices, hop(): lax.ppermute(block, axis, [(i, i ^ step) for i in range(lax.axis_size(axi...  44.7 us
    ppermute x40, starting transfers between devices, hop(): lax.ppermute(block, axis, [(i, i ^ step) for i in range(lax.axis_size(axi...  33.9 us
    pallas_call x4, Pallas kernels, rebuild(): pl.pallas_call(kernel, name='rebuild', grid=(wide // block,), out_shape=[...  32.8 us
    all_to_all x5, starting transfers between devices, across(): lax.all_to_all(block, 'dp', 0, 0, axis_index_groups=groups, tiled=True)  21.5 us
    all_to_all x5, waiting for transfers between devices, across(): lax.all_to_all(block, 'dp', 0, 0, axis_index_groups=groups, tiled=True)  16.8 us
    pallas_call x2, Pallas kernels, project(): pl.pallas_call(kernel, name='project', out_shape=[jax.ShapeDtypeStruct((b...  10.4 us
    pallas_call x2, Pallas kernels, gradients(): pl.pallas_call(kernel, name='gradients', grid=(half // block,), out_shape...  8.75 us
    pallas_call x1, Pallas kernels, chain(): pl.pallas_call(kernel, name='chain', out_shape=jax.ShapeDtypeStruct((rows...  7.2 us
  transfers between devices with their start and end apart: 45, of which 16 were waited for; matrix products, arithmetic and copies ran while one was open for 5% of the time, Pallas kernels for 27%

profile of v4, /device:TPU:0, one launch (start us, length us, event | category | flops | bytes accessed | tf_op | source)
XLA Modules:
  0.0 199.9 jit_solution(3590233301050744069)
XLA Ops:
  0.7 2.4 %pack.1 = (bf16[4,2,1,32,2048]{4,3,2,1,0:T(8,128)(2,1)}, f32[32,1]{1,0:T(8,128)}) custom-call(bf16[1,4,32,8192]{3,2,1,0:T(8,128)(2,1)} %x_ref.1, bf16[1,4,32,8192]{3,2,1,0:T(8,128)(2,1)} %g_ref.1), custom_call_target="tpu_custom_call" | custom-call | bytes 4194304 | tf_op jit(solution)/shard_map/pack/pallas_call | solution.py:100
  3.3 6.3 %all-to-all-start = ((bf16[4,2,32,2048]{3,2,1,0:T(8,128)(2,1)}), bf16[4,2,32,2048]{3,2,1,0:T(8,128)(2,1)S(1)}, u32[]{:S(2)}, u32[]{:S(2)}) async-start(bf16[4,2,32,2048]{3,2,1,0:T(8,128)(2,1)} %bitcast), calls=%async_computation | async-start | bytes 2097152 | tf_op jit(solution)/shard_map/all_to_all | solution.py:46
  9.6 1.5 collective-permute-start
  11.1 1.5 collective-permute-start.1
  12.6 21.7 %collective-permute-done.refs_2_.refs_3_.refs_5_ = bf16[1024,512]{1,0:T(8,128)(2,1)} collective-permute-done((bf16[1024,512]{1,0:T(8,128)(2,1)S(1)}, bf16[1024,512]{1,0:T(8,128)(2,1)}, u32[]{:S(2)}, u32[]{:S(2)}) %collective-permute-start) | collective-permute-done | bytes 1048608 | tf_op jit(solution)/shard_map/ppermute | solution.py:24
  34.3 1.2 collective-permute-done.1.refs_3_.refs_4_.refs_6_
  36.1 1.9 slice.66
  37.9 1.5 collective-permute-start.12
  39.5 1.9 slice.67
  41.3 1.3 collective-permute-start.13
  44.6 6.3 %project.2 = bf16[4,27,32,128]{3,2,1,0:T(8,128)(2,1)} custom-call(bf16[4,2,32,2048]{3,2,1,0:T(8,128)(2,1)} %copy-done.4, bf16[1024,512]{1,0:T(8,128)(2,1)} %copy-done.3, bf16[1024,512]{1,0:T(8,128)(2,1)} %collective-permute-done.refs_2_.refs_3_.refs_5_, bf16[1024,512]{1,0:T(8,128)(2,1)} %collective-permute-done.1.refs_3_.refs_4_.refs_6_, ...), custom_call_target="tpu_custom_call" | custom-call | flops 6442450944 | bytes 12582912 | tf_op jit(solution)/shard_map/project/pallas_call | solution.py:204
  50.8 4.2 %all-to-all-start.1 = ((bf16[4,27,32,128]{3,2,1,0:T(8,128)(2,1)}), bf16[4,27,32,128]{3,2,1,0:T(8,128)(2,1)S(1)}, u32[]{:S(2)}, u32[]{:S(2)}) async-start(bf16[4,27,32,128]{3,2,1,0:T(8,128)(2,1)} %project.2), calls=%async_computation.1 | async-start | bytes 1769472 | tf_op jit(solution)/shard_map/all_to_all | solution.py:46
  55.3 1.5 collective-permute-start.25
  58.0 1.1 copy-done.29
  59.1 4.1 %project.3 = bf16[4,9,32,128]{3,2,1,0:T(8,128)(2,1)} custom-call(bf16[4,2,32,2048]{3,2,1,0:T(8,128)(2,1)} %copy-done.4, bf16[1024,512]{1,0:T(8,128)(2,1)} %copy-done.3, bf16[1024,512]{1,0:T(8,128)(2,1)} %copy-done.10, bf16[1024,512]{1,0:T(8,128)(2,1)} %collective-permute-done.2.refs_4_.refs_3_.refs_6_, bf16[1024,512]{1,0:T(8,128)(2,1)} %copy-done.29), custom_call_target="tpu_custom_call" | custom-call | flops 2147483648 | bytes 8388608 | tf_op jit(solution)/shard_map/project/pallas_call | solution.py:204
  63.2 13.7 %all-to-all-done.1.refs_2_ = bf16[4,27,32,128]{3,2,1,0:T(8,128)(2,1)S(1)} async-done(((bf16[4,27,32,128]{3,2,1,0:T(8,128)(2,1)}), bf16[4,27,32,128]{3,2,1,0:T(8,128)(2,1)S(1)}, u32[]{:S(2)}, u32[]{:S(2)}) %all-to-all-start.1) | async-done | bytes 884768 | tf_op jit(solution)/shard_map/all_to_all | solution.py:46
  76.9 3.6 %all-to-all-start.2 = ((bf16[4,9,32,128]{3,2,1,0:T(8,128)(2,1)}), bf16[4,9,32,128]{3,2,1,0:T(8,128)(2,1)S(1)}, u32[]{:S(2)}, u32[]{:S(2)}) async-start(bf16[4,9,32,128]{3,2,1,0:T(8,128)(2,1)} %project.3), calls=%async_computation.2 | async-start | bytes 589824 | tf_op jit(solution)/shard_map/all_to_all | solution.py:46
  80.7 1.6 collective-permute-start.6
  82.8 1.5 collective-permute-start.10
  84.3 1.8 collective-permute-done.6.refs_5_
  86.1 3.3 %collective-permute-done.8.refs_7_ = bf16[3,128,128]{2,1,0:T(8,128)(2,1)} collective-permute-done((bf16[3,128,128]{2,1,0:T(8,128)(2,1)S(1)}, bf16[3,128,128]{2,1,0:T(8,128)(2,1)}, u32[]{:S(2)}, u32[]{:S(2)}) %collective-permute-start.8) | collective-permute-done | bytes 98336 | tf_op jit(solution)/shard_map/ppermute | solution.py:24
  89.9 1.1 collective-permute-start.16
  91.6 1.9 collective-permute-start.20
  94.0 1.3 collective-permute-done.18.refs_16_
  95.3 1.1 collective-permute-done.20.refs_18_
  96.4 1.1 slice.54
  97.5 1.6 collective-permute-start.27
  100.7 7.2 %chain.1 = bf16[32,2176]{1,0:T(8,128)(2,1)} custom-call(f32[32,1]{1,0:T(8,128)} %get-tuple-element.81.refs_0_, s32[4,1,32]{2,1,0:T(1,128)} %bitcast.42, bf16[4,27,32,128]{3,2,1,0:T(8,128)(2,1)} %copy-done.2, bf16[3,128,128]{2,1,0:T(8,128)(2,1)} %bitcast.36, bf16[3,128,128]{2,1,0:T(8,128)(2,1)} %copy-done.33, ...), custom_call_target="tpu_custom_call" | custom-call | flops 8589934592 | bytes 4194304 | tf_op jit(solution)/shard_map/chain/pallas_call | solution.py:318
  108.0 3.7 %collective-permute-start.24 = (bf16[32,2176]{1,0:T(8,128)(2,1)}, bf16[32,2176]{1,0:T(8,128)(2,1)S(1)}, u32[]{:S(2)}, u32[]{:S(2)}) collective-permute-start(bf16[32,2176]{1,0:T(8,128)(2,1)} %chain.1), channel_id=1, source_target_pairs={{0,6},{1,7},{2,4},{3,5},{4,2},{5,3},{6,0},{7,1},{8,14},{9,15},{10,... | collective-permute-start | bytes 417800 | tf_op jit(solution)/shard_map/ppermute | solution.py:24
  113.2 3.5 %collective-permute-done.24 = bf16[32,2176]{1,0:T(8,128)(2,1)S(1)} collective-permute-done((bf16[32,2176]{1,0:T(8,128)(2,1)}, bf16[32,2176]{1,0:T(8,128)(2,1)S(1)}, u32[]{:S(2)}, u32[]{:S(2)}) %collective-permute-start.24) | collective-permute-done | bytes 139296 | tf_op jit(solution)/shard_map/ppermute | solution.py:24
  116.7 7.3 %collective-permute-done.23 = bf16[32,2176]{1,0:T(8,128)(2,1)S(1)} collective-permute-done((bf16[32,2176]{1,0:T(8,128)(2,1)}, bf16[32,2176]{1,0:T(8,128)(2,1)S(1)}, u32[]{:S(2)}, u32[]{:S(2)}) %collective-permute-start.23) | collective-permute-done | bytes 139296 | tf_op jit(solution)/shard_map/ppermute | solution.py:24
  125.4 9.4 %rebuild.4 = (bf16[4,1,32,2048]{3,2,1,0:T(8,128)(2,1)}, bf16[128,2048]{1,0:T(8,128)(2,1)}, bf16[128,2048]{1,0:T(8,128)(2,1)}) custom-call(bf16[4,2,32,2048]{3,2,1,0:T(8,128)(2,1)} %copy-done.4, bf16[4,32,2176]{2,1,0:T(8,128)(2,1)} %copy-done.7, bf16[1024,512]{1,0:T(8,128)(2,1)} %copy-done.3, bf16[1024,512]{1,0:T(8,128)(2,1)} %collective-permute-done.refs_2_.refs_3_.refs_5_, ...), custom_call_target="tpu_custom_call" | custom-call | flops 6442450944 | bytes 16777216 | tf_op jit(solution)/shard_map/rebuild/pallas_call | solution.py:426
  134.7 3.6 %all-to-all-start.3 = ((bf16[4,1,32,2048]{3,2,1,0:T(8,128)(2,1)}), bf16[4,1,32,2048]{3,2,1,0:T(8,128)(2,1)S(1)}, u32[]{:S(2)}, u32[]{:S(2)}) async-start(bf16[4,1,32,2048]{3,2,1,0:T(8,128)(2,1)} %get-tuple-element.91), calls=%async_computation.3 | async-start | bytes 1048576 | tf_op jit(solution)/shard_map/all_to_all | solution.py:46
  140.0 6.9 %rebuild.5 = (bf16[2,32,1024]{2,1,0:T(8,128)(2,1)}, bf16[2,32,1024]{2,1,0:T(8,128)(2,1)}, bf16[2,32,1024]{2,1,0:T(8,128)(2,1)}, bf16[2,32,1024]{2,1,0:T(8,128)(2...) custom-call(bf16[4,2,32,2048]{3,2,1,0:T(8,128)(2,1)} %copy-done.8, ...), custom_call_target="tpu_custom_call" | custom-call | flops 6442450944 | bytes 16777216 | tf_op jit(solution)/shard_map/rebuild/pallas_call | solution.py:426
  146.9 2.1 %collective-permute-start.31 = (bf16[2,32,1024]{2,1,0:T(8,128)(2,1)}, bf16[2,32,1024]{2,1,0:T(8,128)(2,1)S(1)}, u32[]{:S(2)}, u32[]{:S(2)}) collective-permute-start(bf16[2,32,1024]{2,1,0:T(8,128)(2,1)} %get-tuple-element.105), channel_id=1, source_target_pairs={{0,2},{1,3},{2,0},{3,1},{4,6},{5,7},{6,4},{7,5},{8,10},{9,11},{10,... | collective-permute-start | bytes 393224 | tf_op jit(solution)/shard_map/ppermute | solution.py:24
  149.0 2.4 %collective-permute-start.32 = (bf16[2,32,1024]{2,1,0:T(8,128)(2,1)}, bf16[2,32,1024]{2,1,0:T(8,128)(2,1)S(1)}, u32[]{:S(2)}, u32[]{:S(2)}) collective-permute-start(bf16[2,32,1024]{2,1,0:T(8,128)(2,1)} %get-tuple-element.106), channel_id=1, source_target_pairs={{0,4},{1,5},{2,6},{3,7},{4,0},{5,1},{6,2},{7,3},{8,12},{9,13},{10,... | collective-permute-start | bytes 393224 | tf_op jit(solution)/shard_map/ppermute | solution.py:24
  153.7 1.5 all-to-all-done.3.refs_0_
  155.2 7.2 %rebuild.6 = (bf16[4,2,32,1024]{3,2,1,0:T(8,128)(2,1)}, bf16[256,1024]{1,0:T(8,128)(2,1)}, bf16[256,1024]{1,0:T(8,128)(2,1)}) custom-call(bf16[4,2,32,2048]{3,2,1,0:T(8,128)(2,1)} %copy-done.8, bf16[4,2,32,2048]{3,2,1,0:T(8,128)(2,1)} %collective-permute-done.26.refs_1_, bf16[4,32,2176]{2,1,0:T(8,128)(2,1)} %copy-done.16, bf16[4,32,2176]{2,1,0:T(8,128)(2,1)} %copy-done.17, ...), custom_call_target="tpu_custom_call" | custom-call | flops 6442450944 | bytes 16777216 | tf_op jit(solution)/shard_map/rebuild/pallas_call | solution.py:426
  162.4 3.7 %all-to-all-start.4 = ((bf16[4,2,32,1024]{3,2,1,0:T(8,128)(2,1)}), bf16[4,2,32,1024]{3,2,1,0:T(8,128)(2,1)S(1)}, u32[]{:S(2)}, u32[]{:S(2)}) async-start(bf16[4,2,32,1024]{3,2,1,0:T(8,128)(2,1)} %get-tuple-element.112), calls=%async_computation.4 | async-start | bytes 1048576 | tf_op jit(solution)/shard_map/all_to_all | solution.py:46
  167.0 9.4 %rebuild.7 = (bf16[1,32,2048]{2,1,0:T(8,128)(2,1)}, bf16[1,32,2048]{2,1,0:T(8,128)(2,1)}, bf16[1,32,2048]{2,1,0:T(8,128)(2,1)}, bf16[1,32,2048]{2,1,0:T(8,128)(2...) custom-call(bf16[4,2,32,2048]{3,2,1,0:T(8,128)(2,1)} %copy-done.9, bf16[4,32,2176]{2,1,0:T(8,128)(2,1)} %copy-done.18, ...), custom_call_target="tpu_custom_call" | custom-call | flops 6442450944 | bytes 16777216 | tf_op jit(solution)/shard_map/rebuild/pallas_call | solution.py:426
  176.5 1.5 all-to-all-done.4.refs_5_
  178.0 4.4 %gradients.3 = bf16[1024,512]{1,0:T(8,128)(2,1)} custom-call(bf16[128,2048]{1,0:T(8,128)(2,1)} %get-tuple-element.131.refs_0_, bf16[256,1024]{1,0:T(8,128)(2,1)} %get-tuple-element.137.refs_1_, bf16[128,2048]{1,0:T(8,128)(2,1)} %get-tuple-element.133.refs_2_, bf16[128,2048]{1,0:T(8,128)(2,1)} %get-tuple-element.134.refs_3_, ...), custom_call_target="tpu_custom_call" | custom-call | flops 8589934592 | bytes 8388608 | tf_op jit(solution)/shard_map/gradients/pallas_call | solution.py:475
  183.0 2.4 %collective-permute-start.37 = (bf16[1,32,2048]{2,1,0:T(8,128)(2,1)S(1)}, bf16[1,32,2048]{2,1,0:T(8,128)(2,1)S(1)}, u32[]{:S(2)}, u32[]{:S(2)}) collective-permute-start(bf16[1,32,2048]{2,1,0:T(8,128)(2,1)S(1)} %copy-done.31), channel_id=1, source_target_pairs={{0,4},{1,5},{2,6},{3,7},{4,0},{5,1},{6,2},{7,3},{8,12},{9,13},{10,... | collective-permute-start | bytes 393224 | tf_op jit(solution)/shard_map/ppermute | solution.py:24
  185.3 1.7 collective-permute-start.38
  187.0 4.3 %gradients.2 = f32[1024,512]{1,0:T(8,128)} custom-call(bf16[128,2048]{1,0:T(8,128)(2,1)} %get-tuple-element.131.refs_0_, bf16[256,1024]{1,0:T(8,128)(2,1)} %get-tuple-element.132.refs_1_, bf16[128,2048]{1,0:T(8,128)(2,1)} %get-tuple-element.133.refs_2_, bf16[128,2048]{1,0:T(8,128)(2,1)} %get-tuple-element.134.refs_3_, ...), custom_call_target="tpu_custom_call" | custom-call | flops 8589934592 | bytes 8388608 | tf_op jit(solution)/shard_map/gradients/pallas_call | solution.py:475
  191.3 2.9 %fusion = (f32[1,1024,128]{2,1,0:T(8,128)}, f32[1,1024,128]{2,1,0:T(8,128)}, f32[1,1024,128]{2,1,0:T(8,128)}, f32[1,1024,128]{2,1,0:T(8,128)}) fusion(f32[1024,512]{1,0:T(8,128)} %gradients.2, bf16[1024,512]{1,0:T(8,128)(2,1)S(1)} %collective-permute-done.39), kind=kLoop, calls=%fused_computation.3 | loop fusion | flops 1048576 | bytes 5242880 | tf_op jit(solution)/shard_map/broadcast_in_dim | solution.py:625
  194.2 1.6 collective-permute-done.37.refs_8_
  196.6 3.1 %unpack.1 = bf16[128,8192]{1,0:T(8,128)(2,1)} custom-call(bf16[4,1,32,2048]{3,2,1,0:T(8,128)(2,1)} %copy-done, bf16[2,32,1024]{2,1,0:T(8,128)(2,1)} %get-tuple-element.140.refs_1_, bf16[2,32,1024]{2,1,0:T(8,128)(2,1)} %copy-done.19, bf16[2,32,1024]{2,1,0:T(8,128)(2,1)} %copy-done.20, bf16[2,32,1024]{2,1,0:T(8,128)(2,1)} %copy-done.21, ...), custom_call_target="tpu_custom_call" | custom-call | bytes 8388608 | tf_op jit(solution)/shard_map/unpack/pallas_call | solution.py:145
  (152 shorter events, 16.8 us)
Async XLA Ops:
  3.3 38.1 %copy-start.3 = (bf16[1024,512]{1,0:T(8,128)(2,1)}, bf16[1024,512]{1,0:T(8,128)(2,1)S(1)}, u32[]{:S(2)}) copy-start(bf16[1024,512]{1,0:T(8,128)(2,1)S(1)} %pad_maximum_fusion.refs_1_.refs_2_.refs_4_) | copy-start | bytes 3145732
  3.3 32.3 %all-to-all-start = ((bf16[4,2,32,2048]{3,2,1,0:T(8,128)(2,1)}), bf16[4,2,32,2048]{3,2,1,0:T(8,128)(2,1)S(1)}, u32[]{:S(2)}, u32[]{:S(2)}) async-start(bf16[4,2,32,2048]{3,2,1,0:T(8,128)(2,1)} %bitcast), calls=%async_computation | async-start | bytes 2097152 | tf_op jit(solution)/shard_map/all_to_all | solution.py:46
  9.6 24.7 %collective-permute-start = (bf16[1024,512]{1,0:T(8,128)(2,1)S(1)}, bf16[1024,512]{1,0:T(8,128)(2,1)}, u32[]{:S(2)}, u32[]{:S(2)}) collective-permute-start(bf16[1024,512]{1,0:T(8,128)(2,1)S(1)} %pad_maximum_fusion.refs_1_.refs_2_.refs_4_), channel_id=1, source_target_pairs={{0,8},{8,0},{16,24},{24,16},{1,9},{9,1},{17,25},{25,17},{2,10},{10... | collective-permute-start | bytes 3145736 | tf_op jit(solution)/shard_map/ppermute | solution.py:24
  11.1 24.4 %collective-permute-start.1 = (bf16[1024,512]{1,0:T(8,128)(2,1)S(1)}, bf16[1024,512]{1,0:T(8,128)(2,1)}, u32[]{:S(2)}, u32[]{:S(2)}) collective-permute-start(bf16[1024,512]{1,0:T(8,128)(2,1)S(1)} %pad_maximum_fusion.refs_1_.refs_2_.refs_4_), channel_id=1, source_target_pairs={{0,16},{8,24},{16,0},{24,8},{1,17},{9,25},{17,1},{25,9},{2,18},{10... | collective-permute-start | bytes 3145736 | tf_op jit(solution)/shard_map/ppermute | solution.py:24
  12.6 30.0 %collective-permute-start.2 = (bf16[1024,512]{1,0:T(8,128)(2,1)S(1)}, bf16[1024,512]{1,0:T(8,128)(2,1)}, u32[]{:S(2)}, u32[]{:S(2)}) collective-permute-start(bf16[1024,512]{1,0:T(8,128)(2,1)S(1)} %pad_maximum_fusion.refs_1_.refs_2_.refs_4_), channel_id=1, source_target_pairs={{0,1},{1,0},{2,3},{3,2},{4,5},{5,4},{6,7},{7,6},{8,9},{9,8},{10,11... | collective-permute-start | bytes 3145736 | tf_op jit(solution)/shard_map/ppermute | solution.py:24
  35.6 7.1 %collective-permute-start.3 = (bf16[1024,512]{1,0:T(8,128)(2,1)}, bf16[1024,512]{1,0:T(8,128)(2,1)S(1)}, u32[]{:S(2)}, u32[]{:S(2)}) collective-permute-start(bf16[1024,512]{1,0:T(8,128)(2,1)} %collective-permute-done.refs_2_.refs_3_.refs_5_), channel_id=1, source_target_pairs={{0,1},{1,0},{2,3},{3,2},{4,5},{5,4},{6,7},{7,6},{8,9},{9,8},{10,11... | collective-permute-start | bytes 3145736 | tf_op jit(solution)/shard_map/ppermute | solution.py:24
  35.6 7.1 %collective-permute-start.4 = (bf16[1024,512]{1,0:T(8,128)(2,1)}, bf16[1024,512]{1,0:T(8,128)(2,1)S(1)}, u32[]{:S(2)}, u32[]{:S(2)}) collective-permute-start(bf16[1024,512]{1,0:T(8,128)(2,1)} %collective-permute-done.1.refs_3_.refs_4_.refs_6_), channel_id=1, source_target_pairs={{0,1},{1,0},{2,3},{3,2},{4,5},{5,4},{6,7},{7,6},{8,9},{9,8},{10,11... | collective-permute-start | bytes 3145736 | tf_op jit(solution)/shard_map/ppermute | solution.py:24
  37.9 17.1 %collective-permute-start.12 = (bf16[512,512]{1,0:T(8,128)(2,1)}, bf16[512,512]{1,0:T(8,128)(2,1)S(1)}, u32[]{:S(2)}, u32[]{:S(2)}) collective-permute-start(bf16[512,512]{1,0:T(8,128)(2,1)} %slice.66), channel_id=1, source_target_pairs={{0,16},{8,24},{16,0},{24,8},{1,17},{9,25},{17,1},{25,9},{2,18},{10... | collective-permute-start | bytes 1572872 | tf_op jit(solution)/shard_map/ppermute | solution.py:24
  41.3 13.8 %collective-permute-start.13 = (bf16[512,512]{1,0:T(8,128)(2,1)}, bf16[512,512]{1,0:T(8,128)(2,1)S(1)}, u32[]{:S(2)}, u32[]{:S(2)}) collective-permute-start(bf16[512,512]{1,0:T(8,128)(2,1)} %slice.67), channel_id=1, source_target_pairs={{0,8},{8,0},{16,24},{24,16},{1,9},{9,1},{17,25},{25,17},{2,10},{10... | collective-permute-start | bytes 1572872 | tf_op jit(solution)/shard_map/ppermute | solution.py:24
  50.8 26.1 %all-to-all-start.1 = ((bf16[4,27,32,128]{3,2,1,0:T(8,128)(2,1)}), bf16[4,27,32,128]{3,2,1,0:T(8,128)(2,1)S(1)}, u32[]{:S(2)}, u32[]{:S(2)}) async-start(bf16[4,27,32,128]{3,2,1,0:T(8,128)(2,1)} %project.2), calls=%async_computation.1 | async-start | bytes 1769472 | tf_op jit(solution)/shard_map/all_to_all | solution.py:46
  55.3 2.7 %collective-permute-start.14 = (bf16[1024,512]{1,0:T(8,128)(2,1)S(1)}, bf16[1024,512]{1,0:T(8,128)(2,1)S(1)}, u32[]{:S(2)}, u32[]{:S(2)}) collective-permute-start(bf16[1024,512]{1,0:T(8,128)(2,1)S(1)} %constant_dynamic-update-slice_fusion.refs_2_.refs_5_.refs_7_), channel_id=1, source_target_pairs={{0,1},{1,0},{2,3},{3,2},{4,5},{5,4},{6,7},{7,6},{8,9},{9,8},{10,11... | collective-permute-start | bytes 3145736 | tf_op jit(solution)/shard_map/ppermute | solution.py:24
  55.3 34.6 %collective-permute-start.25 = (bf16[4,2,32,2048]{3,2,1,0:T(8,128)(2,1)S(1)}, bf16[4,2,32,2048]{3,2,1,0:T(8,128)(2,1)S(1)}, u32[]{:S(2)}, u32[]{:S(2)}) collective-permute-start(bf16[4,2,32,2048]{3,2,1,0:T(8,128)(2,1)S(1)} %copy-done.5), channel_id=1, source_target_pairs={{0,8},{8,0},{16,24},{24,16},{1,9},{9,1},{17,25},{25,17},{2,10},{10... | collective-permute-start | bytes 3145736 | tf_op jit(solution)/shard_map/ppermute | solution.py:24
  56.8 34.2 %collective-permute-start.26 = (bf16[4,2,32,2048]{3,2,1,0:T(8,128)(2,1)S(1)}, bf16[4,2,32,2048]{3,2,1,0:T(8,128)(2,1)}, u32[]{:S(2)}, u32[]{:S(2)}) collective-permute-start(bf16[4,2,32,2048]{3,2,1,0:T(8,128)(2,1)S(1)} %copy-done.5), channel_id=1, source_target_pairs={{0,16},{8,24},{16,0},{24,8},{1,17},{9,25},{17,1},{25,9},{2,18},{10... | collective-permute-start | bytes 3145736 | tf_op jit(solution)/shard_map/ppermute | solution.py:24
  76.9 23.2 %copy-start.2 = (bf16[4,27,32,128]{3,2,1,0:T(8,128)(2,1)}, bf16[4,27,32,128]{3,2,1,0:T(8,128)(2,1)S(1)}, u32[]{:S(2)}) copy-start(bf16[4,27,32,128]{3,2,1,0:T(8,128)(2,1)S(1)} %all-to-all-done.1.refs_2_) | copy-start | bytes 2654212
  76.9 12.9 %all-to-all-start.2 = ((bf16[4,9,32,128]{3,2,1,0:T(8,128)(2,1)}), bf16[4,9,32,128]{3,2,1,0:T(8,128)(2,1)S(1)}, u32[]{:S(2)}, u32[]{:S(2)}) async-start(bf16[4,9,32,128]{3,2,1,0:T(8,128)(2,1)} %project.3), calls=%async_computation.2 | async-start | bytes 589824 | tf_op jit(solution)/shard_map/all_to_all | solution.py:46
  80.7 2.2 %collective-permute-start.5 = (bf16[3,128,128]{2,1,0:T(8,128)(2,1)S(1)}, bf16[3,128,128]{2,1,0:T(8,128)(2,1)S(1)}, u32[]{:S(2)}, u32[]{:S(2)}) collective-permute-start(bf16[3,128,128]{2,1,0:T(8,128)(2,1)S(1)} %bitcast.32), channel_id=1, source_target_pairs={{0,1},{1,0},{2,3},{3,2},{4,5},{5,4},{6,7},{7,6},{8,9},{9,8},{10,11... | collective-permute-start | bytes 294920 | tf_op jit(solution)/shard_map/ppermute | solution.py:24
  80.7 5.3 %collective-permute-start.6 = (bf16[3,128,128]{2,1,0:T(8,128)(2,1)S(1)}, bf16[3,128,128]{2,1,0:T(8,128)(2,1)}, u32[]{:S(2)}, u32[]{:S(2)}) collective-permute-start(bf16[3,128,128]{2,1,0:T(8,128)(2,1)S(1)} %bitcast.33), channel_id=1, source_target_pairs={{0,8},{8,0},{16,24},{24,16},{1,9},{9,1},{17,25},{25,17},{2,10},{10... | collective-permute-start | bytes 294920 | tf_op jit(solution)/shard_map/ppermute | solution.py:24
  82.3 7.1 %collective-permute-start.8 = (bf16[3,128,128]{2,1,0:T(8,128)(2,1)S(1)}, bf16[3,128,128]{2,1,0:T(8,128)(2,1)}, u32[]{:S(2)}, u32[]{:S(2)}) collective-permute-start(bf16[3,128,128]{2,1,0:T(8,128)(2,1)S(1)} %bitcast.34), channel_id=1, source_target_pairs={{0,16},{8,24},{16,0},{24,8},{1,17},{9,25},{17,1},{25,9},{2,18},{10... | collective-permute-start | bytes 294920 | tf_op jit(solution)/shard_map/ppermute | solution.py:24
  82.8 6.6 %collective-permute-start.10 = (bf16[3,128,128]{2,1,0:T(8,128)(2,1)S(1)}, bf16[3,128,128]{2,1,0:T(8,128)(2,1)}, u32[]{:S(2)}, u32[]{:S(2)}) collective-permute-start(bf16[3,128,128]{2,1,0:T(8,128)(2,1)S(1)} %bitcast.35), channel_id=1, source_target_pairs={{0,24},{8,16},{16,8},{24,0},{1,25},{9,17},{17,9},{25,1},{2,26},{10... | collective-permute-start | bytes 294920 | tf_op jit(solution)/shard_map/ppermute | solution.py:24
  86.0 5.5 %collective-permute-start.7 = (bf16[3,128,128]{2,1,0:T(8,128)(2,1)}, bf16[3,128,128]{2,1,0:T(8,128)(2,1)}, u32[]{:S(2)}, u32[]{:S(2)}) collective-permute-start(bf16[3,128,128]{2,1,0:T(8,128)(2,1)} %collective-permute-done.6.refs_5_), channel_id=1, source_target_pairs={{0,1},{1,0},{2,3},{3,2},{4,5},{5,4},{6,7},{7,6},{8,9},{9,8},{10,11... | collective-permute-start | bytes 294920 | tf_op jit(solution)/shard_map/ppermute | solution.py:24
  89.4 4.1 %collective-permute-start.9 = (bf16[3,128,128]{2,1,0:T(8,128)(2,1)}, bf16[3,128,128]{2,1,0:T(8,128)(2,1)}, u32[]{:S(2)}, u32[]{:S(2)}) collective-permute-start(bf16[3,128,128]{2,1,0:T(8,128)(2,1)} %collective-permute-done.8.refs_7_), channel_id=1, source_target_pairs={{0,1},{1,0},{2,3},{3,2},{4,5},{5,4},{6,7},{7,6},{8,9},{9,8},{10,11... | collective-permute-start | bytes 294920 | tf_op jit(solution)/shard_map/ppermute | solution.py:24
  89.4 8.2 %collective-permute-start.11 = (bf16[3,128,128]{2,1,0:T(8,128)(2,1)}, bf16[3,128,128]{2,1,0:T(8,128)(2,1)}, u32[]{:S(2)}, u32[]{:S(2)}) collective-permute-start(bf16[3,128,128]{2,1,0:T(8,128)(2,1)} %collective-permute-done.10.refs_9_), channel_id=1, source_target_pairs={{0,1},{1,0},{2,3},{3,2},{4,5},{5,4},{6,7},{7,6},{8,9},{9,8},{10,11... | collective-permute-start | bytes 294920 | tf_op jit(solution)/shard_map/ppermute | solution.py:24
  89.9 4.0 %collective-permute-start.16 = (bf16[1,128,128]{2,1,0:T(8,128)(2,1)S(1)}, bf16[1,128,128]{2,1,0:T(8,128)(2,1)S(1)}, u32[]{:S(2)}, u32[]{:S(2)}) collective-permute-start(bf16[1,128,128]{2,1,0:T(8,128)(2,1)S(1)} %bitcast.37), channel_id=1, source_target_pairs={{0,8},{8,0},{16,24},{24,16},{1,9},{9,1},{17,25},{25,17},{2,10},{10... | collective-permute-start | bytes 98312 | tf_op jit(solution)/shard_map/ppermute | solution.py:24
  91.0 4.3 %collective-permute-start.18 = (bf16[1,128,128]{2,1,0:T(8,128)(2,1)S(1)}, bf16[1,128,128]{2,1,0:T(8,128)(2,1)S(1)}, u32[]{:S(2)}, u32[]{:S(2)}) collective-permute-start(bf16[1,128,128]{2,1,0:T(8,128)(2,1)S(1)} %bitcast.38), channel_id=1, source_target_pairs={{0,16},{8,24},{16,0},{24,8},{1,17},{9,25},{17,1},{25,9},{2,18},{10... | collective-permute-start | bytes 98312 | tf_op jit(solution)/shard_map/ppermute | solution.py:24
  91.6 4.8 %collective-permute-start.20 = (bf16[1,128,128]{2,1,0:T(8,128)(2,1)S(1)}, bf16[1,128,128]{2,1,0:T(8,128)(2,1)S(1)}, u32[]{:S(2)}, u32[]{:S(2)}) collective-permute-start(bf16[1,128,128]{2,1,0:T(8,128)(2,1)S(1)} %bitcast.39), channel_id=1, source_target_pairs={{0,24},{8,16},{16,8},{24,0},{1,25},{9,17},{17,9},{25,1},{2,26},{10... | collective-permute-start | bytes 98312 | tf_op jit(solution)/shard_map/ppermute | solution.py:24
  93.5 5.6 %collective-permute-start.15 = (bf16[1,128,128]{2,1,0:T(8,128)(2,1)S(1)}, bf16[1,128,128]{2,1,0:T(8,128)(2,1)S(1)}, u32[]{:S(2)}, u32[]{:S(2)}) collective-permute-start(bf16[1,128,128]{2,1,0:T(8,128)(2,1)S(1)} %bitcast.40), channel_id=1, source_target_pairs={{0,1},{1,0},{2,3},{3,2},{4,5},{5,4},{6,7},{7,6},{8,9},{9,8},{10,11... | collective-permute-start | bytes 98312 | tf_op jit(solution)/shard_map/ppermute | solution.py:24
  93.9 6.2 %collective-permute-start.17 = (bf16[1,128,128]{2,1,0:T(8,128)(2,1)S(1)}, bf16[1,128,128]{2,1,0:T(8,128)(2,1)S(1)}, u32[]{:S(2)}, u32[]{:S(2)}) collective-permute-start(bf16[1,128,128]{2,1,0:T(8,128)(2,1)S(1)} %collective-permute-done.16.refs_14_), channel_id=1, source_target_pairs={{0,1},{1,0},{2,3},{3,2},{4,5},{5,4},{6,7},{7,6},{8,9},{9,8},{10,11... | collective-permute-start | bytes 98312 | tf_op jit(solution)/shard_map/ppermute | solution.py:24
  95.3 4.8 %collective-permute-start.19 = (bf16[1,128,128]{2,1,0:T(8,128)(2,1)S(1)}, bf16[1,128,128]{2,1,0:T(8,128)(2,1)S(1)}, u32[]{:S(2)}, u32[]{:S(2)}) collective-permute-start(bf16[1,128,128]{2,1,0:T(8,128)(2,1)S(1)} %collective-permute-done.18.refs_16_), channel_id=1, source_target_pairs={{0,1},{1,0},{2,3},{3,2},{4,5},{5,4},{6,7},{7,6},{8,9},{9,8},{10,11... | collective-permute-start | bytes 98312 | tf_op jit(solution)/shard_map/ppermute | solution.py:24
  96.4 3.7 %collective-permute-start.21 = (bf16[1,128,128]{2,1,0:T(8,128)(2,1)S(1)}, bf16[1,128,128]{2,1,0:T(8,128)(2,1)S(1)}, u32[]{:S(2)}, u32[]{:S(2)}) collective-permute-start(bf16[1,128,128]{2,1,0:T(8,128)(2,1)S(1)} %collective-permute-done.20.refs_18_), channel_id=1, source_target_pairs={{0,1},{1,0},{2,3},{3,2},{4,5},{5,4},{6,7},{7,6},{8,9},{9,8},{10,11... | collective-permute-start | bytes 98312 | tf_op jit(solution)/shard_map/ppermute | solution.py:24
  97.5 14.9 %collective-permute-start.27 = (bf16[2,2,32,2048]{3,2,1,0:T(8,128)(2,1)S(1)}, bf16[2,2,32,2048]{3,2,1,0:T(8,128)(2,1)S(1)}, u32[]{:S(2)}, u32[]{:S(2)}) collective-permute-start(bf16[2,2,32,2048]{3,2,1,0:T(8,128)(2,1)S(1)} %slice.53), channel_id=1, source_target_pairs={{0,16},{8,24},{16,0},{24,8},{1,17},{9,25},{17,1},{25,9},{2,18},{10... | collective-permute-start | bytes 1572872 | tf_op jit(solution)/shard_map/ppermute | solution.py:24
  99.1 14.1 %collective-permute-start.28 = (bf16[2,2,32,2048]{3,2,1,0:T(8,128)(2,1)S(1)}, bf16[2,2,32,2048]{3,2,1,0:T(8,128)(2,1)S(1)}, u32[]{:S(2)}, u32[]{:S(2)}) collective-permute-start(bf16[2,2,32,2048]{3,2,1,0:T(8,128)(2,1)S(1)} %slice.54), channel_id=1, source_target_pairs={{0,8},{8,0},{16,24},{24,16},{1,9},{9,1},{17,25},{25,17},{2,10},{10... | collective-permute-start | bytes 1572872 | tf_op jit(solution)/shard_map/ppermute | solution.py:24
  108.0 8.7 %collective-permute-start.24 = (bf16[32,2176]{1,0:T(8,128)(2,1)}, bf16[32,2176]{1,0:T(8,128)(2,1)S(1)}, u32[]{:S(2)}, u32[]{:S(2)}) collective-permute-start(bf16[32,2176]{1,0:T(8,128)(2,1)} %chain.1), channel_id=1, source_target_pairs={{0,6},{1,7},{2,4},{3,5},{4,2},{5,3},{6,0},{7,1},{8,14},{9,15},{10,... | collective-permute-start | bytes 417800 | tf_op jit(solution)/shard_map/ppermute | solution.py:24
  111.6 12.3 %collective-permute-start.23 = (bf16[32,2176]{1,0:T(8,128)(2,1)}, bf16[32,2176]{1,0:T(8,128)(2,1)S(1)}, u32[]{:S(2)}, u32[]{:S(2)}) collective-permute-start(bf16[32,2176]{1,0:T(8,128)(2,1)} %chain.1), channel_id=1, source_target_pairs={{0,4},{1,5},{2,6},{3,7},{4,0},{5,1},{6,2},{7,3},{8,12},{9,13},{10,... | collective-permute-start | bytes 417800 | tf_op jit(solution)/shard_map/ppermute | solution.py:24
  111.6 12.3 %collective-permute-start.22 = (bf16[32,2176]{1,0:T(8,128)(2,1)}, bf16[32,2176]{1,0:T(8,128)(2,1)S(1)}, u32[]{:S(2)}, u32[]{:S(2)}) collective-permute-start(bf16[32,2176]{1,0:T(8,128)(2,1)} %chain.1), channel_id=1, source_target_pairs={{0,2},{1,3},{2,0},{3,1},{4,6},{5,7},{6,4},{7,5},{8,10},{9,11},{10,... | collective-permute-start | bytes 417800 | tf_op jit(solution)/shard_map/ppermute | solution.py:24
  113.2 21.5 %copy-start.9 = (bf16[4,2,32,2048]{3,2,1,0:T(8,128)(2,1)}, bf16[4,2,32,2048]{3,2,1,0:T(8,128)(2,1)S(1)}, u32[]{:S(2)}) copy-start(bf16[4,2,32,2048]{3,2,1,0:T(8,128)(2,1)S(1)} %constant_dynamic-update-slice_fusion.2.refs_0_) | copy-start | bytes 3145732
  124.0 14.3 %collective-permute-start.29 = (bf16[4,32,2176]{2,1,0:T(8,128)(2,1)S(1)}, bf16[4,32,2176]{2,1,0:T(8,128)(2,1)S(1)}, u32[]{:S(2)}, u32[]{:S(2)}) collective-permute-start(bf16[4,32,2176]{2,1,0:T(8,128)(2,1)S(1)} %pad_maximum_fusion.1.refs_1_.refs_6_), channel_id=1, source_target_pairs={{0,8},{8,0},{16,24},{24,16},{1,9},{9,1},{17,25},{25,17},{2,10},{10... | collective-permute-start | bytes 1671176 | tf_op jit(solution)/shard_map/ppermute | solution.py:24
  124.7 13.7 %collective-permute-start.30 = (bf16[4,32,2176]{2,1,0:T(8,128)(2,1)S(1)}, bf16[4,32,2176]{2,1,0:T(8,128)(2,1)S(1)}, u32[]{:S(2)}, u32[]{:S(2)}) collective-permute-start(bf16[4,32,2176]{2,1,0:T(8,128)(2,1)S(1)} %pad_maximum_fusion.1.refs_1_.refs_6_), channel_id=1, source_target_pairs={{0,16},{8,24},{16,0},{24,8},{1,17},{9,25},{17,1},{25,9},{2,18},{10... | collective-permute-start | bytes 1671176 | tf_op jit(solution)/shard_map/ppermute | solution.py:24
  134.7 20.5 %all-to-all-start.3 = ((bf16[4,1,32,2048]{3,2,1,0:T(8,128)(2,1)}), bf16[4,1,32,2048]{3,2,1,0:T(8,128)(2,1)S(1)}, u32[]{:S(2)}, u32[]{:S(2)}) async-start(bf16[4,1,32,2048]{3,2,1,0:T(8,128)(2,1)} %get-tuple-element.91), calls=%async_computation.3 | async-start | bytes 1048576 | tf_op jit(solution)/shard_map/all_to_all | solution.py:46
  146.9 19.4 %collective-permute-start.31 = (bf16[2,32,1024]{2,1,0:T(8,128)(2,1)}, bf16[2,32,1024]{2,1,0:T(8,128)(2,1)S(1)}, u32[]{:S(2)}, u32[]{:S(2)}) collective-permute-start(bf16[2,32,1024]{2,1,0:T(8,128)(2,1)} %get-tuple-element.105), channel_id=1, source_target_pairs={{0,2},{1,3},{2,0},{3,1},{4,6},{5,7},{6,4},{7,5},{8,10},{9,11},{10,... | collective-permute-start | bytes 393224 | tf_op jit(solution)/shard_map/ppermute | solution.py:24
  149.0 17.3 %collective-permute-start.32 = (bf16[2,32,1024]{2,1,0:T(8,128)(2,1)}, bf16[2,32,1024]{2,1,0:T(8,128)(2,1)S(1)}, u32[]{:S(2)}, u32[]{:S(2)}) collective-permute-start(bf16[2,32,1024]{2,1,0:T(8,128)(2,1)} %get-tuple-element.106), channel_id=1, source_target_pairs={{0,4},{1,5},{2,6},{3,7},{4,0},{5,1},{6,2},{7,3},{8,12},{9,13},{10,... | collective-permute-start | bytes 393224 | tf_op jit(solution)/shard_map/ppermute | solution.py:24
  151.3 14.9 %collective-permute-start.33 = (bf16[2,32,1024]{2,1,0:T(8,128)(2,1)}, bf16[2,32,1024]{2,1,0:T(8,128)(2,1)S(1)}, u32[]{:S(2)}, u32[]{:S(2)}) collective-permute-start(bf16[2,32,1024]{2,1,0:T(8,128)(2,1)} %get-tuple-element.107), channel_id=1, source_target_pairs={{0,6},{1,7},{2,4},{3,5},{4,2},{5,3},{6,0},{7,1},{8,14},{9,15},{10,... | collective-permute-start | bytes 393224 | tf_op jit(solution)/shard_map/ppermute | solution.py:24
  152.4 13.8 %collective-permute-start.34 = (bf16[2,32,2176]{2,1,0:T(8,128)(2,1)S(1)}, bf16[2,32,2176]{2,1,0:T(8,128)(2,1)S(1)}, u32[]{:S(2)}, u32[]{:S(2)}) collective-permute-start(bf16[2,32,2176]{2,1,0:T(8,128)(2,1)S(1)} %slice.68), channel_id=1, source_target_pairs={{0,16},{8,24},{16,0},{24,8},{1,17},{9,25},{17,1},{25,9},{2,18},{10... | collective-permute-start | bytes 835592 | tf_op jit(solution)/shard_map/ppermute | solution.py:24
  153.4 12.7 %collective-permute-start.35 = (bf16[2,32,2176]{2,1,0:T(8,128)(2,1)S(1)}, bf16[2,32,2176]{2,1,0:T(8,128)(2,1)S(1)}, u32[]{:S(2)}, u32[]{:S(2)}) collective-permute-start(bf16[2,32,2176]{2,1,0:T(8,128)(2,1)S(1)} %slice.69), channel_id=1, source_target_pairs={{0,8},{8,0},{16,24},{24,16},{1,9},{9,1},{17,25},{25,17},{2,10},{10... | collective-permute-start | bytes 835592 | tf_op jit(solution)/shard_map/ppermute | solution.py:24
  162.4 15.6 %all-to-all-start.4 = ((bf16[4,2,32,1024]{3,2,1,0:T(8,128)(2,1)}), bf16[4,2,32,1024]{3,2,1,0:T(8,128)(2,1)S(1)}, u32[]{:S(2)}, u32[]{:S(2)}) async-start(bf16[4,2,32,1024]{3,2,1,0:T(8,128)(2,1)} %get-tuple-element.112), calls=%async_computation.4 | async-start | bytes 1048576 | tf_op jit(solution)/shard_map/all_to_all | solution.py:46
  182.5 8.9 %collective-permute-start.39 = (bf16[1024,512]{1,0:T(8,128)(2,1)}, bf16[1024,512]{1,0:T(8,128)(2,1)S(1)}, u32[]{:S(2)}, u32[]{:S(2)}) collective-permute-start(bf16[1024,512]{1,0:T(8,128)(2,1)} %gradients.3), channel_id=1, source_target_pairs={{0,1},{1,0},{2,3},{3,2},{4,5},{5,4},{6,7},{7,6},{8,9},{9,8},{10,11... | collective-permute-start | bytes 3145736 | tf_op jit(solution)/shard_map/ppermute | solution.py:24
  182.5 11.7 %collective-permute-start.36 = (bf16[1,32,2048]{2,1,0:T(8,128)(2,1)S(1)}, bf16[1,32,2048]{2,1,0:T(8,128)(2,1)S(1)}, u32[]{:S(2)}, u32[]{:S(2)}) collective-permute-start(bf16[1,32,2048]{2,1,0:T(8,128)(2,1)S(1)} %copy-done.32), channel_id=1, source_target_pairs={{0,2},{1,3},{2,0},{3,1},{4,6},{5,7},{6,4},{7,5},{8,10},{9,11},{10,... | collective-permute-start | bytes 393224 | tf_op jit(solution)/shard_map/ppermute | solution.py:24
  183.0 12.9 %collective-permute-start.37 = (bf16[1,32,2048]{2,1,0:T(8,128)(2,1)S(1)}, bf16[1,32,2048]{2,1,0:T(8,128)(2,1)S(1)}, u32[]{:S(2)}, u32[]{:S(2)}) collective-permute-start(bf16[1,32,2048]{2,1,0:T(8,128)(2,1)S(1)} %copy-done.31), channel_id=1, source_target_pairs={{0,4},{1,5},{2,6},{3,7},{4,0},{5,1},{6,2},{7,3},{8,12},{9,13},{10,... | collective-permute-start | bytes 393224 | tf_op jit(solution)/shard_map/ppermute | solution.py:24
  185.3 10.6 %collective-permute-start.38 = (bf16[1,32,2048]{2,1,0:T(8,128)(2,1)S(1)}, bf16[1,32,2048]{2,1,0:T(8,128)(2,1)S(1)}, u32[]{:S(2)}, u32[]{:S(2)}) collective-permute-start(bf16[1,32,2048]{2,1,0:T(8,128)(2,1)S(1)} %copy-done.30), channel_id=1, source_target_pairs={{0,6},{1,7},{2,4},{3,5},{4,2},{5,3},{6,0},{7,1},{8,14},{9,15},{10,... | collective-permute-start | bytes 393224 | tf_op jit(solution)/shard_map/ppermute | solution.py:24
  (38 other events, 201.6 us)
